TPU v7x, 32 devices: a whole 2x2x4 slice. The times are simulated.
32 devices in a mesh: gx: 4 (over y, core), gy: 8 (over z, x).
Axes of the slice: x: 2, y: 2, z: 4, core: 2. Of those that a mesh axis runs over, the one named last changes fastest.
Arguments:
- density: float32 [80, 80, 384], P('gx', 'gy'), may hold values from 1e-06 to 0.5
- charge: float32 [80, 80, 384], P('gx', 'gy'), may hold values from -6 to 6
Outputs:
- solution_field: float32 [80, 80, 384], P('gx', 'gy')
- residual: float32 [80, 80, 384], P('gx', 'gy')
All inputs are finite; a program needn't handle non-finite values.
Results may differ from a plain program's by a relative error of at most 0.0003.
Values sent between devices are 32-bit elements; how exact they have to be, the bound alone decides.
No kernel may reach another device: no remote copies, remote signals or barrier semaphores. Data moves between devices by JAX's collectives and lax.ppermute only.
A program may use at most 64 MiB of HBM per device.

v0:
```python
import math

import jax
import jax.numpy as jnp
from jax import lax
from jax.sharding import PartitionSpec as P

EPS_SOLVENT = 78.3
RHO_UPPER = 0.005
RHO_LOWER = 0.0001
KAPPA_SCALE = 0.1
EPS_PRECOND = 20.0
SHIFT_PRECOND = 0.05
HIGHEST = lax.Precision.HIGHEST


def extended(block, sides, width):
    for axis, dim in sides:
        count = lax.axis_size(axis)
        forward = [(i, i + 1) for i in range(count - 1)]
        forward.append((count - 1, 0))
        backward = [(target, source) for source, target in forward]
        low = lax.ppermute(
            lax.slice_in_dim(block, block.shape[dim] - width, None, axis=dim), axis, forward
        )
        high = lax.ppermute(lax.slice_in_dim(block, 0, width, axis=dim), axis, backward)
        block = jnp.concatenate([low, block, high], axis=dim)
    return block


def permittivity(density):
    upper = math.log(RHO_UPPER)
    lower = math.log(RHO_LOWER)
    fraction = jnp.clip((upper - jnp.log(density)) / (upper - lower), 0.0, 1.0)
    exponent = fraction - jnp.sin(2.0 * math.pi * fraction) / (2.0 * math.pi)
    return jnp.exp(exponent * math.log(EPS_SOLVENT))


def hartley(length):
    indices = jnp.arange(length, dtype=jnp.int32)
    product = indices[:, None] * indices[None, :] % length
    angles = product.astype(jnp.float32) * (2.0 * math.pi / length)
    return jnp.cos(angles) + jnp.sin(angles)


def spectrum(wavenum, length):
    halfang = wavenum.astype(jnp.float32) * (math.pi / length)
    return ((27.0 * jnp.sin(halfang) - jnp.sin(3.0 * halfang)) / 12.0) ** 2


def cutout(values, offset, length, dimen):
    return lax.slice_in_dim(values, offset, offset + length, axis=dimen)


def padded_term(padded, faces, count, dimen):
    nfaces = count + 3
    grad = (
        27.0 * (cutout(padded, 2, nfaces, dimen) - cutout(padded, 1, nfaces, dimen))
        - (cutout(padded, 3, nfaces, dimen) - cutout(padded, 0, nfaces, dimen))
    ) / 24.0
    flux = faces * grad
    return (
        27.0 * (cutout(flux, 2, count, dimen) - cutout(flux, 1, count, dimen))
        - (cutout(flux, 3, count, dimen) - cutout(flux, 0, count, dimen))
    ) / 24.0


def rolled_term(field, faces):
    grad = (
        27.0 * (jnp.roll(field, -1, 2) - field) - (jnp.roll(field, -2, 2) - jnp.roll(field, 1, 2))
    ) / 24.0
    flux = faces * grad
    return (
        27.0 * (flux - jnp.roll(flux, 1, 2)) - (jnp.roll(flux, -1, 2) - jnp.roll(flux, 2, 2))
    ) / 24.0


def operate(field, faces_x, faces_y, faces_z, kappa):
    cellsx = field.shape[0]
    cellsy = field.shape[1]
    padded = extended(field, (("gx", 0), ("gy", 1)), 3)
    term_x = padded_term(padded[:, 3 : 3 + cellsy], faces_x, cellsx, 0)
    term_y = padded_term(padded[3 : 3 + cellsx], faces_y, cellsy, 1)
    term_z = rolled_term(field, faces_z)
    return kappa * field - (term_x + term_y + term_z)


def precondition(field):
    cellsx, cellsy, length_z = field.shape
    size_x = cellsx * lax.axis_size("gx")
    size_y = cellsy * lax.axis_size("gy")
    hart_x = hartley(size_x)
    hart_y = hartley(size_y)
    hart_z = hartley(length_z)
    scaling = float(size_x * size_y * length_z)
    forward = jnp.dot(field, hart_z, precision=HIGHEST)
    zpiece = length_z // lax.axis_size("gx")
    xpiece = size_x // lax.axis_size("gy")
    lines_x = lax.all_to_all(forward, "gx", split_axis=2, concat_axis=0, tiled=True)
    along_x = jnp.einsum("xyk,xa->yka", lines_x, hart_x, precision=HIGHEST)
    lines_y = lax.all_to_all(along_x, "gy", split_axis=2, concat_axis=0, tiled=True)
    along_y = jnp.einsum("ykb,yc->kbc", lines_y, hart_y, precision=HIGHEST)
    wave_z = lax.axis_index("gx") * zpiece + jnp.arange(zpiece, dtype=jnp.int32)
    wave_x = lax.axis_index("gy") * xpiece + jnp.arange(xpiece, dtype=jnp.int32)
    wave_y = jnp.arange(size_y, dtype=jnp.int32)
    symbol = (
        EPS_PRECOND
        * (
            spectrum(wave_z, length_z)[:, None, None]
            + spectrum(wave_x, size_x)[None, :, None]
            + spectrum(wave_y, size_y)[None, None, :]
        )
        + SHIFT_PRECOND
    )
    scaled = along_y / (symbol * scaling)
    back_y = jnp.einsum("kbc,cy->ykb", scaled, hart_y, precision=HIGHEST)
    lines_back = lax.all_to_all(back_y, "gy", split_axis=0, concat_axis=2, tiled=True)
    back_x = jnp.einsum("yka,ax->xyk", lines_back, hart_x, precision=HIGHEST)
    bricks = lax.all_to_all(back_x, "gx", split_axis=0, concat_axis=2, tiled=True)
    return jnp.dot(bricks, hart_z, precision=HIGHEST)


def residual_inner(residual, precond):
    return lax.psum(jnp.sum(residual * precond), ("gx", "gy"))


def local(density, charge):
    eps = permittivity(density)
    kappa = KAPPA_SCALE * (eps - 1.0) / (EPS_SOLVENT - 1.0)
    cellsx = eps.shape[0]
    cellsy = eps.shape[1]
    eps_padded = extended(eps, (("gx", 0), ("gy", 1)), 2)
    strip_x = eps_padded[:, 2 : 2 + cellsy]
    faces_x = 0.5 * (strip_x[:-1] + strip_x[1:])
    strip_y = eps_padded[2 : 2 + cellsx]
    faces_y = 0.5 * (strip_y[:, :-1] + strip_y[:, 1:])
    faces_z = 0.5 * (eps + jnp.roll(eps, -1, 2))
    rhs = 4.0 * math.pi * charge
    residual = rhs
    precond = precondition(residual)
    inner_now = residual_inner(residual, precond)
    image = operate(precond, faces_x, faces_y, faces_z, kappa)
    alpha = inner_now / lax.psum(jnp.sum(precond * image), ("gx", "gy"))
    solution_field = alpha * precond
    residual = residual - alpha * image
    return (solution_field, residual)


def solution(mesh):
    placed = (P("gx", "gy", None), P("gx", "gy", None))
    return jax.shard_map(
        local,
        mesh=mesh,
        in_specs=placed,
        out_specs=(P("gx", "gy", None), P("gx", "gy", None)),
        check_vma=False,
    )
```

profile of v0, /device:TPU:0, one launch (start us, length us, event | category | flops | bytes accessed | tf_op | source)
XLA Modules:
  0.0 139.0 jit_solution(10146124797497846084)
XLA Ops:
  0.6 4.3 %fusion.4 = f32[20,10,384]{2,0,1:T(8,128)S(1)} fusion(f32[20,10,384]{2,0,1:T(8,128)} %param.3), kind=kOutput, calls=%fused_computation.7 | convolution fusion | flops 355445760 | bytes 614400 | tf_op jit(solution)/shard_map/dot_general | solution.py:96
  4.9 1.4 %copy.11 = f32[20,10,384]{0,1,2:T(8,128)S(1)} copy(f32[20,10,384]{2,0,1:T(8,128)S(1)} %fusion.4) | data formatting | bytes 614400 | tf_op jit(solution)/shard_map/dot_general | solution.py:96
  6.3 1.9 %reshape.76 = f32[4,1,19200]{2,1,0:T(1,128)} reshape(f32[384,10,20]{2,1,0:T(8,128)S(1)} %bitcast.54) | data formatting | bytes 614400
  8.2 4.2 %all-to-all-start = ((f32[4,1,19200]{2,1,0:T(1,128)}), f32[4,1,19200]{2,1,0:T(1,128)S(1)}, u32[]{:S(2)}, u32[]{:S(2)}) async-start(f32[4,1,19200]{2,1,0:T(1,128)} %reshape.76), calls=%async_computation | async-start | bytes 614400 | tf_op jit(solution)/shard_map/all_to_all | solution.py:99
  12.4 6.5 %all-to-all-done = f32[4,1,19200]{2,1,0:T(1,128)S(1)} async-done(((f32[4,1,19200]{2,1,0:T(1,128)}), f32[4,1,19200]{2,1,0:T(1,128)S(1)}, u32[]{:S(2)}, u32[]{:S(2)}) %all-to-all-start) | async-done | bytes 307232 | tf_op jit(solution)/shard_map/all_to_all | solution.py:99
  19.0 0.5 broadcast.171
  19.5 1.5 %reduce = f32[4,19200]{1,0:T(4,128)S(1)} reduce(f32[4,1,19200]{2,1,0:T(1,128)S(1)} %all-to-all-done, f32[]{:T(128)} %broadcast.171), dimensions={1}, to_apply=%all_to_all.52.reduce_sub_computation | reduce | bytes 614404 | tf_op jit(solution)/shard_map/all_to_all | solution.py:99
  21.0 1.2 reshape.77
  22.2 1.9 %copy.12 = f32[20,10,4,96]{3,0,2,1:T(8,128)} copy(f32[20,10,4,96]{0,1,3,2:T(8,128)S(1)} %bitcast.53) | data formatting | bytes 614400 | tf_op jit(solution)/shard_map/all_to_all | solution.py:99
  24.1 1.1 all_to_all.55
  25.2 0.7 fusion.50
  25.9 0.1 copy.31
  26.1 1.3 reshape.78
  27.3 6.4 %all-to-all-start.1 = ((f32[8,1,9600]{2,1,0:T(1,128)}), f32[8,1,9600]{2,1,0:T(1,128)S(1)}, u32[]{:S(2)}, u32[]{:S(2)}) async-start(f32[8,1,9600]{2,1,0:T(1,128)} %reshape.78), calls=%async_computation.1 | async-start | bytes 614400 | tf_op jit(solution)/shard_map/all_to_all | solution.py:101
  33.9 0.1 broadcast_add_fusion
  34.0 9.4 %all-to-all-done.1 = f32[8,1,9600]{2,1,0:T(1,128)S(1)} async-done(((f32[8,1,9600]{2,1,0:T(1,128)}), f32[8,1,9600]{2,1,0:T(1,128)S(1)}, u32[]{:S(2)}, u32[]{:S(2)}) %all-to-all-start.1) | async-done | bytes 307232 | tf_op jit(solution)/shard_map/all_to_all | solution.py:101
  43.5 1.4 reduce.1
  44.8 0.3 reshape.79
  45.1 0.1 copy.15
  45.2 0.7 convolution_divide_fusion
  45.9 0.7 fusion.47
  46.6 0.1 copy.30
  46.8 1.3 reshape.80
  48.0 3.6 %all-to-all-start.2 = ((f32[8,1,9600]{2,1,0:T(1,128)}), f32[8,1,9600]{2,1,0:T(1,128)S(1)}, u32[]{:S(2)}, u32[]{:S(2)}) async-start(f32[8,1,9600]{2,1,0:T(1,128)} %reshape.80), calls=%async_computation.2 | async-start | bytes 614400 | tf_op jit(solution)/shard_map/all_to_all | solution.py:117
  51.6 1.3 multiply_exponential_fusion
  53.1 1.7 %collective-permute-start.1 = (f32[2,10,384]{2,0,1:T(2,128)S(1)}, f32[2,10,384]{2,0,1:T(2,128)S(1)}, u32[]{:S(2)}, u32[]{:S(2)}) collective-permute-start(f32[2,10,384]{2,0,1:T(2,128)S(1)} %get-tuple-element.12), channel_id=1, source_target_pairs={{8,0},{16,8},{24,16},{0,24},{9,1},{17,9},{25,17},{1,25},{10,2},{18... | collective-permute-start | bytes 92168 | tf_op jit(solution)/shard_map/ppermute | solution.py:26
  54.8 0.2 slice.204
  55.0 1.4 %collective-permute-done = f32[2,10,384]{2,0,1:T(2,128)S(1)} collective-permute-done((f32[2,10,384]{2,0,1:T(2,128)S(1)}, f32[2,10,384]{2,0,1:T(2,128)S(1)}, u32[]{:S(2)}, u32[]{:S(2)}) %collective-permute-start) | collective-permute-done | bytes 30752 | tf_op jit(solution)/shard_map/ppermute | solution.py:23
  56.4 2.1 %collective-permute-start.4 = (f32[24,2,384]{2,0,1:T(8,128)S(1)}, f32[24,2,384]{2,0,1:T(8,128)S(1)}, u32[]{:S(2)}, u32[]{:S(2)}) collective-permute-start(f32[24,2,384]{2,0,1:T(8,128)S(1)} %get-tuple-element.9), channel_id=1, source_target_pairs={{0,1},{1,2},{2,3},{3,4},{4,5},{5,6},{6,7},{7,0},{8,9},{9,10},{10,1... | collective-permute-start | bytes 221192 | tf_op jit(solution)/shard_map/ppermute | solution.py:23
  58.5 2.8 %collective-permute-start.5 = (f32[24,2,384]{2,0,1:T(8,128)S(1)}, f32[24,2,384]{2,0,1:T(8,128)S(1)}, u32[]{:S(2)}, u32[]{:S(2)}) collective-permute-start(f32[24,2,384]{2,0,1:T(8,128)S(1)} %get-tuple-element.10), channel_id=1, source_target_pairs={{1,0},{2,1},{3,2},{4,3},{5,4},{6,5},{7,6},{0,7},{9,8},{10,9},{11,1... | collective-permute-start | bytes 221192 | tf_op jit(solution)/shard_map/ppermute | solution.py:26
  61.3 1.4 reduce.2
  62.6 0.3 reshape.81
  62.9 0.1 copy.18
  63.0 0.7 fusion.45
  63.7 0.1 copy.19
  63.9 1.3 reshape.82
  65.1 3.7 %all-to-all-start.3 = ((f32[4,1,19200]{2,1,0:T(1,128)}), f32[4,1,19200]{2,1,0:T(1,128)S(1)}, u32[]{:S(2)}, u32[]{:S(2)}) async-start(f32[4,1,19200]{2,1,0:T(1,128)} %reshape.82), calls=%async_computation.3 | async-start | bytes 614400 | tf_op jit(solution)/shard_map/all_to_all | solution.py:119
  68.8 0.1 pad_maximum_fusion.9
  68.9 0.1 pad_maximum_fusion.1
  69.0 6.2 %all-to-all-done.3 = f32[4,1,19200]{2,1,0:T(1,128)S(1)} async-done(((f32[4,1,19200]{2,1,0:T(1,128)}), f32[4,1,19200]{2,1,0:T(1,128)S(1)}, u32[]{:S(2)}, u32[]{:S(2)}) %all-to-all-start.3) | async-done | bytes 307232 | tf_op jit(solution)/shard_map/all_to_all | solution.py:119
  75.2 1.5 %reduce.3 = f32[4,19200]{1,0:T(4,128)S(1)} reduce(f32[4,1,19200]{2,1,0:T(1,128)S(1)} %all-to-all-done.3, f32[]{:T(128)} %broadcast.171), dimensions={1}, to_apply=%all_to_all.64.reduce_sub_computation | reduce | bytes 614404 | tf_op jit(solution)/shard_map/all_to_all | solution.py:119
  76.7 0.3 reshape.83
  77.1 0.3 copy.21
  77.4 0.2 all_to_all.67
  77.6 3.3 %fusion.2 = f32[20,10,384]{2,0,1:T(8,128)S(1)} fusion(f32[20,10,384]{2,0,1:T(8,128)S(1)} %all_to_all.67), kind=kOutput, calls=%fused_computation.5 | convolution fusion | flops 355368960 | bytes 614400 | tf_op jit(solution)/shard_map/dot_general | solution.py:120
  80.9 0.2 fusion.81
  81.1 0.1 fusion.80
  81.2 0.2 slice.208
  81.4 1.7 %collective-permute-start.3 = (f32[3,10,384]{2,0,1:T(4,128)S(1)}, f32[3,10,384]{2,0,1:T(4,128)S(1)}, u32[]{:S(2)}, u32[]{:S(2)}) collective-permute-start(f32[3,10,384]{2,0,1:T(4,128)S(1)} %get-tuple-element.14), channel_id=1, source_target_pairs={{8,0},{16,8},{24,16},{0,24},{9,1},{17,9},{25,17},{1,25},{10,2},{18... | collective-permute-start | bytes 138248 | tf_op jit(solution)/shard_map/ppermute | solution.py:26
  83.1 1.5 %fusion.29 = f32[20,10,384]{2,0,1:T(8,128)S(1)} fusion(f32[20,10,1]{2,0,1:T(8,128)S(1)} %slice-done, f32[20,10,383]{2,0,1:T(8,128)S(1)} %slice.204, f32[20,10,384]{2,0,1:T(8,128)S(1)} %fusion.2, f32[20,10,1]{2,0,1:T(8,128)S(1)} %get-tuple-element.20, f32[20,10,383]{2,0,1:T(8,128)S(1)} %get-tuple-element.22, f32[20,10,2]{2,0,1:T(8,128)S(1)} %slice.209, ...), kind=kLoop, calls=%fused_computation.53 | loop fusion | flops 1459200 | bytes 2150400 | tf_op jit(solution)/shard_map/mul | solution.py:72
  84.7 0.2 fusion.79
  84.8 0.1 fusion.78
  84.9 0.1 slice.216
  85.1 0.1 pad_maximum_fusion.2
  85.2 1.2 collective-permute-start.6
  86.4 3.6 %collective-permute-start.7 = (f32[26,3,384]{2,0,1:T(8,128)S(1)}, f32[26,3,384]{2,0,1:T(8,128)S(1)}, u32[]{:S(2)}, u32[]{:S(2)}) collective-permute-start(f32[26,3,384]{2,0,1:T(8,128)S(1)} %get-tuple-element.7), channel_id=1, source_target_pairs={{1,0},{2,1},{3,2},{4,3},{5,4},{6,5},{7,6},{0,7},{9,8},{10,9},{11,1... | collective-permute-start | bytes 359432 | tf_op jit(solution)/shard_map/ppermute | solution.py:26
  90.0 0.2 fusion.26
  90.2 4.3 %collective-permute-done.6 = f32[26,3,384]{2,0,1:T(8,128)S(1)} collective-permute-done((f32[26,3,384]{2,0,1:T(8,128)S(1)}, f32[26,3,384]{2,0,1:T(8,128)S(1)}, u32[]{:S(2)}, u32[]{:S(2)}) %collective-permute-start.6) | collective-permute-done | bytes 119840 | tf_op jit(solution)/shard_map/ppermute | solution.py:23
  94.5 1.0 collective-permute-done.7
  95.5 0.1 pad_maximum_fusion
  95.6 0.3 fusion.12
  95.9 2.5 %multiply_reduce_fusion = (f32[]{:T(128)}, f32[]{:T(128)}, f32[20,10,384]{2,0,1:T(8,128)S(1)}) fusion(f32[20,10,384]{2,0,1:T(8,128)S(1)} %fusion.2, f32[20,10,384]{2,0,1:T(8,128)S(1)} %copy-done.2, f32[20,10,382]{2,0,1:T(8,128)S(1)} %bitcast.52, f32[20,10,2]{2,0,1:T(8,128)S(1)} %slice.216, f32[20,10,1]{2,0,1:T(8,128)S(1)} %get-tuple-element.16, ...), kind=kLoop, calls=%fused_computation.64 | loop fusion | flops 2611198 | bytes 4915208 | tf_op jit(solution)/shard_map/reduce_sum | solution.py:143
  98.4 38.3 %all-reduce = (f32[]{:T(128)}, f32[]{:T(128)}) all-reduce(f32[]{:T(128)} %get-tuple-element.3, f32[]{:T(128)} %get-tuple-element.2), channel_id=1, replica_groups=mesh['gx'=4,'gy'=8] {'gx','gy'}, use_global_device_ids=true, to_apply=%region_1.2 | all-reduce | flops 2 | bytes 16 | tf_op jit(solution)/shard_map/psum | solution.py:124
  138.1 0.9 multiply_subtract_fusion
  (26 shorter events, 0.5 us)
Async XLA Ops:
  8.2 10.8 %all-to-all-start = ((f32[4,1,19200]{2,1,0:T(1,128)}), f32[4,1,19200]{2,1,0:T(1,128)S(1)}, u32[]{:S(2)}, u32[]{:S(2)}) async-start(f32[4,1,19200]{2,1,0:T(1,128)} %reshape.76), calls=%async_computation | async-start | bytes 614400 | tf_op jit(solution)/shard_map/all_to_all | solution.py:99
  27.3 16.1 %all-to-all-start.1 = ((f32[8,1,9600]{2,1,0:T(1,128)}), f32[8,1,9600]{2,1,0:T(1,128)S(1)}, u32[]{:S(2)}, u32[]{:S(2)}) async-start(f32[8,1,9600]{2,1,0:T(1,128)} %reshape.78), calls=%async_computation.1 | async-start | bytes 614400 | tf_op jit(solution)/shard_map/all_to_all | solution.py:101
  45.2 6.5 %copy-start.1 = (f32[20,10,384]{2,0,1:T(8,128)S(1)}, f32[20,10,384]{2,0,1:T(8,128)}, u32[]{:S(2)}) copy-start(f32[20,10,384]{2,0,1:T(8,128)} %param.2) | copy-start | bytes 921604
  48.0 13.2 %all-to-all-start.2 = ((f32[8,1,9600]{2,1,0:T(1,128)}), f32[8,1,9600]{2,1,0:T(1,128)S(1)}, u32[]{:S(2)}, u32[]{:S(2)}) async-start(f32[8,1,9600]{2,1,0:T(1,128)} %reshape.80), calls=%async_computation.2 | async-start | bytes 614400 | tf_op jit(solution)/shard_map/all_to_all | solution.py:117
  53.0 16.0 %copy-start = (f32[20,10,384]{2,0,1:T(8,128)}, f32[20,10,384]{2,0,1:T(8,128)S(1)}, u32[]{:S(2)}) copy-start(f32[20,10,384]{2,0,1:T(8,128)S(1)} %multiply_exponential_fusion) | copy-start | bytes 921604
  53.0 3.4 %collective-permute-start = (f32[2,10,384]{2,0,1:T(2,128)S(1)}, f32[2,10,384]{2,0,1:T(2,128)S(1)}, u32[]{:S(2)}, u32[]{:S(2)}) collective-permute-start(f32[2,10,384]{2,0,1:T(2,128)S(1)} %get-tuple-element.11), channel_id=1, source_target_pairs={{0,8},{8,16},{16,24},{24,0},{1,9},{9,17},{17,25},{25,1},{2,10},{10... | collective-permute-start | bytes 92168 | tf_op jit(solution)/shard_map/ppermute | solution.py:23
  53.1 3.3 %collective-permute-start.1 = (f32[2,10,384]{2,0,1:T(2,128)S(1)}, f32[2,10,384]{2,0,1:T(2,128)S(1)}, u32[]{:S(2)}, u32[]{:S(2)}) collective-permute-start(f32[2,10,384]{2,0,1:T(2,128)S(1)} %get-tuple-element.12), channel_id=1, source_target_pairs={{8,0},{16,8},{24,16},{0,24},{9,1},{17,9},{25,17},{1,25},{10,2},{18... | collective-permute-start | bytes 92168 | tf_op jit(solution)/shard_map/ppermute | solution.py:26
  56.4 12.5 %collective-permute-start.4 = (f32[24,2,384]{2,0,1:T(8,128)S(1)}, f32[24,2,384]{2,0,1:T(8,128)S(1)}, u32[]{:S(2)}, u32[]{:S(2)}) collective-permute-start(f32[24,2,384]{2,0,1:T(8,128)S(1)} %get-tuple-element.9), channel_id=1, source_target_pairs={{0,1},{1,2},{2,3},{3,4},{4,5},{5,6},{6,7},{7,0},{8,9},{9,10},{10,1... | collective-permute-start | bytes 221192 | tf_op jit(solution)/shard_map/ppermute | solution.py:23
  58.5 10.4 %collective-permute-start.5 = (f32[24,2,384]{2,0,1:T(8,128)S(1)}, f32[24,2,384]{2,0,1:T(8,128)S(1)}, u32[]{:S(2)}, u32[]{:S(2)}) collective-permute-start(f32[24,2,384]{2,0,1:T(8,128)S(1)} %get-tuple-element.10), channel_id=1, source_target_pairs={{1,0},{2,1},{3,2},{4,3},{5,4},{6,5},{7,6},{0,7},{9,8},{10,9},{11,1... | collective-permute-start | bytes 221192 | tf_op jit(solution)/shard_map/ppermute | solution.py:26
  65.1 10.1 %all-to-all-start.3 = ((f32[4,1,19200]{2,1,0:T(1,128)}), f32[4,1,19200]{2,1,0:T(1,128)S(1)}, u32[]{:S(2)}, u32[]{:S(2)}) async-start(f32[4,1,19200]{2,1,0:T(1,128)} %reshape.82), calls=%async_computation.3 | async-start | bytes 614400 | tf_op jit(solution)/shard_map/all_to_all | solution.py:119
  77.3 5.8 %slice-start = ((f32[20,10,384]{2,0,1:T(8,128)}), f32[20,10,1]{2,0,1:T(8,128)S(1)}, s32[]{:S(2)}) async-start(f32[20,10,384]{2,0,1:T(8,128)} %copy-done), calls=%async_computation.4 | async-start | bytes 245760 | tf_op jit(solution)/shard_map/jit(_roll_static)/slice | solution.py:137
  81.3 3.7 %collective-permute-start.2 = (f32[3,10,384]{2,0,1:T(4,128)S(1)}, f32[3,10,384]{2,0,1:T(4,128)S(1)}, u32[]{:S(2)}, u32[]{:S(2)}) collective-permute-start(f32[3,10,384]{2,0,1:T(4,128)S(1)} %get-tuple-element.13), channel_id=1, source_target_pairs={{0,8},{8,16},{16,24},{24,0},{1,9},{9,17},{17,25},{25,1},{2,10},{10... | collective-permute-start | bytes 138248 | tf_op jit(solution)/shard_map/ppermute | solution.py:23
  81.4 3.7 %collective-permute-start.3 = (f32[3,10,384]{2,0,1:T(4,128)S(1)}, f32[3,10,384]{2,0,1:T(4,128)S(1)}, u32[]{:S(2)}, u32[]{:S(2)}) collective-permute-start(f32[3,10,384]{2,0,1:T(4,128)S(1)} %get-tuple-element.14), channel_id=1, source_target_pairs={{8,0},{16,8},{24,16},{0,24},{9,1},{17,9},{25,17},{1,25},{10,2},{18... | collective-permute-start | bytes 138248 | tf_op jit(solution)/shard_map/ppermute | solution.py:26
  85.2 9.3 %collective-permute-start.6 = (f32[26,3,384]{2,0,1:T(8,128)S(1)}, f32[26,3,384]{2,0,1:T(8,128)S(1)}, u32[]{:S(2)}, u32[]{:S(2)}) collective-permute-start(f32[26,3,384]{2,0,1:T(8,128)S(1)} %get-tuple-element.8), channel_id=1, source_target_pairs={{0,1},{1,2},{2,3},{3,4},{4,5},{5,6},{6,7},{7,0},{8,9},{9,10},{10,1... | collective-permute-start | bytes 359432 | tf_op jit(solution)/shard_map/ppermute | solution.py:23
  86.4 9.5 %copy-start.2 = (f32[20,10,384]{2,0,1:T(8,128)S(1)}, f32[20,10,384]{2,0,1:T(8,128)}, u32[]{:S(2)}) copy-start(f32[20,10,384]{2,0,1:T(8,128)} %param.3) | copy-start | bytes 921604
  86.4 9.1 %collective-permute-start.7 = (f32[26,3,384]{2,0,1:T(8,128)S(1)}, f32[26,3,384]{2,0,1:T(8,128)S(1)}, u32[]{:S(2)}, u32[]{:S(2)}) collective-permute-start(f32[26,3,384]{2,0,1:T(8,128)S(1)} %get-tuple-element.7), channel_id=1, source_target_pairs={{1,0},{2,1},{3,2},{4,3},{5,4},{6,5},{7,6},{0,7},{9,8},{10,9},{11,1... | collective-permute-start | bytes 359432 | tf_op jit(solution)/shard_map/ppermute | solution.py:26
where the time goes:
time: 140 us; the launch traced here: 139 us
  blocking collectives  38.3 us (27%)
  starting transfers between devices  31.1 us (22%)
  waiting for transfers between devices  28.9 us (21%)
  local copies, waits for them, and re-layouts  14.9 us (11%)
  other arithmetic  13.1 us (9%)
  matrix products  10.3 us (7%)
  between operations  2.37 us (2%)
    psum x1, blocking collectives, residual_inner(): return lax.psum(jnp.sum(residual * precond), ('gx', 'gy'))  38.3 us
    ppermute x4, starting transfers between devices, extended(): lax.ppermute(lax.slice_in_dim(block, 0, width, axis=dim), axis, backward)  9.79 us
    all_to_all x1, waiting for transfers between devices, precondition(): lax.all_to_all(along_x, 'gy', split_axis=2, concat_axis=0, tiled=True)  9.44 us
    unnamed x14, local copies, waits for them, and re-layouts  7.8 us
    all_to_all x1, waiting for transfers between devices, precondition(): lax.all_to_all(forward, 'gx', split_axis=2, concat_axis=0, tiled=True)  6.52 us
    all_to_all x1, starting transfers between devices, precondition(): lax.all_to_all(along_x, 'gy', split_axis=2, concat_axis=0, tiled=True)  6.44 us
    all_to_all x1, waiting for transfers between devices, precondition(): lax.all_to_all(back_x, 'gx', split_axis=0, concat_axis=2, tiled=True)  6.23 us
    ppermute x4, waiting for transfers between devices, extended(): lax.ppermute(lax.slice_in_dim(block, block.shape[dim] - width, None, axis...  5.7 us
  transfers between devices with their start and end apart: 12, of which 6 were waited for; matrix products, arithmetic and copies ran while one was open for 6% of the time, Pallas kernels for 0%

commit v1 on v0

--- a/solution.py
+++ b/solution.py
@@ -2,7 +2,11 @@
 
 import jax
 import jax.numpy as jnp
+import ml_dtypes
+import numpy as np
 from jax import lax
+from jax.experimental import pallas as pl
+from jax.experimental.pallas import tpu as pltpu
 from jax.sharding import PartitionSpec as P
 
 EPS_SOLVENT = 78.3
@@ -12,6 +16,9 @@
 EPS_PRECOND = 20.0
 SHIFT_PRECOND = 0.05
 HIGHEST = lax.Precision.HIGHEST
+LANES = 128
+HALO = 3
+VMEM_LIMIT = 48 << 20
 
 
 def extended(block, sides, width):
@@ -124,7 +131,7 @@
     return lax.psum(jnp.sum(residual * precond), ("gx", "gy"))
 
 
-def local(density, charge):
+def local_lines(density, charge):
     eps = permittivity(density)
     kappa = KAPPA_SCALE * (eps - 1.0) / (EPS_SOLVENT - 1.0)
     cellsx = eps.shape[0]
@@ -146,6 +153,405 @@
     return (solution_field, residual)
 
 
+def cas_table(rows, columns, length):
+    angle = (np.outer(rows, columns) % length).astype(np.float64) * (2.0 * np.pi / length)
+    return np.cos(angle) + np.sin(angle)
+
+
+def symbol_table(length):
+    halfang = np.arange(length, dtype=np.float64) * (np.pi / length)
+    return ((27.0 * np.sin(halfang) - np.sin(3.0 * halfang)) / 12.0) ** 2
+
+
+def halves(table):
+    high = table.astype(ml_dtypes.bfloat16)
+    low = (table - high.astype(np.float64)).astype(ml_dtypes.bfloat16)
+    return high, low
+
+
+def split(values):
+    high = values.astype(jnp.bfloat16)
+    low = (values - high.astype(jnp.float32)).astype(jnp.bfloat16)
+    return high, low
+
+
+def mul(left, right):
+    return jnp.dot(left, right, preferred_element_type=jnp.float32)
+
+
+def mul_t(left, right):
+    return lax.dot_general(
+        left, right, (((1,), (1,)), ((), ())), preferred_element_type=jnp.float32
+    )
+
+
+class Plan:
+    def __init__(self, cellsx, cellsy, length_z, count_x, count_y):
+        self.cx, self.cy, self.nz = cellsx, cellsy, length_z
+        self.gx, self.gy = count_x, count_y
+        self.nd = count_x * count_y
+        self.nx, self.ny = cellsx * count_x, cellsy * count_y
+        self.kz = length_z // self.nd
+        self.xp = -(-cellsx // 8) * 8
+        self.xe = cellsx + 2 * HALO
+        self.rows = -(-(self.xe + cellsx) // 8) * 8
+        self.xep = -(-self.xe // 8) * 8
+        self.group = LANES // max(self.kz, 1)
+        self.chunks = -(-self.nd // self.group)
+
+    def fits(self):
+        return (
+            self.nz % self.nd == 0
+            and self.nz % LANES == 0
+            and self.cy * self.kz <= LANES
+            and (self.cy * self.kz) % 8 == 0
+            and 2 * HALO * self.kz <= LANES
+            and self.cx >= HALO
+            and self.cy >= HALO
+            and self.nx <= LANES
+            and self.ny % 16 == 0
+            and self.gx * self.xep <= LANES
+        )
+
+    def z_columns(self):
+        wave = np.arange(self.nz)
+        place = (wave // self.kz // self.group) * LANES + (
+            wave // self.kz % self.group
+        ) * self.kz + wave % self.kz
+        return place
+
+    def z_forward(self):
+        table = np.zeros((self.nz, self.chunks * LANES))
+        table[:, self.z_columns()] = cas_table(np.arange(self.nz), np.arange(self.nz), self.nz)
+        return halves(table)
+
+    def z_backward(self):
+        high, low = self.z_forward()
+        return np.ascontiguousarray(high.T), np.ascontiguousarray(low.T)
+
+    def x_forward(self):
+        table = np.zeros((LANES, self.gx * self.xp))
+        for g in range(self.gx):
+            table[: self.nx, g * self.xp : g * self.xp + self.cx] = cas_table(
+                np.arange(self.nx), g * self.cx + np.arange(self.cx), self.nx
+            )
+        high, low = halves(table)
+        return np.concatenate([high, low, high], axis=1)
+
+    def y_table(self):
+        high, low = halves(cas_table(np.arange(self.ny), np.arange(self.ny), self.ny))
+        return np.concatenate([high, low, high], axis=1)
+
+    def x_backward(self):
+        extended_rows = np.zeros((self.gx * self.xep, LANES))
+        own_rows = np.zeros((self.gx * self.xp, LANES))
+        for g in range(self.gx):
+            x = (g * self.cx - HALO + np.arange(self.xe)) % self.nx
+            extended_rows[g * self.xep : g * self.xep + self.xe, : self.nx] = cas_table(
+                x, np.arange(self.nx), self.nx
+            )
+            x = g * self.cx + np.arange(self.cx)
+            own_rows[g * self.xp : g * self.xp + self.cx, : self.nx] = cas_table(
+                x, np.arange(self.nx), self.nx
+            )
+        high, low = halves(np.concatenate([extended_rows, own_rows], axis=0))
+        return np.concatenate([high, low, high], axis=1)
+
+    def scales(self):
+        lam_x, lam_y, lam_z = symbol_table(self.nx), symbol_table(self.ny), symbol_table(self.nz)
+        plane = np.full((self.ny, LANES), 1e30)
+        plane[:, : self.nx] = lam_x[None, :] + lam_y[:, None]
+        return plane.astype(np.float32), lam_z.reshape(self.nd, self.kz).astype(np.float32)
+
+
+def call(kernel, outs, args, scratch=(), flops=0):
+    vmem = pl.BlockSpec(memory_space=pltpu.VMEM)
+    nbytes = sum(int(np.prod(a.shape)) * a.dtype.itemsize for a in (*args, *outs))
+    return pl.pallas_call(
+        kernel,
+        out_shape=tuple(outs),
+        in_specs=[vmem] * len(args),
+        out_specs=tuple([vmem] * len(outs)),
+        scratch_shapes=list(scratch),
+        compiler_params=pltpu.CompilerParams(vmem_limit_bytes=VMEM_LIMIT),
+        cost_estimate=pl.CostEstimate(flops=flops, bytes_accessed=nbytes, transcendentals=0),
+    )(*args)
+
+
+def lane_index(rows):
+    return lax.broadcasted_iota(jnp.int32, (rows, LANES), 1)
+
+
+def moved(values, shift):
+    shift = shift % LANES
+    return values if shift == 0 else pltpu.roll(values, shift, 1)
+
+
+def forward_kernel(plan, charge, high_z, low_z, out):
+    p = plan
+    gap = jnp.zeros((p.xp - p.cx, p.nz), jnp.float32)
+    rows = []
+    for y in range(p.cy):
+        rows.append(charge[y])
+        if p.xp > p.cx:
+            rows.append(gap)
+    high, low = split(jnp.concatenate(rows, axis=0))
+    spec = mul(high, high_z[...]) + mul(low, high_z[...]) + mul(high, low_z[...])
+    lane = lane_index(p.xp)
+    for target in range(p.nd):
+        chunk, slot = divmod(target, p.group)
+        block = jnp.zeros((p.xp, LANES), jnp.float32)
+        for y in range(p.cy):
+            part = spec[y * p.xp : (y + 1) * p.xp, chunk * LANES : (chunk + 1) * LANES]
+            part = moved(part, (y - slot) * p.kz)
+            block = jnp.where((lane >= y * p.kz) & (lane < (y + 1) * p.kz), part, block)
+        out[target] = block
+
+
+def plane_kernel(plan, lines, x_fwd, y_both, x_bwd, plane, waves, out, turned, planes):
+    p = plan
+    step = p.cy * p.kz
+    field = jnp.concatenate(
+        [
+            jnp.concatenate([lines[gx * p.gy + gy] for gx in range(p.gx)], axis=0)
+            for gy in range(p.gy)
+        ],
+        axis=1,
+    )
+    high, low = split(field)
+    along_x = mul(x_fwd[...], jnp.concatenate([high, high, low], axis=0))
+    for gy in range(p.gy):
+        turned[pl.ds(gy * step, LANES), :] = along_x[:, gy * LANES : (gy + 1) * LANES].T
+    field = jnp.concatenate(
+        [turned[pl.ds(k, p.ny, stride=p.kz), :] for k in range(p.kz)], axis=1
+    )
+    high, low = split(field)
+    along_y = mul(y_both[...], jnp.concatenate([high, high, low], axis=0))
+    total = 4.0 * math.pi / float(p.nx * p.ny * p.nz)
+    scaled = []
+    for k in range(p.kz):
+        symbol = EPS_PRECOND * (plane[...] + waves[k]) + SHIFT_PRECOND
+        scaled.append(along_y[:, k * LANES : (k + 1) * LANES] * (total / symbol))
+    high, low = split(jnp.concatenate(scaled, axis=1))
+    back_y = mul(y_both[...], jnp.concatenate([high, high, low], axis=0))
+    edge = HALO * p.kz
+    base = -(-edge // 8) * 8
+    for k in range(p.kz):
+        planes[pl.ds(base + k, p.ny, stride=p.kz), :] = back_y[:, k * LANES : (k + 1) * LANES]
+    planes[pl.ds(base - edge, edge), :] = planes[pl.ds(base + p.ny * p.kz - edge, edge), :]
+    planes[pl.ds(base + p.ny * p.kz, edge), :] = planes[pl.ds(base, edge), :]
+    cut = p.gx * p.xep
+    for gy in range(p.gy):
+        start = base + gy * step
+        high, low = split(planes[pl.ds(start, LANES), :])
+        ext = mul_t(x_bwd[:cut, :], jnp.concatenate([high, high, low], axis=1))
+        sides = jnp.concatenate(
+            [
+                planes[pl.ds(start - edge, edge), :],
+                planes[pl.ds(start + step, edge), :],
+                jnp.zeros((LANES - 2 * edge, LANES), jnp.float32),
+            ],
+            axis=0,
+        )
+        high, low = split(sides)
+        own = mul_t(x_bwd[cut:, :], jnp.concatenate([high, high, low], axis=1))
+        for gx in range(p.gx):
+            out[gx * p.gy + gy, : p.xe] = ext[gx * p.xep : gx * p.xep + p.xe]
+            out[gx * p.gy + gy, p.xe : p.xe + p.cx] = own[gx * p.xp : gx * p.xp + p.cx]
+            rest = p.rows - p.xe - p.cx
+            if rest:
+                out[gx * p.gy + gy, p.xe + p.cx :] = jnp.zeros((rest, LANES), jnp.float32)
+
+
+def stencil_kernel(
+    plan, blocks, high_z, low_z, charge, eps, ex_low, ex_high, ey_low, ey_high,
+    pre, image, sums, z_high, z_low, field, eps_x, eps_y,
+):
+    p = plan
+    lane = lane_index(p.xep)
+    for chunk in range(p.chunks):
+        count = min(p.group, p.nd - chunk * p.group)
+        for y in range(p.cy + 2 * HALO):
+            inner = HALO <= y < HALO + p.cy
+            if inner:
+                first, rows, piece = 0, p.xep, y - HALO
+                at = piece * p.xep
+            else:
+                piece = y if y < HALO else y - p.cy
+                first, rows = p.xe, p.xp
+                at = p.cy * p.xep + piece * p.xp
+            line = jnp.zeros((rows, LANES), jnp.float32)
+            for slot in range(count):
+                part = blocks[chunk * p.group + slot, first : min(first + rows, p.rows), :]
+                if part.shape[0] < rows:
+                    part = jnp.concatenate(
+                        [part, jnp.zeros((rows - part.shape[0], LANES), jnp.float32)], axis=0
+                    )
+                part = moved(part, (slot - piece) * p.kz)
+                here = lane[:rows]
+                line = jnp.where((here >= slot * p.kz) & (here < (slot + 1) * p.kz), part, line)
+            high, low = split(line)
+            z_high[at : at + rows, chunk * LANES : (chunk + 1) * LANES] = high
+            z_low[at : at + rows, chunk * LANES : (chunk + 1) * LANES] = low
+    whole = (
+        mul(z_high[...], high_z[...]) + mul(z_low[...], high_z[...]) + mul(z_high[...], low_z[...])
+    )
+    for y in range(p.cy):
+        field[HALO + y] = whole[y * p.xep : (y + 1) * p.xep]
+    for piece in range(2 * HALO):
+        at = p.cy * p.xep + piece * p.xp
+        y = piece if piece < HALO else piece + p.cy
+        field[y, HALO : HALO + p.cx] = whole[at : at + p.cx]
+    eps_x[:, 0:2, :] = ex_low[...]
+    eps_x[:, 2 : 2 + p.cx, :] = eps[...]
+    eps_x[:, 2 + p.cx : 4 + p.cx, :] = ex_high[...]
+    eps_y[0:2] = ey_low[...]
+    eps_y[2 : 2 + p.cy] = eps[...]
+    eps_y[2 + p.cy : 4 + p.cy] = ey_high[...]
+
+    def stretch(flux_at):
+        return 27.0 * (flux_at(2) - flux_at(1)) - (flux_at(3) - flux_at(0))
+
+    rz = jnp.zeros((p.cx, LANES), jnp.float32)
+    dot = jnp.zeros((p.cx, LANES), jnp.float32)
+    faces_y = {}
+
+    def face_y(y):
+        if y not in faces_y:
+            val = [field[y + i, HALO : HALO + p.cx, :] for i in range(4)]
+            grad = 27.0 * (val[2] - val[1]) - (val[3] - val[0])
+            faces_y[y] = (eps_y[y] + eps_y[y + 1]) * grad
+        return faces_y[y]
+
+    for y in range(p.cy):
+        line = field[HALO + y]
+        val = [line[i : i + p.cx + 3] for i in range(4)]
+        grad = 27.0 * (val[2] - val[1]) - (val[3] - val[0])
+        eps_line = eps_x[y]
+        flux = (eps_line[0 : p.cx + 3] + eps_line[1 : p.cx + 4]) * grad
+        term = stretch(lambda i: flux[i : i + p.cx])
+        term = term + stretch(lambda i: face_y(y + i))
+        here = line[HALO : HALO + p.cx]
+        eps_here = eps[y]
+        n = p.nz
+        grad = 27.0 * (pltpu.roll(here, n - 1, 1) - here) - (
+            pltpu.roll(here, n - 2, 1) - pltpu.roll(here, 1, 1)
+        )
+        flux = (eps_here + pltpu.roll(eps_here, n - 1, 1)) * grad
+        term = term + (
+            27.0 * (flux - pltpu.roll(flux, 1, 1))
+            - (pltpu.roll(flux, n - 1, 1) - pltpu.roll(flux, 2, 1))
+        )
+        result = (KAPPA_SCALE / (EPS_SOLVENT - 1.0)) * (eps_here - 1.0) * here - term * (0.5 / 576.0)
+        pre[y] = here
+        image[y] = result
+        one = charge[y] * here
+        two = result * here
+        for c in range(n // LANES):
+            rz = rz + one[:, c * LANES : (c + 1) * LANES]
+            dot = dot + two[:, c * LANES : (c + 1) * LANES]
+    rz = jnp.sum(rz, axis=0, keepdims=True)
+    dot = jnp.sum(dot, axis=0, keepdims=True)
+    half = LANES // 2
+    rz = rz + pltpu.roll(rz, half, 1)
+    dot = dot + pltpu.roll(dot, half, 1)
+    both = jnp.where(lane_index(1) < half, rz, dot)
+    sums[...] = jnp.broadcast_to(both[None], sums.shape)
+
+
+def update_kernel(plan, sums, charge, pre, image, solution_field, residual):
+    p = plan
+    half = LANES // 2
+    total = jnp.sum(sums[...], axis=0)
+    lane = lane_index(1)
+    rz = jnp.sum(jnp.where(lane < half, total, 0.0), axis=1, keepdims=True)
+    dot = jnp.sum(jnp.where(lane < half, 0.0, total), axis=1, keepdims=True)
+    alpha = jnp.broadcast_to((4.0 * math.pi) * rz / dot, (p.cx, p.nz))
+    for y in range(p.cy):
+        solution_field[y] = alpha * pre[y]
+        residual[y] = (4.0 * math.pi) * charge[y] - alpha * image[y]
+
+
+def local_planes(plan, density, charge):
+    p = plan
+    axes = ("gx", "gy")
+    f32 = jnp.float32
+
+    def shape(*dims, kind=f32):
+        return jax.ShapeDtypeStruct(dims, kind)
+
+    density = density.transpose(1, 0, 2)
+    charge = charge.transpose(1, 0, 2)
+    high_z, low_z = p.z_forward()
+    (lines,) = call(
+        lambda *refs: forward_kernel(p, *refs),
+        [shape(p.nd, p.xp, LANES)],
+        [charge, jnp.asarray(high_z), jnp.asarray(low_z)],
+    )
+    lines = lax.all_to_all(lines, axes, 0, 0)
+    eps = permittivity(density)
+    fwd_x = [(i, (i + 1) % p.gx) for i in range(p.gx)]
+    fwd_y = [(i, (i + 1) % p.gy) for i in range(p.gy)]
+    ex_low = lax.ppermute(eps[:, p.cx - 2 :], "gx", fwd_x)
+    ex_high = lax.ppermute(eps[:, :2], "gx", [(b, a) for a, b in fwd_x])
+    ey_low = lax.ppermute(eps[p.cy - 2 :], "gy", fwd_y)
+    ey_high = lax.ppermute(eps[:2], "gy", [(b, a) for a, b in fwd_y])
+    plane, waves = p.scales()
+    me = lax.axis_index("gx") * p.gy + lax.axis_index("gy")
+    mine = lax.dynamic_slice_in_dim(jnp.asarray(waves), me, 1, axis=0)
+    mine = jnp.broadcast_to(mine.reshape(p.kz, 1, 1), (p.kz, 1, LANES))
+    edge = -(-HALO * p.kz // 8) * 8
+    (blocks,) = call(
+        lambda *refs: plane_kernel(p, *refs),
+        [shape(p.nd, p.rows, LANES)],
+        [
+            lines,
+            jnp.asarray(p.x_forward()),
+            jnp.asarray(p.y_table()),
+            jnp.asarray(p.x_backward()),
+            jnp.asarray(plane),
+            mine,
+        ],
+        [
+            pltpu.VMEM((p.ny * p.kz + LANES, LANES), f32),
+            pltpu.VMEM((2 * edge + p.ny * p.kz + LANES, LANES), f32),
+        ],
+    )
+    blocks = lax.all_to_all(blocks, axes, 0, 0)
+    back_high, back_low = p.z_backward()
+    nrows = p.cy * p.xep + 2 * HALO * p.xp
+    pre, image, sums = call(
+        lambda *refs: stencil_kernel(p, *refs),
+        [shape(p.cy, p.cx, p.nz), shape(p.cy, p.cx, p.nz), shape(p.nd, 1, LANES)],
+        [
+            blocks, jnp.asarray(back_high), jnp.asarray(back_low), charge,
+            eps, ex_low, ex_high, ey_low, ey_high,
+        ],
+        [
+            pltpu.VMEM((nrows, p.chunks * LANES), jnp.bfloat16),
+            pltpu.VMEM((nrows, p.chunks * LANES), jnp.bfloat16),
+            pltpu.VMEM((p.cy + 2 * HALO, p.xep, p.nz), f32),
+            pltpu.VMEM((p.cy, p.cx + 4, p.nz), f32),
+            pltpu.VMEM((p.cy + 4, p.cx, p.nz), f32),
+        ],
+    )
+    sums = lax.all_to_all(sums, axes, 0, 0)
+    solution_field, residual = call(
+        lambda *refs: update_kernel(p, *refs),
+        [shape(p.cy, p.cx, p.nz), shape(p.cy, p.cx, p.nz)],
+        [sums, charge, pre, image],
+    )
+    return solution_field.transpose(1, 0, 2), residual.transpose(1, 0, 2)
+
+
+def local(density, charge):
+    cellsx, cellsy, length_z = charge.shape
+    plan = Plan(cellsx, cellsy, length_z, lax.axis_size("gx"), lax.axis_size("gy"))
+    if plan.fits():
+        return local_planes(plan, density, charge)
+    return local_lines(density, charge)
+
+
 def solution(mesh):
     placed = (P("gx", "gy", None), P("gx", "gy", None))
     return jax.shard_map(

time: 140 us -> 70 us (0.50)
  blocking collectives: 38.3 us -> 8.82 us
  starting transfers between devices: 31.1 us -> 16.6 us
  other arithmetic: 13.1 us -> 1.32 us
  local copies, waits for them, and re-layouts: 14.9 us -> 3.82 us
  matrix products: 10.3 us -> 0 us
  Pallas kernels: 0 us -> 9.82 us
  between operations: 2.37 us -> 0.76 us
    psum x1 -> x0, blocking collectives: 38.3 us -> none  [residual_inner(): return lax.psum(jnp.sum(residual * precond), ('gx', 'gy'))]
    dot_general x6 -> x0, matrix products: 10.3 us -> none  [the longest x1 4.26 us: precondition(): forward = jnp.dot(field, hart_z, precision=HIGHEST)]
    pallas_call x0 -> x4, Pallas kernels: none -> 9.82 us  [call(): pl.pallas_call(kernel, out_shape=tuple(outs), in_specs=[vmem] * len(args)...]
    all_to_all x0 -> x1, blocking collectives: none -> 8.82 us  [local_planes(): sums = lax.all_to_all(sums, axes, 0, 0)]
    all_to_all x4 -> x2, starting transfers between devices: 17.9 us -> 10.1 us  [the longest x1 7.3 us: local_planes(): lines = lax.all_to_all(lines, axes, 0, 0)]
    ppermute x8 -> x4, starting transfers between devices: 13.2 us -> 6.57 us  [the longest x1 3.09 us: local_planes(): ey_high = lax.ppermute(eps[:2], 'gy', [(b, a) for a, b in fwd_y])]
    all_to_all x4 -> x0, other arithmetic: 5.71 us -> none  [the longest x1 1.49 us: precondition(): lax.all_to_all(back_x, 'gx', split_axis=0, concat_axis=2, tiled=True)]
    all_to_all x4 -> x2, waiting for transfers between devices: 22.2 us -> 16.5 us  [the longest x1 12.8 us: local_planes(): lines = lax.all_to_all(lines, axes, 0, 0)]
  transfers between devices with their start and end apart: 12 -> 6, of which waited for: 6 -> 5; matrix products, arithmetic and copies ran while one was open for 6% -> 3% of each run, Pallas kernels for 0% -> 0%
where the time goes in v1:
time: 70 us; the launch traced here: 69.6 us
  waiting for transfers between devices  28.4 us (41%)
  starting transfers between devices  16.6 us (24%)
  Pallas kernels  9.82 us (14%)
  blocking collectives  8.82 us (13%)
  local copies, waits for them, and re-layouts  3.82 us (5%)
  other arithmetic  1.32 us (2%)
  between operations  0.76 us (1%)
    all_to_all x1, waiting for transfers between devices, local_planes(): lines = lax.all_to_all(lines, axes, 0, 0)  12.8 us
    pallas_call x4, Pallas kernels, call(): pl.pallas_call(kernel, out_shape=tuple(outs), in_specs=[vmem] * len(args)...  9.82 us
    ppermute x1, waiting for transfers between devices, local_planes(): ey_low = lax.ppermute(eps[p.cy - 2:], 'gy', fwd_y)  9.5 us
    all_to_all x1, blocking collectives, local_planes(): sums = lax.all_to_all(sums, axes, 0, 0)  8.82 us
    all_to_all x1, starting transfers between devices, local_planes(): lines = lax.all_to_all(lines, axes, 0, 0)  7.3 us
    all_to_all x1, waiting for transfers between devices, local_planes(): blocks = lax.all_to_all(blocks, axes, 0, 0)  3.69 us
    ppermute x1, starting transfers between devices, local_planes(): ey_high = lax.ppermute(eps[:2], 'gy', [(b, a) for a, b in fwd_y])  3.09 us
    unnamed x22, local copies, waits for them, and re-layouts  3.01 us
  transfers between devices with their start and end apart: 6, of which 5 were waited for; matrix products, arithmetic and copies ran while one was open for 3% of the time, Pallas kernels for 0%

profile of v1, /device:TPU:0, one launch (start us, length us, event | category | flops | bytes accessed | tf_op | source)
XLA Modules:
  0.0 69.6 jit_solution(7621980871499948413)
XLA Ops:
  0.6 0.0 copy-start
  0.6 1.0 %copy-done = f32[20,10,384]{2,0,1:T(8,128)S(1)} copy-done((f32[20,10,384]{2,0,1:T(8,128)S(1)}, f32[20,10,384]{2,0,1:T(8,128)}, u32[]{:S(2)}) %copy-start) | copy-done | bytes 307224
  1.6 0.0 copy-start.4
  1.6 1.0 %copy-done.4 = bf16[384,512]{1,0:T(8,128)(2,1)S(1)} copy-done((bf16[384,512]{1,0:T(8,128)(2,1)S(1)}, bf16[384,512]{1,0:T(8,128)(2,1)}, u32[]{:S(2)}) %copy-start.4) | copy-done | bytes 393240
  2.6 0.0 copy-start.5
  2.6 1.0 %copy-done.5 = bf16[384,512]{1,0:T(8,128)(2,1)S(1)} copy-done((bf16[384,512]{1,0:T(8,128)(2,1)S(1)}, bf16[384,512]{1,0:T(8,128)(2,1)}, u32[]{:S(2)}) %copy-start.5) | copy-done | bytes 393240
  3.6 2.2 %shard_map.122 = f32[32,24,128]{2,1,0:T(8,128)} custom-call(f32[10,20,384]{2,1,0:T(8,128)S(1)} %bitcast.18, bf16[384,512]{1,0:T(8,128)(2,1)S(1)} %copy-done.4, bf16[384,512]{1,0:T(8,128)(2,1)S(1)} %copy-done.5), custom_call_target="tpu_custom_call" | custom-call | bytes 1486848 | tf_op jit(solution)/shard_map/pallas_call | solution.py:270
  5.8 0.0 copy-start.6
  5.8 0.0 copy-start.7
  5.8 0.0 copy-start.8
  5.8 0.0 copy-start.9
  5.9 7.3 %all-to-all-start = ((f32[32,24,128]{2,1,0:T(8,128)}), f32[32,24,128]{2,1,0:T(8,128)S(1)}, u32[]{:S(2)}, u32[]{:S(2)}) async-start(f32[32,24,128]{2,1,0:T(8,128)} %shard_map.122), calls=%async_computation | async-start | bytes 786432 | tf_op jit(solution)/shard_map/all_to_all | solution.py:491
  13.2 0.7 %dynamic-slice_bitcast_fusion = f32[12]{0:T(128)S(1)} fusion(f32[32,12]{1,0:T(8,128)} %constant.49.clone, s32[]{:T(128)S(6)} %select_n.3), kind=kLoop, calls=%fused_computation.6 | loop fusion | bytes 100 | tf_op jit(solution)/shard_map/broadcast_in_dim | solution.py:502
  13.9 12.8 %all-to-all-done.refs_0_ = f32[32,24,128]{2,1,0:T(8,128)S(1)} async-done(((f32[32,24,128]{2,1,0:T(8,128)}), f32[32,24,128]{2,1,0:T(8,128)S(1)}, u32[]{:S(2)}, u32[]{:S(2)}) %all-to-all-start) | async-done | bytes 393248 | tf_op jit(solution)/shard_map/all_to_all | solution.py:491
  26.7 0.1 broadcast_in_dim.8.refs_5_
  26.8 0.0 copy-done.6
  26.8 0.0 copy-done.7
  26.8 0.0 copy-done.8
  26.8 0.0 copy-done.9
  26.8 2.5 %shard_map.123 = f32[32,48,128]{2,1,0:T(8,128)} custom-call(f32[32,24,128]{2,1,0:T(8,128)S(1)} %all-to-all-done.refs_0_, bf16[128,288]{1,0:T(8,128)(2,1)S(1)} %copy-done.7, bf16[80,240]{1,0:T(8,128)(2,1)S(1)} %copy-done.8, bf16[224,384]{1,0:T(8,128)(2,1)S(1)} %copy-done.6, f32[80,128]{1,0:T(8,128)S(1)} %copy-done.9, f32[12,1,128]{2,1,0:T(1,128)S(1)} %broadcast_in_dim.8.refs_5_), custom_call_target="tpu_custom_call" | custom-call | bytes 1510912 | tf_op jit(solution)/shard_map/pallas_call | solution.py:270
  29.3 0.0 copy-start.10
  29.3 2.8 %all-to-all-start.1 = ((f32[32,48,128]{2,1,0:T(8,128)}), f32[32,48,128]{2,1,0:T(8,128)S(1)}, u32[]{:S(2)}, u32[]{:S(2)}) async-start(f32[32,48,128]{2,1,0:T(8,128)} %shard_map.123), calls=%async_computation.1 | async-start | bytes 1572864 | tf_op jit(solution)/shard_map/all_to_all | solution.py:520
  32.1 0.0 copy-done.10
  32.1 0.0 copy-start.2
  32.1 0.0 copy-start.3
  32.1 1.3 %fusion.3.refs_4_ = f32[10,20,384]{2,1,0:T(8,128)S(1)} fusion(f32[20,10,384]{2,0,1:T(8,128)S(1)} %copy-done.10), kind=kLoop, calls=%fused_computation.5 | loop fusion | flops 537600 | bytes 614400 | tf_op jit(solution)/shard_map/exp | solution.py:43
  33.4 0.0 copy-start.1
  33.5 1.7 %collective-permute-start.2 = (f32[2,20,384]{2,1,0:T(8,128)S(1)}, f32[2,20,384]{2,1,0:T(8,128)S(1)}, u32[]{:S(2)}, u32[]{:S(2)}) collective-permute-start(f32[2,20,384]{2,1,0:T(8,128)S(1)} %get-tuple-element.13), channel_id=1, source_target_pairs={{0,1},{1,2},{2,3},{3,4},{4,5},{5,6},{6,7},{7,0},{8,9},{9,10},{10,1... | collective-permute-start | bytes 184328 | tf_op jit(solution)/shard_map/ppermute | solution.py:497
  35.2 3.1 %collective-permute-start.3 = (f32[2,20,384]{2,1,0:T(8,128)S(1)}, f32[2,20,384]{2,1,0:T(8,128)S(1)}, u32[]{:S(2)}, u32[]{:S(2)}) collective-permute-start(f32[2,20,384]{2,1,0:T(8,128)S(1)} %get-tuple-element.12), channel_id=1, source_target_pairs={{1,0},{2,1},{3,2},{4,3},{5,4},{6,5},{7,6},{0,7},{9,8},{10,9},{11,1... | collective-permute-start | bytes 184328 | tf_op jit(solution)/shard_map/ppermute | solution.py:498
  38.3 0.1 collective-permute-start
  38.3 1.7 %collective-permute-start.1 = (f32[10,2,384]{2,1,0:T(2,128)S(1)}, f32[10,2,384]{2,1,0:T(2,128)S(1)}, u32[]{:S(2)}, u32[]{:S(2)}) collective-permute-start(f32[10,2,384]{2,1,0:T(2,128)S(1)} %get-tuple-element.14), channel_id=1, source_target_pairs={{8,0},{16,8},{24,16},{0,24},{9,1},{17,9},{25,17},{1,25},{10,2},{18... | collective-permute-start | bytes 92168 | tf_op jit(solution)/shard_map/ppermute | solution.py:496
  40.1 1.6 %collective-permute-done.refs_5_ = f32[10,2,384]{2,1,0:T(2,128)S(1)} collective-permute-done((f32[10,2,384]{2,1,0:T(2,128)S(1)}, f32[10,2,384]{2,1,0:T(2,128)S(1)}, u32[]{:S(2)}, u32[]{:S(2)}) %collective-permute-start) | collective-permute-done | bytes 30752 | tf_op jit(solution)/shard_map/ppermute | solution.py:495
  41.7 0.8 %collective-permute-done.1.refs_6_ = f32[10,2,384]{2,1,0:T(2,128)S(1)} collective-permute-done((f32[10,2,384]{2,1,0:T(2,128)S(1)}, f32[10,2,384]{2,1,0:T(2,128)S(1)}, u32[]{:S(2)}, u32[]{:S(2)}) %collective-permute-start.1) | collective-permute-done | bytes 30752 | tf_op jit(solution)/shard_map/ppermute | solution.py:496
  42.4 9.5 %collective-permute-done.2.refs_7_ = f32[2,20,384]{2,1,0:T(8,128)S(1)} collective-permute-done((f32[2,20,384]{2,1,0:T(8,128)S(1)}, f32[2,20,384]{2,1,0:T(8,128)S(1)}, u32[]{:S(2)}, u32[]{:S(2)}) %collective-permute-start.2) | collective-permute-done | bytes 61472 | tf_op jit(solution)/shard_map/ppermute | solution.py:497
  51.9 0.0 collective-permute-done.3.refs_8_
  51.9 3.7 %all-to-all-done.1.refs_0_ = f32[32,48,128]{2,1,0:T(8,128)S(1)} async-done(((f32[32,48,128]{2,1,0:T(8,128)}), f32[32,48,128]{2,1,0:T(8,128)S(1)}, u32[]{:S(2)}, u32[]{:S(2)}) %all-to-all-start.1) | async-done | bytes 786464 | tf_op jit(solution)/shard_map/all_to_all | solution.py:520
  55.6 0.0 copy-done.2
  55.6 0.0 copy-done.3
  55.6 0.0 copy-done.1
  55.6 4.0 %shard_map.124 = (f32[10,20,384]{2,1,0:T(8,128)S(1)}, f32[10,20,384]{2,1,0:T(8,128)S(1)}, f32[32,1,128]{2,1,0:T(1,128)S(1)}) custom-call(f32[32,48,128]{2,1,0:T(8,128)S(1)} %all-to-all-done.1.refs_0_, bf16[512,384]{1,0:T(8,128)(2,1)S(1)} %copy-done.2, bf16[512,384]{1,0:T(8,128)(2,1)S(1)} %copy-done.3, f32[10,20,384]{2,1,0:T(8,128)S(1)} %bitcast.19, ...), custom_call_target="tpu_custom_call" | custom-call | bytes 3002368 | tf_op jit(solution)/shard_map/pallas_call | solution.py:270
  59.7 8.8 %all_to_all.15.refs_0_ = f32[32,1,128]{2,1,0:T(1,128)S(1)} all-to-all(f32[32,1,128]{2,1,0:T(1,128)S(1)} %get-tuple-element.7), channel_id=1, replica_groups=mesh['gx'=4,'gy'=8] {'gx','gy'}, dimensions={0} | all-to-all | bytes 32768 | tf_op jit(solution)/shard_map/all_to_all | solution.py:538
  68.5 1.0 %shard_map.125 = (f32[10,20,384]{2,1,0:T(8,128)}, f32[10,20,384]{2,1,0:T(8,128)}) custom-call(f32[32,1,128]{2,1,0:T(1,128)S(1)} %all_to_all.15.refs_0_, f32[10,20,384]{2,1,0:T(8,128)S(1)} %bitcast.20, f32[10,20,384]{2,1,0:T(8,128)S(1)} %get-tuple-element.8.refs_2_, f32[10,20,384]{2,1,0:T(8,128)S(1)} %get-tuple-element.9.refs_3_), custom_call_target="tpu_custom_call" | custom-call | bytes 1552384 | tf_op jit(solution)/shard_map/pallas_call | solution.py:270
  (2 shorter events, 0.0 us)
Async XLA Ops:
  0.6 1.0 %copy-start = (f32[20,10,384]{2,0,1:T(8,128)S(1)}, f32[20,10,384]{2,0,1:T(8,128)}, u32[]{:S(2)}) copy-start(f32[20,10,384]{2,0,1:T(8,128)} %param.12) | copy-start | bytes 921604
  1.6 1.0 %copy-start.4 = (bf16[384,512]{1,0:T(8,128)(2,1)S(1)}, bf16[384,512]{1,0:T(8,128)(2,1)}, u32[]{:S(2)}) copy-start(bf16[384,512]{1,0:T(8,128)(2,1)} %constant.47.clone.refs_1_) | copy-start | bytes 1179652
  2.6 1.0 %copy-start.5 = (bf16[384,512]{1,0:T(8,128)(2,1)S(1)}, bf16[384,512]{1,0:T(8,128)(2,1)}, u32[]{:S(2)}) copy-start(bf16[384,512]{1,0:T(8,128)(2,1)} %constant.48.clone.refs_2_) | copy-start | bytes 1179652
  5.8 20.9 %copy-start.6 = (bf16[224,384]{1,0:T(8,128)(2,1)S(1)}, bf16[224,384]{1,0:T(8,128)(2,1)}, u32[]{:S(2)}) copy-start(bf16[224,384]{1,0:T(8,128)(2,1)} %constant.52.clone.refs_3_) | copy-start | bytes 516100
  5.8 20.9 %copy-start.7 = (bf16[128,288]{1,0:T(8,128)(2,1)S(1)}, bf16[128,288]{1,0:T(8,128)(2,1)}, u32[]{:S(2)}) copy-start(bf16[128,288]{1,0:T(8,128)(2,1)} %constant.50.clone.refs_1_) | copy-start | bytes 221188
  5.8 20.9 %copy-start.8 = (bf16[80,240]{1,0:T(8,128)(2,1)S(1)}, bf16[80,240]{1,0:T(8,128)(2,1)}, u32[]{:S(2)}) copy-start(bf16[80,240]{1,0:T(8,128)(2,1)} %constant.51.clone.refs_2_) | copy-start | bytes 115204
  5.8 21.0 %copy-start.9 = (f32[80,128]{1,0:T(8,128)S(1)}, f32[80,128]{1,0:T(8,128)}, u32[]{:S(2)}) copy-start(f32[80,128]{1,0:T(8,128)} %constant.53.clone.refs_4_) | copy-start | bytes 122884
  5.9 20.9 %all-to-all-start = ((f32[32,24,128]{2,1,0:T(8,128)}), f32[32,24,128]{2,1,0:T(8,128)S(1)}, u32[]{:S(2)}, u32[]{:S(2)}) async-start(f32[32,24,128]{2,1,0:T(8,128)} %shard_map.122), calls=%async_computation | async-start | bytes 786432 | tf_op jit(solution)/shard_map/all_to_all | solution.py:491
  29.3 2.8 %copy-start.10 = (f32[20,10,384]{2,0,1:T(8,128)S(1)}, f32[20,10,384]{2,0,1:T(8,128)}, u32[]{:S(2)}) copy-start(f32[20,10,384]{2,0,1:T(8,128)} %param.11) | copy-start | bytes 921604
  29.3 26.3 %all-to-all-start.1 = ((f32[32,48,128]{2,1,0:T(8,128)}), f32[32,48,128]{2,1,0:T(8,128)S(1)}, u32[]{:S(2)}, u32[]{:S(2)}) async-start(f32[32,48,128]{2,1,0:T(8,128)} %shard_map.123), calls=%async_computation.1 | async-start | bytes 1572864 | tf_op jit(solution)/shard_map/all_to_all | solution.py:520
  32.1 23.5 %copy-start.2 = (bf16[512,384]{1,0:T(8,128)(2,1)S(1)}, bf16[512,384]{1,0:T(8,128)(2,1)}, u32[]{:S(2)}) copy-start(bf16[512,384]{1,0:T(8,128)(2,1)} %constant.54.clone.refs_1_) | copy-start | bytes 1179652
  32.1 23.5 %copy-start.3 = (bf16[512,384]{1,0:T(8,128)(2,1)S(1)}, bf16[512,384]{1,0:T(8,128)(2,1)}, u32[]{:S(2)}) copy-start(bf16[512,384]{1,0:T(8,128)(2,1)} %constant.55.clone.refs_2_) | copy-start | bytes 1179652
  33.4 22.2 %copy-start.1 = (f32[20,10,384]{2,0,1:T(8,128)S(1)}, f32[20,10,384]{2,0,1:T(8,128)}, u32[]{:S(2)}) copy-start(f32[20,10,384]{2,0,1:T(8,128)} %param.12) | copy-start | bytes 921604
  33.5 18.5 %collective-permute-start.2 = (f32[2,20,384]{2,1,0:T(8,128)S(1)}, f32[2,20,384]{2,1,0:T(8,128)S(1)}, u32[]{:S(2)}, u32[]{:S(2)}) collective-permute-start(f32[2,20,384]{2,1,0:T(8,128)S(1)} %get-tuple-element.13), channel_id=1, source_target_pairs={{0,1},{1,2},{2,3},{3,4},{4,5},{5,6},{6,7},{7,0},{8,9},{9,10},{10,1... | collective-permute-start | bytes 184328 | tf_op jit(solution)/shard_map/ppermute | solution.py:497
  35.2 16.8 %collective-permute-start.3 = (f32[2,20,384]{2,1,0:T(8,128)S(1)}, f32[2,20,384]{2,1,0:T(8,128)S(1)}, u32[]{:S(2)}, u32[]{:S(2)}) collective-permute-start(f32[2,20,384]{2,1,0:T(8,128)S(1)} %get-tuple-element.12), channel_id=1, source_target_pairs={{1,0},{2,1},{3,2},{4,3},{5,4},{6,5},{7,6},{0,7},{9,8},{10,9},{11,1... | collective-permute-start | bytes 184328 | tf_op jit(solution)/shard_map/ppermute | solution.py:498
  38.3 3.4 %collective-permute-start = (f32[10,2,384]{2,1,0:T(2,128)S(1)}, f32[10,2,384]{2,1,0:T(2,128)S(1)}, u32[]{:S(2)}, u32[]{:S(2)}) collective-permute-start(f32[10,2,384]{2,1,0:T(2,128)S(1)} %get-tuple-element.15), channel_id=1, source_target_pairs={{0,8},{8,16},{16,24},{24,0},{1,9},{9,17},{17,25},{25,1},{2,10},{10... | collective-permute-start | bytes 92168 | tf_op jit(solution)/shard_map/ppermute | solution.py:495
  38.3 4.1 %collective-permute-start.1 = (f32[10,2,384]{2,1,0:T(2,128)S(1)}, f32[10,2,384]{2,1,0:T(2,128)S(1)}, u32[]{:S(2)}, u32[]{:S(2)}) collective-permute-start(f32[10,2,384]{2,1,0:T(2,128)S(1)} %get-tuple-element.14), channel_id=1, source_target_pairs={{8,0},{16,8},{24,16},{0,24},{9,1},{17,9},{25,17},{1,25},{10,2},{18... | collective-permute-start | bytes 92168 | tf_op jit(solution)/shard_map/ppermute | solution.py:496

commit v2 on v0

--- a/solution.py
+++ b/solution.py
@@ -2,7 +2,11 @@
 
 import jax
 import jax.numpy as jnp
+import ml_dtypes
+import numpy as np
 from jax import lax
+from jax.experimental import pallas as pl
+from jax.experimental.pallas import tpu as pltpu
 from jax.sharding import PartitionSpec as P
 
 EPS_SOLVENT = 78.3
@@ -12,6 +16,9 @@
 EPS_PRECOND = 20.0
 SHIFT_PRECOND = 0.05
 HIGHEST = lax.Precision.HIGHEST
+LANES = 128
+HALO = 3
+VMEM_LIMIT = 48 << 20
 
 
 def extended(block, sides, width):
@@ -124,7 +131,7 @@
     return lax.psum(jnp.sum(residual * precond), ("gx", "gy"))
 
 
-def local(density, charge):
+def local_lines(density, charge):
     eps = permittivity(density)
     kappa = KAPPA_SCALE * (eps - 1.0) / (EPS_SOLVENT - 1.0)
     cellsx = eps.shape[0]
@@ -146,12 +153,584 @@
     return (solution_field, residual)
 
 
+def cas_table(rows, columns, length):
+    angle = (np.outer(rows, columns) % length).astype(np.float64) * (2.0 * np.pi / length)
+    return np.cos(angle) + np.sin(angle)
+
+
+def symbol_table(length):
+    halfang = np.arange(length, dtype=np.float64) * (np.pi / length)
+    return ((27.0 * np.sin(halfang) - np.sin(3.0 * halfang)) / 12.0) ** 2
+
+
+def halves(table):
+    high = table.astype(ml_dtypes.bfloat16)
+    low = (table - high.astype(np.float64)).astype(ml_dtypes.bfloat16)
+    return high, low
+
+
+def thirds(table):
+    high, low = halves(table)
+    return np.concatenate([high, low, high], axis=1)
+
+
+def split(values):
+    high = values.astype(jnp.bfloat16)
+    low = (values - high.astype(jnp.float32)).astype(jnp.bfloat16)
+    return high, low
+
+
+def stacked(values, axis):
+    high, low = split(values)
+    return jnp.concatenate([high, high, low], axis=axis)
+
+
+def mul(left, right):
+    return jnp.dot(left, right, preferred_element_type=jnp.float32)
+
+
+def mul_t(left, right):
+    return lax.dot_general(
+        left, right, (((1,), (1,)), ((), ())), preferred_element_type=jnp.float32
+    )
+
+
+def padded_rows(values, rows):
+    if values.shape[0] == rows:
+        return values
+    gap = jnp.zeros((rows - values.shape[0],) + values.shape[1:], values.dtype)
+    return jnp.concatenate([values, gap], axis=0)
+
+
+def up(size, step):
+    return -(-size // step) * step
+
+
+STENCIL = tuple(EPS_PRECOND * c / 576.0 for c in (-783.0, 54.0, -1.0))
+
+
+class Plan:
+    def __init__(self, shape, count_x, count_y):
+        size_x, size_y, self.nz = shape
+        self.gx, self.gl = count_x, count_y // 2
+        self.nx, self.ny = size_x, size_y // 2
+        self.cx, self.cy = size_x // count_x, size_y // count_y
+        self.ng = self.gx * self.gl
+        self.even = count_y % 2 == 0 and self.cy % 2 == 0 and self.ng > 0
+        self.kz = self.nz // max(self.ng, 1)
+        self.yq = self.cy // 2
+        self.xp = up(self.cx, 8)
+        self.xe = self.cx + 2 * HALO
+        self.xw = up(self.xe, 8)
+        self.yp = up(self.ny, 16)
+        self.step = self.yq * self.kz
+        self.edge = HALO * self.kz
+        self.group = LANES // max(self.kz, 1)
+        self.chunks = -(-self.ng // self.group)
+        self.deep = self.chunks * LANES
+        self.extra = self.cx // self.yq if self.yq else 0
+        self.rows = up(2 * self.xe + self.cx + self.extra, 8)
+        self.lines = self.cy * self.xw + (2 * HALO - 1) * self.xp + self.yq * 8
+
+    def fits(self):
+        return (
+            self.even
+            and self.nz % (self.ng * 8) == 0
+            and self.nz % LANES == 0
+            and self.yq == 2 * HALO - 1
+            and self.cx == 4 * self.yq
+            and self.step <= LANES
+            and self.step % 8 == 0
+            and self.nx <= LANES
+            and 2 * (LANES - self.nx) >= self.nx
+            and self.nx % 16 == 0
+            and self.ny >= 2 * HALO
+            and self.gx * self.xw <= LANES
+        )
+
+    def z_forward(self):
+        wave = np.arange(self.nz)
+        owner = wave // self.kz
+        place = owner // self.group * LANES + owner % self.group * self.kz + wave % self.kz
+        table = np.zeros((self.nz, self.deep))
+        table[:, place] = cas_table(wave, wave, self.nz)
+        return halves(table)
+
+    def z_backward(self):
+        return tuple(np.ascontiguousarray(part.T) for part in self.z_forward())
+
+    def x_forward(self):
+        table = np.zeros((LANES, self.nx))
+        table[: self.nx] = cas_table(np.arange(self.nx), np.arange(self.nx), self.nx)
+        return thirds(table)
+
+    def y_both(self):
+        table = np.zeros((self.ny, self.yp))
+        table[:, : self.ny] = cas_table(np.arange(self.ny), np.arange(self.ny), self.ny)
+        return thirds(table)
+
+    def ends(self):
+        low = np.arange(HALO)
+        return np.concatenate([low, self.ny - 1 - low])
+
+    def y_ends(self):
+        table = np.zeros((8, self.yp))
+        table[: 2 * HALO, : self.ny] = cas_table(self.ends(), np.arange(self.ny), self.ny)
+        return thirds(table)
+
+    def y_sources(self):
+        columns = cas_table(np.arange(self.ny), self.ends(), self.ny).T
+        wide = np.broadcast_to(columns[:, :, None], (2 * HALO, self.ny, LANES))
+        return np.ascontiguousarray(wide).astype(np.float32)
+
+    def x_backward(self):
+        wide = np.zeros((self.gx * self.xw, LANES))
+        own = np.zeros((self.gx * self.xp, LANES))
+        waves = np.arange(self.nx)
+        for g in range(self.gx):
+            x = (g * self.cx - HALO + np.arange(self.xe)) % self.nx
+            wide[g * self.xw : g * self.xw + self.xe, : self.nx] = cas_table(x, waves, self.nx)
+            x = g * self.cx + np.arange(self.cx)
+            own[g * self.xp : g * self.xp + self.cx, : self.nx] = cas_table(x, waves, self.nx)
+        scale = 4.0 * np.pi / (self.nx * self.nz)
+        return thirds(np.concatenate([wide, own], axis=0) * scale)
+
+    def plane(self):
+        plane = np.full((self.ny, LANES), 1e30)
+        plane[:, : self.nx] = symbol_table(self.nx)[None, :] + symbol_table(self.ny)[:, None]
+        return plane.astype(np.float32)
+
+    def waves(self):
+        return symbol_table(self.nz).reshape(self.ng, self.kz).astype(np.float32)
+
+    def joins(self):
+        lam_x, lam_y, lam_z = symbol_table(self.nx), symbol_table(self.ny), symbol_table(self.nz)
+        total = EPS_PRECOND * (lam_z[:, None, None] + lam_x[None, :, None] + lam_y) + SHIFT_PRECOND
+        green = np.real(np.fft.ifft(1.0 / total, axis=-1))
+        i = np.arange(HALO)
+        near = green[..., np.abs(i[:, None] - i[None, :])]
+        far = green[..., i[:, None] + i[None, :] + 1]
+        band = np.zeros((HALO, HALO))
+        for row in range(HALO):
+            for column in range(HALO - row):
+                band[row, column] = STENCIL[row + column]
+        eye = np.eye(HALO)
+        even = np.linalg.inv(eye - 2.0 * (near + far) @ band)
+        odd = np.linalg.inv(eye + 2.0 * (near - far) @ band)
+        both = np.stack([even, odd], axis=2).reshape(self.nz, self.nx, 2 * HALO * HALO)
+        table = np.zeros((self.ng, 2 * HALO * HALO, self.kz, LANES), np.float32)
+        table[..., : self.nx] = both.reshape(self.ng, self.kz, self.nx, -1).transpose(0, 3, 1, 2)
+        return table
+
+
+VMEM_SPEC = pl.BlockSpec(memory_space=pltpu.VMEM)
+ANY_SPEC = pl.BlockSpec(memory_space=pl.ANY)
+
+
+def call(kernel, outs, args, scratch=(), specs=None):
+    nbytes = sum(int(np.prod(a.shape)) * a.dtype.itemsize for a in (*args, *outs))
+    return pl.pallas_call(
+        kernel,
+        out_shape=tuple(outs),
+        in_specs=specs or [VMEM_SPEC] * len(args),
+        out_specs=tuple([VMEM_SPEC] * len(outs)),
+        scratch_shapes=list(scratch),
+        compiler_params=pltpu.CompilerParams(vmem_limit_bytes=VMEM_LIMIT),
+        cost_estimate=pl.CostEstimate(flops=0, bytes_accessed=nbytes, transcendentals=0),
+    )(*args)
+
+
+def lane_index(rows):
+    return lax.broadcasted_iota(jnp.int32, (rows, LANES), 1)
+
+
+def moved(values, shift):
+    shift = shift % LANES
+    return values if shift == 0 else pltpu.roll(values, shift, 1)
+
+
+def between(lane, slot, width):
+    return (lane >= slot * width) & (lane < (slot + 1) * width)
+
+
+def forward_kernel(p, charge_in, high_in, low_in, out, charge, high_z, low_z, sems):
+    copies = [
+        pltpu.make_async_copy(source, target, sems.at[i])
+        for i, (source, target) in enumerate(
+            ((charge_in, charge), (high_in, high_z), (low_in, low_z))
+        )
+    ]
+    for copy in copies:
+        copy.start()
+    copies[0].wait()
+    rows = [padded_rows(charge[y], p.xp) for y in range(p.cy)]
+    high, low = split(jnp.concatenate(rows, axis=0))
+    copies[1].wait()
+    spec = mul(high, high_z[...]) + mul(low, high_z[...])
+    copies[2].wait()
+    spec = spec + mul(high, low_z[...])
+    lane = lane_index(p.xp)
+    for target in range(p.ng):
+        chunk, slot = divmod(target, p.group)
+        for part in range(2):
+            block = jnp.zeros((p.xp, LANES), jnp.float32)
+            for i in range(p.yq):
+                y = part * p.yq + i
+                piece = spec[y * p.xp : (y + 1) * p.xp, chunk * LANES : (chunk + 1) * LANES]
+                block = jnp.where(between(lane, i, p.kz), moved(piece, (i - slot) * p.kz), block)
+            out[target, part * p.cx : (part + 1) * p.cx] = block[: p.cx]
+
+
+def table_kernel(p, plane, waves, out):
+    for k in range(p.kz):
+        symbol = EPS_PRECOND * (plane[...] + waves[k]) + SHIFT_PRECOND
+        out[:, k * LANES : (k + 1) * LANES] = 1.0 / (float(p.ny) * symbol)
+
+
+def lanes_of(values, k):
+    return values[:, k * LANES : (k + 1) * LANES]
+
+
+def solve_kernel(p, blocks, x_fwd, y_both, y_ends, table, spectrum_out, own, sent, turned, ends):
+    columns = []
+    for gl in range(p.gl):
+        for part in range(2):
+            pieces = [
+                blocks[gx * p.gl + gl, part * p.cx : (part + 1) * p.cx] for gx in range(p.gx)
+            ]
+            columns.append(jnp.concatenate(pieces, axis=0))
+    along_x = mul(x_fwd[...], stacked(jnp.concatenate(columns, axis=1), 0))
+    for b in range(2 * p.gl):
+        turned[pl.ds(b * p.step, LANES), :] = lanes_of(along_x, b).T
+    field = jnp.concatenate(
+        [turned[pl.ds(k, p.ny, stride=p.kz), :] for k in range(p.kz)], axis=1
+    )
+    along_y = mul(y_both[...], stacked(padded_rows(field, p.yp), 0))
+    solved = along_y * table[...]
+    spectrum_out[...] = solved
+    at_ends = mul(y_ends[...], stacked(padded_rows(solved, p.yp), 0))
+    for k in range(p.kz):
+        ends[pl.ds(k, 8, stride=p.kz), :] = lanes_of(at_ends, k)
+    own[...] = ends[pl.ds(0, 2 * HALO * p.kz), :]
+    piece = [ends[pl.ds(j * p.kz, p.kz), :] for j in range(2 * HALO)]
+    lane = lane_index(p.kz)
+    free = LANES - p.nx
+    for i in range(4):
+        spare = moved(piece[4 + i // 2], p.nx if i % 2 == 0 else p.nx - free)
+        sent[pl.ds(i * p.kz, p.kz), :] = jnp.where(lane < p.nx, piece[i], spare)
+
+
+def return_kernel(
+    p, spectrum_in, own, received, table, joins, y_both, y_sources, x_bwd,
+    out, sources, planes,
+):
+    lane = lane_index(p.kz)
+    free = LANES - p.nx
+    part = [received[pl.ds(i * p.kz, p.kz), :] for i in range(4)]
+    other = [jnp.where(lane < p.nx, value, 0.0) for value in part]
+    for i in range(2):
+        first = moved(part[2 * i], -p.nx)
+        second = moved(part[2 * i + 1], free - p.nx)
+        other.append(jnp.where(lane < free, first, jnp.where(lane < p.nx, second, 0.0)))
+    mine = [own[pl.ds(j * p.kz, p.kz), :] for j in range(2 * HALO)]
+    jump = [mine[j] - other[j] for j in range(2 * HALO)]
+    even = [jump[j] + jump[HALO + j] for j in range(HALO)]
+    odd = [jump[j] - jump[HALO + j] for j in range(HALO)]
+
+    def mixed(base, vector):
+        return [
+            sum(joins[base + HALO * i + j] * vector[j] for j in range(HALO)) for i in range(HALO)
+        ]
+
+    even_full, odd_full = mixed(0, even), mixed(HALO * HALO, odd)
+    low_full = [0.5 * (e + o) for e, o in zip(even_full, odd_full)]
+    high_full = [0.5 * (e - o) for e, o in zip(even_full, odd_full)]
+    far_low = [other[j] - 0.5 * (low_full[j] - jump[j]) for j in range(HALO)]
+    far_high = [other[HALO + j] - 0.5 * (high_full[j] - jump[HALO + j]) for j in range(HALO)]
+    for i in range(HALO):
+        sources[pl.ds(i * p.kz, p.kz), :] = sum(
+            STENCIL[i + j] * high_full[j] for j in range(HALO - i)
+        )
+        sources[pl.ds((HALO + i) * p.kz, p.kz), :] = sum(
+            STENCIL[i + j] * low_full[j] for j in range(HALO - i)
+        )
+    whole = []
+    for k in range(p.kz):
+        added = sum(y_sources[j] * sources[pl.ds(j * p.kz + k, 1), :] for j in range(2 * HALO))
+        whole.append(
+            spectrum_in[:, k * LANES : (k + 1) * LANES]
+            + added * table[:, k * LANES : (k + 1) * LANES]
+        )
+    back_y = mul(y_both[...], stacked(padded_rows(jnp.concatenate(whole, axis=1), p.yp), 0))
+    base = p.edge
+    for k in range(p.kz):
+        planes[pl.ds(base + k, p.ny, stride=p.kz), :] = lanes_of(back_y, k)
+    after = base + p.ny * p.kz
+    for i in range(HALO):
+        planes[pl.ds(base - (i + 1) * p.kz, p.kz), :] = far_high[i]
+        planes[pl.ds(after + i * p.kz, p.kz), :] = far_low[i]
+    cut = p.gx * p.xw
+    wide_rows = x_bwd[:cut, :]
+    own_rows = x_bwd[cut:, :]
+    gap = jnp.zeros((LANES - p.step, LANES), jnp.float32)
+    slots = lane_index(p.extra)
+    rest = p.rows - 2 * p.xe - p.cx - p.extra
+    for gl in range(p.gl):
+        start = base + gl * 2 * p.step
+        end = start + 2 * p.step
+        last = planes[pl.ds(end + p.edge - p.kz, p.kz), :]
+        both = jnp.concatenate(
+            [planes[pl.ds(start, LANES), :], planes[pl.ds(start + p.step, LANES), :]], axis=0
+        )
+        wide = mul_t(wide_rows, stacked(both, 1))
+        sides = jnp.concatenate(
+            [
+                planes[pl.ds(start - p.edge, p.edge), :],
+                planes[pl.ds(end, p.edge - p.kz), :],
+                gap,
+                *[last] * p.yq,
+                gap,
+            ],
+            axis=0,
+        )
+        side = mul_t(own_rows, stacked(sides, 1))
+        for gx in range(p.gx):
+            target = gx * p.gl + gl
+            for half in range(2):
+                out[target, half * p.xe : (half + 1) * p.xe] = wide[
+                    gx * p.xw : gx * p.xw + p.xe, half * LANES : (half + 1) * LANES
+                ]
+            at, line = 2 * p.xe, gx * p.xp
+            out[target, at : at + p.cx] = side[line : line + p.cx, :LANES]
+            at += p.cx
+            extra = jnp.zeros((p.extra, LANES), jnp.float32)
+            for q in range(p.yq):
+                value = side[line + q * p.extra : line + (q + 1) * p.extra, LANES:]
+                extra = jnp.where(between(slots, q, p.kz), value, extra)
+            out[target, at : at + p.extra] = extra
+            if rest:
+                out[target, at + p.extra :] = jnp.zeros((rest, LANES), jnp.float32)
+
+
+def stencil_kernel(
+    p, blocks, high_z, low_z, charge, eps, ex_low, ex_high, ey_low, ey_high,
+    pre, image, sums, lines, field, eps_x, eps_y,
+):
+    lane = lane_index(p.xw)
+    windows, at = [], 0
+    for y in range(p.cy):
+        half = y // p.yq
+        windows.append((half * p.xe // 8 * 8, p.xw, y % p.yq, at))
+        at += p.xw
+    side = 2 * p.xe
+    for h in range(2 * HALO - 1):
+        windows.append((side // 8 * 8, p.xp, h, at))
+        at += p.xp
+    tail = side + p.cx
+    for q in range(p.yq):
+        windows.append((tail // 8 * 8, 8, q, at))
+        at += 8
+    for chunk in range(p.chunks):
+        count = min(p.group, p.ng - chunk * p.group)
+        for first, rows, piece, at in windows:
+            here = lane[:rows]
+            line = jnp.zeros((rows, LANES), jnp.float32)
+            for slot in range(count):
+                part = blocks[chunk * p.group + slot, first : first + rows, :]
+                part = moved(part, (slot - piece) * p.kz)
+                line = jnp.where(between(here, slot, p.kz), part, line)
+            lines[at : at + rows, chunk * LANES : (chunk + 1) * LANES] = line
+    high, low = split(lines[...])
+    whole = mul(high, high_z[...]) + mul(low, high_z[...]) + mul(high, low_z[...])
+    for y in range(p.cy):
+        first, rows, piece, at = windows[y]
+        off = (y // p.yq) * p.xe - first
+        field[HALO + y, : p.xe] = whole[at + off : at + off + p.xe]
+    for h in range(2 * HALO - 1):
+        first, rows, piece, at = windows[p.cy + h]
+        off = side - first
+        y = h if h < HALO else h + p.cy
+        field[y, HALO : HALO + p.cx] = whole[at + off : at + off + p.cx]
+    for q in range(p.yq):
+        first, rows, piece, at = windows[p.cy + 2 * HALO - 1 + q]
+        off = tail - first
+        field[p.cy + 2 * HALO - 1, HALO + q * p.extra : HALO + (q + 1) * p.extra] = whole[
+            at + off : at + off + p.extra
+        ]
+    eps_x[:, 0:2, :] = ex_low[...]
+    eps_x[:, 2 : 2 + p.cx, :] = eps[...]
+    eps_x[:, 2 + p.cx : 4 + p.cx, :] = ex_high[...]
+    eps_y[0:2] = ey_low[...]
+    eps_y[2 : 2 + p.cy] = eps[...]
+    eps_y[2 + p.cy : 4 + p.cy] = ey_high[...]
+
+    def stretch(flux_at):
+        return 27.0 * (flux_at(2) - flux_at(1)) - (flux_at(3) - flux_at(0))
+
+    rz = jnp.zeros((p.cx, LANES), jnp.float32)
+    dot = jnp.zeros((p.cx, LANES), jnp.float32)
+    faces_y = {}
+
+    def face_y(y):
+        if y not in faces_y:
+            val = [field[y + i, HALO : HALO + p.cx, :] for i in range(4)]
+            grad = 27.0 * (val[2] - val[1]) - (val[3] - val[0])
+            faces_y[y] = (eps_y[y] + eps_y[y + 1]) * grad
+        return faces_y[y]
+
+    for y in range(p.cy):
+        line = field[HALO + y]
+        val = [line[i : i + p.cx + 3] for i in range(4)]
+        grad = 27.0 * (val[2] - val[1]) - (val[3] - val[0])
+        eps_line = eps_x[y]
+        flux = (eps_line[0 : p.cx + 3] + eps_line[1 : p.cx + 4]) * grad
+        term = stretch(lambda i: flux[i : i + p.cx])
+        term = term + stretch(lambda i: face_y(y + i))
+        here = line[HALO : HALO + p.cx]
+        eps_here = eps[y]
+        n = p.nz
+        grad = 27.0 * (pltpu.roll(here, n - 1, 1) - here) - (
+            pltpu.roll(here, n - 2, 1) - pltpu.roll(here, 1, 1)
+        )
+        flux = (eps_here + pltpu.roll(eps_here, n - 1, 1)) * grad
+        term = term + (
+            27.0 * (flux - pltpu.roll(flux, 1, 1))
+            - (pltpu.roll(flux, n - 1, 1) - pltpu.roll(flux, 2, 1))
+        )
+        result = (KAPPA_SCALE / (EPS_SOLVENT - 1.0)) * (eps_here - 1.0) * here - term * (0.5 / 576.0)
+        pre[y] = here
+        image[y] = result
+        one = charge[y] * here
+        two = result * here
+        for c in range(n // LANES):
+            rz = rz + one[:, c * LANES : (c + 1) * LANES]
+            dot = dot + two[:, c * LANES : (c + 1) * LANES]
+    rz = jnp.sum(rz, axis=0, keepdims=True)
+    dot = jnp.sum(dot, axis=0, keepdims=True)
+    half = LANES // 2
+    rz = rz + pltpu.roll(rz, half, 1)
+    dot = dot + pltpu.roll(dot, half, 1)
+    both = jnp.where(lane_index(1) < half, rz, dot)
+    sums[...] = jnp.broadcast_to(both[None], sums.shape)
+
+
+def update_kernel(p, sums, charge, pre, image, solution_field, residual):
+    half = LANES // 2
+    total = jnp.sum(sums[...], axis=0)
+    lane = lane_index(1)
+    rz = jnp.sum(jnp.where(lane < half, total, 0.0), axis=1, keepdims=True)
+    dot = jnp.sum(jnp.where(lane < half, 0.0, total), axis=1, keepdims=True)
+    alpha = jnp.broadcast_to((4.0 * math.pi) * rz / dot, (p.cx, p.nz))
+    for y in range(p.cy):
+        solution_field[y] = alpha * pre[y]
+        residual[y] = (4.0 * math.pi) * charge[y] - alpha * image[y]
+
+
+def local_planes(p, density, charge):
+    group = ("gx", "gl")
+    along_y = ("gh", "gl")
+    f32, bf16 = jnp.float32, jnp.bfloat16
+
+    def shape(*dims):
+        return jax.ShapeDtypeStruct(dims, f32)
+
+    def ring(count):
+        return [(i, (i + 1) % count) for i in range(count)]
+
+    def back(pairs):
+        return [(target, source) for source, target in pairs]
+
+    density = density.transpose(1, 0, 2)
+    charge = charge.transpose(1, 0, 2)
+    high_z, low_z = p.z_forward()
+    (blocks,) = call(
+        lambda *refs: forward_kernel(p, *refs),
+        [shape(p.ng, 2 * p.cx, LANES)],
+        [charge, jnp.asarray(high_z), jnp.asarray(low_z)],
+        [
+            pltpu.VMEM((p.cy, p.cx, p.nz), f32),
+            pltpu.VMEM((p.nz, p.deep), bf16),
+            pltpu.VMEM((p.nz, p.deep), bf16),
+            pltpu.SemaphoreType.DMA((3,)),
+        ],
+        specs=[ANY_SPEC] * 3,
+    )
+    blocks = lax.all_to_all(blocks, group, 0, 0)
+    eps = permittivity(density)
+    ex_low = lax.ppermute(eps[:, p.cx - 2 :], "gx", ring(p.gx))
+    ex_high = lax.ppermute(eps[:, :2], "gx", back(ring(p.gx)))
+    ey_low = lax.ppermute(eps[p.cy - 2 :], along_y, ring(2 * p.gl))
+    ey_high = lax.ppermute(eps[:2], along_y, back(ring(2 * p.gl)))
+    me = lax.axis_index("gx") * p.gl + lax.axis_index("gl")
+    waves = lax.dynamic_slice_in_dim(jnp.asarray(p.waves()), me, 1, axis=0)
+    waves = jnp.broadcast_to(waves.reshape(p.kz, 1, 1), (p.kz, 1, LANES))
+    joins = lax.dynamic_index_in_dim(jnp.asarray(p.joins()), me, 0, keepdims=False)
+    (table,) = call(
+        lambda *refs: table_kernel(p, *refs),
+        [shape(p.ny, p.kz * LANES)],
+        [jnp.asarray(p.plane()), waves],
+    )
+    y_both = jnp.asarray(p.y_both())
+    spectrum_half, own, sent = call(
+        lambda *refs: solve_kernel(p, *refs),
+        [shape(p.ny, p.kz * LANES), shape(2 * HALO * p.kz, LANES), shape(4 * p.kz, LANES)],
+        [blocks, jnp.asarray(p.x_forward()), y_both, jnp.asarray(p.y_ends()), table],
+        [pltpu.VMEM((p.ny * p.kz + LANES, LANES), f32), pltpu.VMEM((8 * p.kz, LANES), f32)],
+    )
+    received = lax.ppermute(sent, "gh", [(0, 1), (1, 0)])
+    (blocks,) = call(
+        lambda *refs: return_kernel(p, *refs),
+        [shape(p.ng, p.rows, LANES)],
+        [
+            spectrum_half, own, received, table, joins, y_both,
+            jnp.asarray(p.y_sources()), jnp.asarray(p.x_backward()),
+        ],
+        [
+            pltpu.VMEM((2 * HALO * p.kz, LANES), f32),
+            pltpu.VMEM((p.ny * p.kz + 2 * p.edge, LANES), f32),
+        ],
+    )
+    blocks = lax.all_to_all(blocks, group, 0, 0)
+    back_high, back_low = p.z_backward()
+    pre, image, sums = call(
+        lambda *refs: stencil_kernel(p, *refs),
+        [shape(p.cy, p.cx, p.nz), shape(p.cy, p.cx, p.nz), shape(2 * p.ng, 1, LANES)],
+        [
+            blocks, jnp.asarray(back_high), jnp.asarray(back_low), charge,
+            eps, ex_low, ex_high, ey_low, ey_high,
+        ],
+        [
+            pltpu.VMEM((p.lines, p.deep), f32),
+            pltpu.VMEM((p.cy + 2 * HALO, p.xw, p.nz), f32),
+            pltpu.VMEM((p.cy, p.cx + 4, p.nz), f32),
+            pltpu.VMEM((p.cy + 4, p.cx, p.nz), f32),
+        ],
+    )
+    sums = lax.all_to_all(sums, ("gx", "gh", "gl"), 0, 0)
+    solution_field, residual = call(
+        lambda *refs: update_kernel(p, *refs),
+        [shape(p.cy, p.cx, p.nz), shape(p.cy, p.cx, p.nz)],
+        [sums, charge, pre, image],
+    )
+    return solution_field.transpose(1, 0, 2), residual.transpose(1, 0, 2)
+
+
 def solution(mesh):
-    placed = (P("gx", "gy", None), P("gx", "gy", None))
-    return jax.shard_map(
-        local,
-        mesh=mesh,
-        in_specs=placed,
-        out_specs=(P("gx", "gy", None), P("gx", "gy", None)),
-        check_vma=False,
-    )
+    count_x, count_y = mesh.shape["gx"], mesh.shape["gy"]
+
+    def run(density, charge):
+        plan = Plan(charge.shape, count_x, count_y)
+        if plan.fits():
+            split_mesh = jax.sharding.Mesh(
+                mesh.devices.reshape(count_x, 2, count_y // 2), ("gx", "gh", "gl")
+            )
+            spec = P("gx", ("gh", "gl"), None)
+            body, over = (lambda *args: local_planes(plan, *args)), split_mesh
+        else:
+            spec = P("gx", "gy", None)
+            body, over = local_lines, mesh
+        return jax.shard_map(
+            body, mesh=over, in_specs=(spec, spec), out_specs=(spec, spec), check_vma=False
+        )(density, charge)
+
+    return run

time: 140 us -> 63.6 us (0.45)
  blocking collectives: 38.3 us -> 10 us
  waiting for transfers between devices: 28.9 us -> 14.5 us
  starting transfers between devices: 31.1 us -> 19.2 us
  other arithmetic: 13.1 us -> 1.32 us
  matrix products: 10.3 us -> 0 us
  Pallas kernels: 0 us -> 9.27 us
  local copies, waits for them, and re-layouts: 14.9 us -> 7.75 us
  between operations: 2.37 us -> 0.79 us
    psum x1 -> x0, blocking collectives: 38.3 us -> none  [residual_inner(): return lax.psum(jnp.sum(residual * precond), ('gx', 'gy'))]
    all_to_all x4 -> x2, waiting for transfers between devices: 22.2 us -> 5.98 us  [local_planes(): blocks = lax.all_to_all(blocks, group, 0, 0)]
    dot_general x6 -> x0, matrix products: 10.3 us -> none  [the longest x1 4.26 us: precondition(): forward = jnp.dot(field, hart_z, precision=HIGHEST)]
    all_to_all x0 -> x1, blocking collectives: none -> 10 us  [local_planes(): sums = lax.all_to_all(sums, ('gx', 'gh', 'gl'), 0, 0)]
    pallas_call x0 -> x6, Pallas kernels: none -> 9.27 us  [call(): pl.pallas_call(kernel, out_shape=tuple(outs), in_specs=specs or [VMEM_SPE...]
    all_to_all x4 -> x2, starting transfers between devices: 17.9 us -> 10 us  [local_planes(): blocks = lax.all_to_all(blocks, group, 0, 0)]
    all_to_all x4 -> x0, other arithmetic: 5.71 us -> none  [the longest x1 1.49 us: precondition(): lax.all_to_all(back_x, 'gx', split_axis=0, concat_axis=2, tiled=True)]
    all_to_all x9 -> x0, local copies, waits for them, and re-layouts: 4.23 us -> none  [the longest x3 3.52 us: precondition(): lax.all_to_all(forward, 'gx', split_axis=2, concat_axis=0, tiled=True)]
  transfers between devices with their start and end apart: 12 -> 7, of which waited for: 6 -> 4; matrix products, arithmetic and copies ran while one was open for 6% -> 5% of each run, Pallas kernels for 0% -> 0%
where the time goes in v2:
time: 63.6 us; the launch traced here: 62.9 us
  starting transfers between devices  19.2 us (30%)
  waiting for transfers between devices  14.5 us (23%)
  blocking collectives  10 us (16%)
  Pallas kernels  9.27 us (15%)
  local copies, waits for them, and re-layouts  7.75 us (12%)
  other arithmetic  1.32 us (2%)
  between operations  0.79 us (1%)
    all_to_all x1, blocking collectives, local_planes(): sums = lax.all_to_all(sums, ('gx', 'gh', 'gl'), 0, 0)  10 us
    all_to_all x2, starting transfers between devices, local_planes(): blocks = lax.all_to_all(blocks, group, 0, 0)  10 us
    pallas_call x6, Pallas kernels, call(): pl.pallas_call(kernel, out_shape=tuple(outs), in_specs=specs or [VMEM_SPE...  9.27 us
    unnamed x26, local copies, waits for them, and re-layouts  5.98 us
    all_to_all x2, waiting for transfers between devices, local_planes(): blocks = lax.all_to_all(blocks, group, 0, 0)  5.98 us
    ppermute x1, waiting for transfers between devices, local_planes(): ey_low = lax.ppermute(eps[p.cy - 2:], along_y, ring(2 * p.gl))  3.46 us
    ppermute x1, starting transfers between devices, local_planes(): ey_high = lax.ppermute(eps[:2], along_y, back(ring(2 * p.gl)))  2.92 us
    ppermute x1, waiting for transfers between devices, local_planes(): ex_low = lax.ppermute(eps[:, p.cx - 2:], 'gx', ring(p.gx))  2.77 us
  transfers between devices with their start and end apart: 7, of which 4 were waited for; matrix products, arithmetic and copies ran while one was open for 5% of the time, Pallas kernels for 0%

profile of v2, /device:TPU:0, one launch (start us, length us, event | category | flops | bytes accessed | tf_op | source)
XLA Modules:
  0.0 62.9 jit_solution(9370106549335044844)
XLA Ops:
  0.6 0.0 copy-start
  0.6 1.0 %copy-done = f32[20,10,384]{2,0,1:T(8,128)S(1)} copy-done((f32[20,10,384]{2,0,1:T(8,128)S(1)}, f32[20,10,384]{2,0,1:T(8,128)}, u32[]{:S(2)}) %copy-start) | copy-done | bytes 307224
  1.6 0.0 copy-start.4
  1.6 1.0 %copy-done.4 = bf16[384,512]{1,0:T(8,128)(2,1)S(1)} copy-done((bf16[384,512]{1,0:T(8,128)(2,1)S(1)}, bf16[384,512]{1,0:T(8,128)(2,1)}, u32[]{:S(2)}) %copy-start.4) | copy-done | bytes 393240
  2.6 0.0 copy-start.5
  2.6 1.0 %copy-done.5 = bf16[384,512]{1,0:T(8,128)(2,1)S(1)} copy-done((bf16[384,512]{1,0:T(8,128)(2,1)S(1)}, bf16[384,512]{1,0:T(8,128)(2,1)}, u32[]{:S(2)}) %copy-start.5) | copy-done | bytes 393240
  3.6 0.0 copy-start.6
  3.6 0.0 copy-start.7
  3.6 0.0 copy-start.12
  3.6 2.3 %shard_map.149 = f32[16,40,128]{2,1,0:T(8,128)} custom-call(f32[10,20,384]{2,1,0:T(8,128)S(1)} %bitcast.20, bf16[384,512]{1,0:T(8,128)(2,1)S(1)} %copy-done.4, bf16[384,512]{1,0:T(8,128)(2,1)S(1)} %copy-done.5), custom_call_target="tpu_custom_call" | custom-call | bytes 1421312 | tf_op jit(solution)/shard_map/pallas_call | solution.py:332
  6.0 0.0 copy-start.1
  6.0 0.0 copy-start.2
  6.0 0.0 copy-start.3
  6.0 6.4 %all-to-all-start = ((f32[16,40,128]{2,1,0:T(8,128)}), f32[16,40,128]{2,1,0:T(8,128)S(1)}, u32[]{:S(2)}, u32[]{:S(2)}) async-start(f32[16,40,128]{2,1,0:T(8,128)} %shard_map.149), calls=%async_computation | async-start | bytes 655360 | tf_op jit(solution)/shard_map/all_to_all | solution.py:658
  12.4 0.7 %dynamic-slice_bitcast_fusion.1 = f32[24]{0:T(128)S(1)} fusion(f32[16,24]{1,0:T(8,128)} %constant.58.clone, s32[]{:T(128)S(6)} %select_n.5), kind=kLoop, calls=%fused_computation.7 | loop fusion | bytes 196 | tf_op jit(solution)/shard_map/broadcast_in_dim | solution.py:666
  13.1 0.1 broadcast_in_dim.8.refs_1_
  13.2 0.0 copy-start.10
  13.2 0.7 %copy-done.10 = f32[40,128]{1,0:T(8,128)S(1)} copy-done((f32[40,128]{1,0:T(8,128)S(1)}, f32[40,128]{1,0:T(8,128)}, u32[]{:S(2)}) %copy-start.10) | copy-done | bytes 20504
  14.0 0.1 shard_map.150.refs_4_.refs_3_
  14.1 6.0 %all-to-all-done.refs_0_ = f32[16,40,128]{2,1,0:T(8,128)S(1)} async-done(((f32[16,40,128]{2,1,0:T(8,128)}), f32[16,40,128]{2,1,0:T(8,128)S(1)}, u32[]{:S(2)}, u32[]{:S(2)}) %all-to-all-start) | async-done | bytes 327712 | tf_op jit(solution)/shard_map/all_to_all | solution.py:658
  20.0 0.0 copy-start.8
  20.0 0.7 %copy-done.8 = bf16[40,144]{1,0:T(8,128)(2,1)S(1)} copy-done((bf16[40,144]{1,0:T(8,128)(2,1)S(1)}, bf16[40,144]{1,0:T(8,128)(2,1)}, u32[]{:S(2)}) %copy-start.8) | copy-done | bytes 11544
  20.8 0.0 copy-start.9
  20.8 0.8 %copy-done.9 = bf16[128,240]{1,0:T(8,128)(2,1)S(1)} copy-done((bf16[128,240]{1,0:T(8,128)(2,1)S(1)}, bf16[128,240]{1,0:T(8,128)(2,1)}, u32[]{:S(2)}) %copy-start.9) | copy-done | bytes 61464
  21.6 0.0 copy-start.11
  21.6 0.7 %copy-done.11 = bf16[8,144]{1,0:T(8,128)(2,1)S(1)} copy-done((bf16[8,144]{1,0:T(8,128)(2,1)S(1)}, bf16[8,144]{1,0:T(8,128)(2,1)}, u32[]{:S(2)}) %copy-start.11) | copy-done | bytes 2328
  22.3 0.8 %shard_map.151 = (f32[40,3072]{1,0:T(8,128)S(1)}, f32[144,128]{1,0:T(8,128)S(1)}, f32[96,128]{1,0:T(8,128)S(1)}) custom-call(f32[16,40,128]{2,1,0:T(8,128)S(1)} %all-to-all-done.refs_0_, bf16[128,240]{1,0:T(8,128)(2,1)S(1)} %copy-done.9, bf16[40,144]{1,0:T(8,128)(2,1)S(1)} %copy-done.8, bf16[8,144]{1,0:T(8,128)(2,1)S(1)} %copy-done.11, ...), custom_call_target="tpu_custom_call" | custom-call | bytes 1508864 | tf_op jit(solution)/shard_map/pallas_call | solution.py:332
  23.1 2.6 %collective-permute-start = (f32[96,128]{1,0:T(8,128)S(1)}, f32[96,128]{1,0:T(8,128)S(1)}, u32[]{:S(2)}, u32[]{:S(2)}) collective-permute-start(f32[96,128]{1,0:T(8,128)S(1)} %get-tuple-element.12), channel_id=1, source_target_pairs={{0,4},{4,0},{1,5},{5,1},{2,6},{6,2},{3,7},{7,3},{8,12},{12,8},{9,1... | collective-permute-start | bytes 147464 | tf_op jit(solution)/shard_map/ppermute | solution.py:680
  25.7 0.9 %dynamic-slice_bitcast_fusion.refs_4_ = f32[18,24,128]{2,1,0:T(8,128)S(1)} fusion(f32[16,18,24,128]{3,2,1,0:T(8,128)} %constant.59.clone, s32[]{:T(128)S(6)} %select_n.5), kind=kLoop, calls=%fused_computation.6 | loop fusion | bytes 442372 | tf_op jit(solution)/shard_map/jit(dynamic_index_in_dim)/squeeze | solution.py:667
  26.7 2.3 %collective-permute-done.refs_2_ = f32[96,128]{1,0:T(8,128)S(1)} collective-permute-done((f32[96,128]{1,0:T(8,128)S(1)}, f32[96,128]{1,0:T(8,128)S(1)}, u32[]{:S(2)}, u32[]{:S(2)}) %collective-permute-start) | collective-permute-done | bytes 49184 | tf_op jit(solution)/shard_map/ppermute | solution.py:680
  29.0 0.0 copy-done.6
  29.0 0.0 copy-done.7
  29.0 2.1 %shard_map.152 = f32[16,80,128]{2,1,0:T(8,128)} custom-call(f32[40,3072]{1,0:T(8,128)S(1)} %get-tuple-element.10.refs_0_, f32[144,128]{1,0:T(8,128)S(1)} %get-tuple-element.11.refs_1_, f32[96,128]{1,0:T(8,128)S(1)} %collective-permute-done.refs_2_, f32[40,3072]{1,0:T(8,128)S(1)} %shard_map.150.refs_4_.refs_3_, ...), custom_call_target="tpu_custom_call" | custom-call | bytes 2288896 | tf_op jit(solution)/shard_map/pallas_call | solution.py:332
  31.1 3.6 %all-to-all-start.1 = ((f32[16,80,128]{2,1,0:T(8,128)}), f32[16,80,128]{2,1,0:T(8,128)S(1)}, u32[]{:S(2)}, u32[]{:S(2)}) async-start(f32[16,80,128]{2,1,0:T(8,128)} %shard_map.152), calls=%async_computation.1 | async-start | bytes 1310720 | tf_op jit(solution)/shard_map/all_to_all | solution.py:693
  34.7 0.0 copy-done.12
  34.7 1.3 %fusion.3.refs_4_ = f32[10,20,384]{2,1,0:T(8,128)S(1)} fusion(f32[20,10,384]{2,0,1:T(8,128)S(1)} %copy-done.12), kind=kLoop, calls=%fused_computation.5 | loop fusion | flops 537600 | bytes 614400 | tf_op jit(solution)/shard_map/exp | solution.py:43
  36.0 1.9 %collective-permute-start.3 = (f32[2,20,384]{2,1,0:T(8,128)S(1)}, f32[2,20,384]{2,1,0:T(8,128)S(1)}, u32[]{:S(2)}, u32[]{:S(2)}) collective-permute-start(f32[2,20,384]{2,1,0:T(8,128)S(1)} %get-tuple-element.19), channel_id=1, source_target_pairs={{0,1},{1,2},{2,3},{3,4},{4,5},{5,6},{6,7},{7,0},{8,9},{9,10},{10,1... | collective-permute-start | bytes 184328 | tf_op jit(solution)/shard_map/ppermute | solution.py:662
  37.9 2.9 %collective-permute-start.4 = (f32[2,20,384]{2,1,0:T(8,128)S(1)}, f32[2,20,384]{2,1,0:T(8,128)S(1)}, u32[]{:S(2)}, u32[]{:S(2)}) collective-permute-start(f32[2,20,384]{2,1,0:T(8,128)S(1)} %get-tuple-element.18), channel_id=1, source_target_pairs={{1,0},{2,1},{3,2},{4,3},{5,4},{6,5},{7,6},{0,7},{9,8},{10,9},{11,1... | collective-permute-start | bytes 184328 | tf_op jit(solution)/shard_map/ppermute | solution.py:663
  40.8 0.1 collective-permute-start.1
  40.9 1.7 %collective-permute-start.2 = (f32[10,2,384]{2,1,0:T(2,128)S(1)}, f32[10,2,384]{2,1,0:T(2,128)S(1)}, u32[]{:S(2)}, u32[]{:S(2)}) collective-permute-start(f32[10,2,384]{2,1,0:T(2,128)S(1)} %get-tuple-element.20), channel_id=1, source_target_pairs={{8,0},{16,8},{24,16},{0,24},{9,1},{17,9},{25,17},{1,25},{10,2},{18... | collective-permute-start | bytes 92168 | tf_op jit(solution)/shard_map/ppermute | solution.py:661
  42.6 2.8 %collective-permute-done.1.refs_5_ = f32[10,2,384]{2,1,0:T(2,128)S(1)} collective-permute-done((f32[10,2,384]{2,1,0:T(2,128)S(1)}, f32[10,2,384]{2,1,0:T(2,128)S(1)}, u32[]{:S(2)}, u32[]{:S(2)}) %collective-permute-start.1) | collective-permute-done | bytes 30752 | tf_op jit(solution)/shard_map/ppermute | solution.py:660
  45.4 0.0 collective-permute-done.2.refs_6_
  45.4 3.5 %collective-permute-done.3.refs_7_ = f32[2,20,384]{2,1,0:T(8,128)S(1)} collective-permute-done((f32[2,20,384]{2,1,0:T(8,128)S(1)}, f32[2,20,384]{2,1,0:T(8,128)S(1)}, u32[]{:S(2)}, u32[]{:S(2)}) %collective-permute-start.3) | collective-permute-done | bytes 61472 | tf_op jit(solution)/shard_map/ppermute | solution.py:662
  48.9 0.0 collective-permute-done.4.refs_8_
  48.9 0.0 all-to-all-done.1.refs_0_
  48.9 0.0 copy-done.1
  48.9 0.0 copy-done.2
  48.9 0.0 copy-done.3
  48.9 2.9 %shard_map.153 = (f32[10,20,384]{2,1,0:T(8,128)S(1)}, f32[10,20,384]{2,1,0:T(8,128)S(1)}, f32[32,1,128]{2,1,0:T(1,128)S(1)}) custom-call(f32[16,80,128]{2,1,0:T(8,128)S(1)} %all-to-all-done.1.refs_0_, bf16[512,384]{1,0:T(8,128)(2,1)S(1)} %copy-done.2, bf16[512,384]{1,0:T(8,128)(2,1)S(1)} %copy-done.3, f32[10,20,384]{2,1,0:T(8,128)S(1)} %bitcast.21, ...), custom_call_target="tpu_custom_call" | custom-call | bytes 2871296 | tf_op jit(solution)/shard_map/pallas_call | solution.py:332
  51.8 10.0 %all_to_all.15.refs_0_ = f32[32,1,128]{2,1,0:T(1,128)S(1)} all-to-all(f32[32,1,128]{2,1,0:T(1,128)S(1)} %get-tuple-element.13), channel_id=1, replica_groups=mesh['gx'=4,'gh'=2,'gl'=4] {'gx','gh','gl'}, dimensions={0} | all-to-all | bytes 32768 | tf_op jit(solution)/shard_map/all_to_all | solution.py:709
  61.8 1.0 %shard_map.154 = (f32[10,20,384]{2,1,0:T(8,128)}, f32[10,20,384]{2,1,0:T(8,128)}) custom-call(f32[32,1,128]{2,1,0:T(1,128)S(1)} %all_to_all.15.refs_0_, f32[10,20,384]{2,1,0:T(8,128)S(1)} %bitcast.22, f32[10,20,384]{2,1,0:T(8,128)S(1)} %get-tuple-element.14.refs_2_, f32[10,20,384]{2,1,0:T(8,128)S(1)} %get-tuple-element.15.refs_3_), custom_call_target="tpu_custom_call" | custom-call | bytes 1552384 | tf_op jit(solution)/shard_map/pallas_call | solution.py:332
  (2 shorter events, 0.0 us)
Async XLA Ops:
  0.6 1.0 %copy-start = (f32[20,10,384]{2,0,1:T(8,128)S(1)}, f32[20,10,384]{2,0,1:T(8,128)}, u32[]{:S(2)}) copy-start(f32[20,10,384]{2,0,1:T(8,128)} %param.15) | copy-start | bytes 921604
  1.6 1.0 %copy-start.4 = (bf16[384,512]{1,0:T(8,128)(2,1)S(1)}, bf16[384,512]{1,0:T(8,128)(2,1)}, u32[]{:S(2)}) copy-start(bf16[384,512]{1,0:T(8,128)(2,1)} %constant.56.clone.refs_1_) | copy-start | bytes 1179652
  2.6 1.0 %copy-start.5 = (bf16[384,512]{1,0:T(8,128)(2,1)S(1)}, bf16[384,512]{1,0:T(8,128)(2,1)}, u32[]{:S(2)}) copy-start(bf16[384,512]{1,0:T(8,128)(2,1)} %constant.57.clone.refs_2_) | copy-start | bytes 1179652
  3.6 25.4 %copy-start.6 = (bf16[224,384]{1,0:T(8,128)(2,1)S(1)}, bf16[224,384]{1,0:T(8,128)(2,1)}, u32[]{:S(2)}) copy-start(bf16[224,384]{1,0:T(8,128)(2,1)} %constant.65.clone.refs_7_) | copy-start | bytes 516100
  3.6 25.4 %copy-start.7 = (f32[6,40,128]{2,1,0:T(8,128)S(1)}, f32[6,40,128]{2,1,0:T(8,128)}, u32[]{:S(2)}) copy-start(f32[6,40,128]{2,1,0:T(8,128)} %constant.64.clone.refs_6_) | copy-start | bytes 368644
  3.6 31.0 %copy-start.12 = (f32[20,10,384]{2,0,1:T(8,128)S(1)}, f32[20,10,384]{2,0,1:T(8,128)}, u32[]{:S(2)}) copy-start(f32[20,10,384]{2,0,1:T(8,128)} %param.14) | copy-start | bytes 921604
  6.0 42.9 %copy-start.1 = (f32[20,10,384]{2,0,1:T(8,128)S(1)}, f32[20,10,384]{2,0,1:T(8,128)}, u32[]{:S(2)}) copy-start(f32[20,10,384]{2,0,1:T(8,128)} %param.15) | copy-start | bytes 921604
  6.0 42.9 %copy-start.2 = (bf16[512,384]{1,0:T(8,128)(2,1)S(1)}, bf16[512,384]{1,0:T(8,128)(2,1)}, u32[]{:S(2)}) copy-start(bf16[512,384]{1,0:T(8,128)(2,1)} %constant.66.clone.refs_1_) | copy-start | bytes 1179652
  6.0 42.9 %copy-start.3 = (bf16[512,384]{1,0:T(8,128)(2,1)S(1)}, bf16[512,384]{1,0:T(8,128)(2,1)}, u32[]{:S(2)}) copy-start(bf16[512,384]{1,0:T(8,128)(2,1)} %constant.67.clone.refs_2_) | copy-start | bytes 1179652
  6.0 14.0 %all-to-all-start = ((f32[16,40,128]{2,1,0:T(8,128)}), f32[16,40,128]{2,1,0:T(8,128)S(1)}, u32[]{:S(2)}, u32[]{:S(2)}) async-start(f32[16,40,128]{2,1,0:T(8,128)} %shard_map.149), calls=%async_computation | async-start | bytes 655360 | tf_op jit(solution)/shard_map/all_to_all | solution.py:658
  13.2 0.7 %copy-start.10 = (f32[40,128]{1,0:T(8,128)S(1)}, f32[40,128]{1,0:T(8,128)}, u32[]{:S(2)}) copy-start(f32[40,128]{1,0:T(8,128)} %constant.60.clone.refs_0_) | copy-start | bytes 61444
  20.0 0.7 %copy-start.8 = (bf16[40,144]{1,0:T(8,128)(2,1)S(1)}, bf16[40,144]{1,0:T(8,128)(2,1)}, u32[]{:S(2)}) copy-start(bf16[40,144]{1,0:T(8,128)(2,1)} %constant.61.clone.refs_2_.refs_5_) | copy-start | bytes 34564
  20.8 0.8 %copy-start.9 = (bf16[128,240]{1,0:T(8,128)(2,1)S(1)}, bf16[128,240]{1,0:T(8,128)(2,1)}, u32[]{:S(2)}) copy-start(bf16[128,240]{1,0:T(8,128)(2,1)} %constant.62.clone.refs_1_) | copy-start | bytes 184324
  21.6 0.7 %copy-start.11 = (bf16[8,144]{1,0:T(8,128)(2,1)S(1)}, bf16[8,144]{1,0:T(8,128)(2,1)}, u32[]{:S(2)}) copy-start(bf16[8,144]{1,0:T(8,128)(2,1)} %constant.63.clone.refs_3_) | copy-start | bytes 6916
  23.1 5.8 %collective-permute-start = (f32[96,128]{1,0:T(8,128)S(1)}, f32[96,128]{1,0:T(8,128)S(1)}, u32[]{:S(2)}, u32[]{:S(2)}) collective-permute-start(f32[96,128]{1,0:T(8,128)S(1)} %get-tuple-element.12), channel_id=1, source_target_pairs={{0,4},{4,0},{1,5},{5,1},{2,6},{6,2},{3,7},{7,3},{8,12},{12,8},{9,1... | collective-permute-start | bytes 147464 | tf_op jit(solution)/shard_map/ppermute | solution.py:680
  31.1 17.8 %all-to-all-start.1 = ((f32[16,80,128]{2,1,0:T(8,128)}), f32[16,80,128]{2,1,0:T(8,128)S(1)}, u32[]{:S(2)}, u32[]{:S(2)}) async-start(f32[16,80,128]{2,1,0:T(8,128)} %shard_map.152), calls=%async_computation.1 | async-start | bytes 1310720 | tf_op jit(solution)/shard_map/all_to_all | solution.py:693
  36.0 12.8 %collective-permute-start.3 = (f32[2,20,384]{2,1,0:T(8,128)S(1)}, f32[2,20,384]{2,1,0:T(8,128)S(1)}, u32[]{:S(2)}, u32[]{:S(2)}) collective-permute-start(f32[2,20,384]{2,1,0:T(8,128)S(1)} %get-tuple-element.19), channel_id=1, source_target_pairs={{0,1},{1,2},{2,3},{3,4},{4,5},{5,6},{6,7},{7,0},{8,9},{9,10},{10,1... | collective-permute-start | bytes 184328 | tf_op jit(solution)/shard_map/ppermute | solution.py:662
  37.9 11.0 %collective-permute-start.4 = (f32[2,20,384]{2,1,0:T(8,128)S(1)}, f32[2,20,384]{2,1,0:T(8,128)S(1)}, u32[]{:S(2)}, u32[]{:S(2)}) collective-permute-start(f32[2,20,384]{2,1,0:T(8,128)S(1)} %get-tuple-element.18), channel_id=1, source_target_pairs={{1,0},{2,1},{3,2},{4,3},{5,4},{6,5},{7,6},{0,7},{9,8},{10,9},{11,1... | collective-permute-start | bytes 184328 | tf_op jit(solution)/shard_map/ppermute | solution.py:663
  40.8 4.6 %collective-permute-start.1 = (f32[10,2,384]{2,1,0:T(2,128)S(1)}, f32[10,2,384]{2,1,0:T(2,128)S(1)}, u32[]{:S(2)}, u32[]{:S(2)}) collective-permute-start(f32[10,2,384]{2,1,0:T(2,128)S(1)} %get-tuple-element.21), channel_id=1, source_target_pairs={{0,8},{8,16},{16,24},{24,0},{1,9},{9,17},{17,25},{25,1},{2,10},{10... | collective-permute-start | bytes 92168 | tf_op jit(solution)/shard_map/ppermute | solution.py:660
  40.9 4.5 %collective-permute-start.2 = (f32[10,2,384]{2,1,0:T(2,128)S(1)}, f32[10,2,384]{2,1,0:T(2,128)S(1)}, u32[]{:S(2)}, u32[]{:S(2)}) collective-permute-start(f32[10,2,384]{2,1,0:T(2,128)S(1)} %get-tuple-element.20), channel_id=1, source_target_pairs={{8,0},{16,8},{24,16},{0,24},{9,1},{17,9},{25,17},{1,25},{10,2},{18... | collective-permute-start | bytes 92168 | tf_op jit(solution)/shard_map/ppermute | solution.py:661

commit v3 on v2

--- a/solution.py
+++ b/solution.py
@@ -230,6 +230,7 @@
         self.deep = self.chunks * LANES
         self.extra = self.cx // self.yq if self.yq else 0
         self.rows = up(2 * self.xe + self.cx + self.extra, 8)
+        self.mirror = self.nx // 2 + 1
         self.lines = self.cy * self.xw + (2 * HALO - 1) * self.xp + self.yq * 8
 
     def fits(self):
@@ -243,6 +244,8 @@
             and self.step % 8 == 0
             and self.nx <= LANES
             and 2 * (LANES - self.nx) >= self.nx
+            and 3 * self.mirror <= LANES
+            and self.ny % 8 == 0
             and self.nx % 16 == 0
             and self.ny >= 2 * HALO
             and self.gx * self.xw <= LANES
@@ -256,12 +259,12 @@
         table[:, place] = cas_table(wave, wave, self.nz)
         return halves(table)
 
-    def z_backward(self):
-        return tuple(np.ascontiguousarray(part.T) for part in self.z_forward())
+    def x_waves(self):
+        return np.concatenate([np.arange(self.mirror), np.arange(self.nx - 1, self.mirror - 1, -1)])
 
     def x_forward(self):
         table = np.zeros((LANES, self.nx))
-        table[: self.nx] = cas_table(np.arange(self.nx), np.arange(self.nx), self.nx)
+        table[: self.nx] = cas_table(self.x_waves(), np.arange(self.nx), self.nx)
         return thirds(table)
 
     def y_both(self):
@@ -286,7 +289,7 @@
     def x_backward(self):
         wide = np.zeros((self.gx * self.xw, LANES))
         own = np.zeros((self.gx * self.xp, LANES))
-        waves = np.arange(self.nx)
+        waves = self.x_waves()
         for g in range(self.gx):
             x = (g * self.cx - HALO + np.arange(self.xe)) % self.nx
             wide[g * self.xw : g * self.xw + self.xe, : self.nx] = cas_table(x, waves, self.nx)
@@ -297,14 +300,39 @@
 
     def plane(self):
         plane = np.full((self.ny, LANES), 1e30)
-        plane[:, : self.nx] = symbol_table(self.nx)[None, :] + symbol_table(self.ny)[:, None]
+        lam_x = symbol_table(self.nx)[self.x_waves()]
+        plane[:, : self.nx] = lam_x[None, :] + symbol_table(self.ny)[:, None]
         return plane.astype(np.float32)
 
-    def waves(self):
-        return symbol_table(self.nz).reshape(self.ng, self.kz).astype(np.float32)
+    def coarse_pack(self):
+        parts = [self.x_forward(), self.y_both(), self.y_ends(), self.x_backward()]
+        width = max(part.shape[1] for part in parts)
+        self.places, rows = [], 0
+        for part in parts:
+            self.places.append((rows, part.shape))
+            rows = up(rows + part.shape[0], 16)
+        table = np.zeros((rows, width), ml_dtypes.bfloat16)
+        for (row, shape), part in zip(self.places, parts):
+            table[row : row + shape[0], : shape[1]] = part
+        return table
+
+    def fine_pack(self):
+        parts = [self.plane(), self.y_sources(), self.joins()]
+        return np.concatenate([part.reshape(-1, LANES) for part in parts], axis=0)
+
+    def coarse(self, ref, which):
+        row, shape = self.places[which]
+        return ref[row : row + shape[0], : shape[1]]
+
+    def join_rows(self, ref, row):
+        me = lax.axis_index("gx") * self.gl + lax.axis_index("gl")
+        size = (2 * HALO + 1) * self.kz
+        start = (2 * HALO + 1) * self.ny + me * size + row * self.kz
+        return ref[pl.ds(pl.multiple_of(start, 8), self.kz), :]
 
     def joins(self):
-        lam_x, lam_y, lam_z = symbol_table(self.nx), symbol_table(self.ny), symbol_table(self.nz)
+        lam_x = symbol_table(self.nx)[: self.mirror]
+        lam_y, lam_z = symbol_table(self.ny), symbol_table(self.nz)
         total = EPS_PRECOND * (lam_z[:, None, None] + lam_x[None, :, None] + lam_y) + SHIFT_PRECOND
         green = np.real(np.fft.ifft(1.0 / total, axis=-1))
         i = np.arange(HALO)
@@ -317,9 +345,11 @@
         eye = np.eye(HALO)
         even = np.linalg.inv(eye - 2.0 * (near + far) @ band)
         odd = np.linalg.inv(eye + 2.0 * (near - far) @ band)
-        both = np.stack([even, odd], axis=2).reshape(self.nz, self.nx, 2 * HALO * HALO)
-        table = np.zeros((self.ng, 2 * HALO * HALO, self.kz, LANES), np.float32)
-        table[..., : self.nx] = both.reshape(self.ng, self.kz, self.nx, -1).transpose(0, 3, 1, 2)
+        both = np.stack([even, odd], axis=2).reshape(self.ng, self.kz, self.mirror, 2 * HALO, HALO)
+        both = both.transpose(0, 3, 1, 4, 2).reshape(self.ng, 2 * HALO, self.kz, HALO * self.mirror)
+        table = np.zeros((self.ng, 2 * HALO + 1, self.kz, LANES), np.float32)
+        table[:, : 2 * HALO, :, : HALO * self.mirror] = both
+        table[:, 2 * HALO] = lam_z.reshape(self.ng, self.kz, 1)
         return table
 
 
@@ -327,7 +357,7 @@
 ANY_SPEC = pl.BlockSpec(memory_space=pl.ANY)
 
 
-def call(kernel, outs, args, scratch=(), specs=None):
+def call(kernel, outs, args, scratch=(), specs=None, limit=VMEM_LIMIT, flops=0):
     nbytes = sum(int(np.prod(a.shape)) * a.dtype.itemsize for a in (*args, *outs))
     return pl.pallas_call(
         kernel,
@@ -335,8 +365,8 @@
         in_specs=specs or [VMEM_SPEC] * len(args),
         out_specs=tuple([VMEM_SPEC] * len(outs)),
         scratch_shapes=list(scratch),
-        compiler_params=pltpu.CompilerParams(vmem_limit_bytes=VMEM_LIMIT),
-        cost_estimate=pl.CostEstimate(flops=0, bytes_accessed=nbytes, transcendentals=0),
+        compiler_params=pltpu.CompilerParams(vmem_limit_bytes=limit),
+        cost_estimate=pl.CostEstimate(flops=flops, bytes_accessed=nbytes, transcendentals=0),
     )(*args)
 
 
@@ -353,15 +383,18 @@
     return (lane >= slot * width) & (lane < (slot + 1) * width)
 
 
-def forward_kernel(p, charge_in, high_in, low_in, out, charge, high_z, low_z, sems):
+def fetched(pairs, sems):
     copies = [
         pltpu.make_async_copy(source, target, sems.at[i])
-        for i, (source, target) in enumerate(
-            ((charge_in, charge), (high_in, high_z), (low_in, low_z))
-        )
+        for i, (source, target) in enumerate(pairs)
     ]
     for copy in copies:
         copy.start()
+    return copies
+
+
+def forward_kernel(p, charge_in, high_in, low_in, out, charge, high_z, low_z, sems):
+    copies = fetched(((charge_in, charge), (high_in, high_z), (low_in, low_z)), sems)
     copies[0].wait()
     rows = [padded_rows(charge[y], p.xp) for y in range(p.cy)]
     high, low = split(jnp.concatenate(rows, axis=0))
@@ -381,9 +414,11 @@
             out[target, part * p.cx : (part + 1) * p.cx] = block[: p.cx]
 
 
-def table_kernel(p, plane, waves, out):
+def table_kernel(p, fine, out):
+    plane = fine[: p.ny, :]
+    waves = p.join_rows(fine, 2 * HALO)
     for k in range(p.kz):
-        symbol = EPS_PRECOND * (plane[...] + waves[k]) + SHIFT_PRECOND
+        symbol = EPS_PRECOND * (plane + waves[k : k + 1]) + SHIFT_PRECOND
         out[:, k * LANES : (k + 1) * LANES] = 1.0 / (float(p.ny) * symbol)
 
 
@@ -391,7 +426,8 @@
     return values[:, k * LANES : (k + 1) * LANES]
 
 
-def solve_kernel(p, blocks, x_fwd, y_both, y_ends, table, spectrum_out, own, sent, turned, ends):
+def solve_kernel(p, blocks, coarse, table, spectrum_out, own, sent, turned, ends):
+    x_fwd, y_both, y_ends = (p.coarse(coarse, i) for i in range(3))
     columns = []
     for gl in range(p.gl):
         for part in range(2):
@@ -399,16 +435,16 @@
                 blocks[gx * p.gl + gl, part * p.cx : (part + 1) * p.cx] for gx in range(p.gx)
             ]
             columns.append(jnp.concatenate(pieces, axis=0))
-    along_x = mul(x_fwd[...], stacked(jnp.concatenate(columns, axis=1), 0))
+    along_x = mul(x_fwd, stacked(jnp.concatenate(columns, axis=1), 0))
     for b in range(2 * p.gl):
         turned[pl.ds(b * p.step, LANES), :] = lanes_of(along_x, b).T
     field = jnp.concatenate(
         [turned[pl.ds(k, p.ny, stride=p.kz), :] for k in range(p.kz)], axis=1
     )
-    along_y = mul(y_both[...], stacked(padded_rows(field, p.yp), 0))
+    along_y = mul(y_both, stacked(padded_rows(field, p.yp), 0))
     solved = along_y * table[...]
     spectrum_out[...] = solved
-    at_ends = mul(y_ends[...], stacked(padded_rows(solved, p.yp), 0))
+    at_ends = mul(y_ends, stacked(padded_rows(solved, p.yp), 0))
     for k in range(p.kz):
         ends[pl.ds(k, 8, stride=p.kz), :] = lanes_of(at_ends, k)
     own[...] = ends[pl.ds(0, 2 * HALO * p.kz), :]
@@ -421,9 +457,11 @@
 
 
 def return_kernel(
-    p, spectrum_in, own, received, table, joins, y_both, y_sources, x_bwd,
+    p, spectrum_in, own, received, table, fine, coarse,
     out, sources, planes,
 ):
+    y_both, x_bwd = p.coarse(coarse, 1), p.coarse(coarse, 3)
+    y_sources = [fine[(j + 1) * p.ny : (j + 2) * p.ny, :] for j in range(2 * HALO)]
     lane = lane_index(p.kz)
     free = LANES - p.nx
     part = [received[pl.ds(i * p.kz, p.kz), :] for i in range(4)]
@@ -438,11 +476,18 @@
     odd = [jump[j] - jump[HALO + j] for j in range(HALO)]
 
     def mixed(base, vector):
-        return [
-            sum(joins[base + HALO * i + j] * vector[j] for j in range(HALO)) for i in range(HALO)
-        ]
-
-    even_full, odd_full = mixed(0, even), mixed(HALO * HALO, odd)
+        results = []
+        for i in range(HALO):
+            packed = p.join_rows(fine, base + i)
+            total = 0.0
+            for j in range(HALO):
+                first = moved(packed, -j * p.mirror)
+                second = moved(packed, p.mirror - 1 - j * p.mirror)
+                total = total + jnp.where(lane < p.mirror, first, second) * vector[j]
+            results.append(total)
+        return results
+
+    even_full, odd_full = mixed(0, even), mixed(HALO, odd)
     low_full = [0.5 * (e + o) for e, o in zip(even_full, odd_full)]
     high_full = [0.5 * (e - o) for e, o in zip(even_full, odd_full)]
     far_low = [other[j] - 0.5 * (low_full[j] - jump[j]) for j in range(HALO)]
@@ -461,7 +506,7 @@
             spectrum_in[:, k * LANES : (k + 1) * LANES]
             + added * table[:, k * LANES : (k + 1) * LANES]
         )
-    back_y = mul(y_both[...], stacked(padded_rows(jnp.concatenate(whole, axis=1), p.yp), 0))
+    back_y = mul(y_both, stacked(padded_rows(jnp.concatenate(whole, axis=1), p.yp), 0))
     base = p.edge
     for k in range(p.kz):
         planes[pl.ds(base + k, p.ny, stride=p.kz), :] = lanes_of(back_y, k)
@@ -541,7 +586,7 @@
                 line = jnp.where(between(here, slot, p.kz), part, line)
             lines[at : at + rows, chunk * LANES : (chunk + 1) * LANES] = line
     high, low = split(lines[...])
-    whole = mul(high, high_z[...]) + mul(low, high_z[...]) + mul(high, low_z[...])
+    whole = mul_t(high, high_z[...]) + mul_t(low, high_z[...]) + mul_t(high, low_z[...])
     for y in range(p.cy):
         first, rows, piece, at = windows[y]
         off = (y // p.yq) * p.xe - first
@@ -629,7 +674,7 @@
 def local_planes(p, density, charge):
     group = ("gx", "gl")
     along_y = ("gh", "gl")
-    f32, bf16 = jnp.float32, jnp.bfloat16
+    f32 = jnp.float32
 
     def shape(*dims):
         return jax.ShapeDtypeStruct(dims, f32)
@@ -642,48 +687,49 @@
 
     density = density.transpose(1, 0, 2)
     charge = charge.transpose(1, 0, 2)
-    high_z, low_z = p.z_forward()
+    high_z, low_z = (jnp.asarray(part) for part in p.z_forward())
+    coarse, fine = jnp.asarray(p.coarse_pack()), jnp.asarray(p.fine_pack())
     (blocks,) = call(
         lambda *refs: forward_kernel(p, *refs),
         [shape(p.ng, 2 * p.cx, LANES)],
-        [charge, jnp.asarray(high_z), jnp.asarray(low_z)],
+        [charge, high_z, low_z],
         [
             pltpu.VMEM((p.cy, p.cx, p.nz), f32),
-            pltpu.VMEM((p.nz, p.deep), bf16),
-            pltpu.VMEM((p.nz, p.deep), bf16),
+            pltpu.VMEM((p.nz, p.deep), jnp.bfloat16),
+            pltpu.VMEM((p.nz, p.deep), jnp.bfloat16),
             pltpu.SemaphoreType.DMA((3,)),
         ],
         specs=[ANY_SPEC] * 3,
+        limit=None,
     )
     blocks = lax.all_to_all(blocks, group, 0, 0)
+    (table,) = call(
+        lambda *refs: table_kernel(p, *refs), [shape(p.ny, p.kz * LANES)], [fine]
+    )
     eps = permittivity(density)
+    blocks, eps, table = lax.optimization_barrier(
+        (blocks, eps, table)
+    )
+    spectrum_half, own, sent = call(
+        lambda *refs: solve_kernel(p, *refs),
+        [shape(p.ny, p.kz * LANES), shape(2 * HALO * p.kz, LANES), shape(4 * p.kz, LANES)],
+        [blocks, coarse, table],
+        [pltpu.VMEM((p.ny * p.kz + LANES, LANES), f32), pltpu.VMEM((8 * p.kz, LANES), f32)],
+    )
+    sent, eps = lax.optimization_barrier((sent, eps))
+    received = lax.ppermute(sent, "gh", [(0, 1), (1, 0)])
     ex_low = lax.ppermute(eps[:, p.cx - 2 :], "gx", ring(p.gx))
     ex_high = lax.ppermute(eps[:, :2], "gx", back(ring(p.gx)))
     ey_low = lax.ppermute(eps[p.cy - 2 :], along_y, ring(2 * p.gl))
     ey_high = lax.ppermute(eps[:2], along_y, back(ring(2 * p.gl)))
-    me = lax.axis_index("gx") * p.gl + lax.axis_index("gl")
-    waves = lax.dynamic_slice_in_dim(jnp.asarray(p.waves()), me, 1, axis=0)
-    waves = jnp.broadcast_to(waves.reshape(p.kz, 1, 1), (p.kz, 1, LANES))
-    joins = lax.dynamic_index_in_dim(jnp.asarray(p.joins()), me, 0, keepdims=False)
-    (table,) = call(
-        lambda *refs: table_kernel(p, *refs),
-        [shape(p.ny, p.kz * LANES)],
-        [jnp.asarray(p.plane()), waves],
-    )
-    y_both = jnp.asarray(p.y_both())
-    spectrum_half, own, sent = call(
-        lambda *refs: solve_kernel(p, *refs),
-        [shape(p.ny, p.kz * LANES), shape(2 * HALO * p.kz, LANES), shape(4 * p.kz, LANES)],
-        [blocks, jnp.asarray(p.x_forward()), y_both, jnp.asarray(p.y_ends()), table],
-        [pltpu.VMEM((p.ny * p.kz + LANES, LANES), f32), pltpu.VMEM((8 * p.kz, LANES), f32)],
-    )
-    received = lax.ppermute(sent, "gh", [(0, 1), (1, 0)])
+    received, ex_low, ex_high, ey_low, ey_high = lax.optimization_barrier(
+        (received, ex_low, ex_high, ey_low, ey_high)
+    )
     (blocks,) = call(
         lambda *refs: return_kernel(p, *refs),
         [shape(p.ng, p.rows, LANES)],
         [
-            spectrum_half, own, received, table, joins, y_both,
-            jnp.asarray(p.y_sources()), jnp.asarray(p.x_backward()),
+            spectrum_half, own, received, table, fine, coarse,
         ],
         [
             pltpu.VMEM((2 * HALO * p.kz, LANES), f32),
@@ -691,13 +737,11 @@
         ],
     )
     blocks = lax.all_to_all(blocks, group, 0, 0)
-    back_high, back_low = p.z_backward()
     pre, image, sums = call(
         lambda *refs: stencil_kernel(p, *refs),
         [shape(p.cy, p.cx, p.nz), shape(p.cy, p.cx, p.nz), shape(2 * p.ng, 1, LANES)],
         [
-            blocks, jnp.asarray(back_high), jnp.asarray(back_low), charge,
-            eps, ex_low, ex_high, ey_low, ey_high,
+            blocks, high_z, low_z, charge, eps, ex_low, ex_high, ey_low, ey_high,
         ],
         [
             pltpu.VMEM((p.lines, p.deep), f32),

time: 63.6 us -> 57.8 us (0.909)
  blocking collectives: 10 us -> 23.3 us
  local copies, waits for them, and re-layouts: 7.75 us -> 0.07 us
  starting transfers between devices: 19.2 us -> 11.7 us
  waiting for transfers between devices: 14.5 us -> 11.3 us
    all_to_all x0 -> x1, blocking collectives: none -> 14.4 us  [local_planes(): blocks = lax.all_to_all(blocks, group, 0, 0)]
    unnamed x26 -> x12, local copies, waits for them, and re-layouts: 5.98 us -> 0.04 us
    all_to_all x2 -> x1, starting transfers between devices: 10 us -> 6.43 us  [local_planes(): blocks = lax.all_to_all(blocks, group, 0, 0)]
    ppermute x1, waiting for transfers between devices: 2.28 us -> 0.01 us  [local_planes(): received = lax.ppermute(sent, 'gh', [(0, 1), (1, 0)])]
    ppermute x1, starting transfers between devices: 2.92 us -> 0.79 us  [local_planes(): ey_high = lax.ppermute(eps[:2], along_y, back(ring(2 * p.gl)))]
    ppermute x1, starting transfers between devices: 1.73 us -> 0.06 us  [local_planes(): ex_high = lax.ppermute(eps[:, :2], 'gx', back(ring(p.gx)))]
    all_to_all x1, blocking collectives: 10 us -> 8.81 us  [local_planes(): sums = lax.all_to_all(sums, ('gx', 'gh', 'gl'), 0, 0)]
    ppermute x1, waiting for transfers between devices: 3.46 us -> 2.29 us  [local_planes(): ey_low = lax.ppermute(eps[p.cy - 2:], along_y, ring(2 * p.gl))]
  transfers between devices with their start and end apart: 7 -> 6, of which waited for: 4 -> 4; matrix products, arithmetic and copies ran while one was open for 5% -> 2% of each run, Pallas kernels for 0% -> 0%
where the time goes in v3:
time: 57.8 us; the launch traced here: 57.5 us
  blocking collectives  23.3 us (40%)
  starting transfers between devices  11.7 us (20%)
  waiting for transfers between devices  11.3 us (20%)
  Pallas kernels  9.12 us (16%)
  other arithmetic  1.32 us (2%)
  between operations  0.76 us (1%)
    all_to_all x1, blocking collectives, local_planes(): blocks = lax.all_to_all(blocks, group, 0, 0)  14.4 us
    pallas_call x6, Pallas kernels, call(): pl.pallas_call(kernel, out_shape=tuple(outs), in_specs=specs or [VMEM_SPE...  9.12 us
    all_to_all x1, blocking collectives, local_planes(): sums = lax.all_to_all(sums, ('gx', 'gh', 'gl'), 0, 0)  8.81 us
    all_to_all x1, starting transfers between devices, local_planes(): blocks = lax.all_to_all(blocks, group, 0, 0)  6.43 us
    all_to_all x1, waiting for transfers between devices, local_planes(): blocks = lax.all_to_all(blocks, group, 0, 0)  6.13 us
    ppermute x1, starting transfers between devices, local_planes(): received = lax.ppermute(sent, 'gh', [(0, 1), (1, 0)])  2.61 us
    ppermute x1, waiting for transfers between devices, local_planes(): ey_low = lax.ppermute(eps[p.cy - 2:], along_y, ring(2 * p.gl))  2.29 us
    ppermute x1, waiting for transfers between devices, local_planes(): ex_low = lax.ppermute(eps[:, p.cx - 2:], 'gx', ring(p.gx))  1.81 us
  transfers between devices with their start and end apart: 6, of which 4 were waited for; matrix products, arithmetic and copies ran while one was open for 2% of the time, Pallas kernels for 0%

profile of v3, /device:TPU:0, one launch (start us, length us, event | category | flops | bytes accessed | tf_op | source)
XLA Modules:
  0.0 57.5 jit_solution(5032996131414233645)
XLA Ops:
  0.6 0.0 copy-start
  0.6 3.0 %shard_map.77 = f32[16,40,128]{2,1,0:T(8,128)} custom-call(f32[10,20,384]{2,1,0:T(8,128)} %bitcast.16, bf16[384,512]{1,0:T(8,128)(2,1)} %constant.23.clone.refs_1_, bf16[384,512]{1,0:T(8,128)(2,1)} %constant.24.clone.refs_2_), custom_call_target="tpu_custom_call" | custom-call | bytes 1421312 | tf_op jit(solution)/shard_map/pallas_call | solution.py:362
  3.6 0.0 copy-start.5
  3.6 6.4 %all-to-all-start = ((f32[16,40,128]{2,1,0:T(8,128)}), f32[16,40,128]{2,1,0:T(8,128)S(1)}, u32[]{:S(2)}, u32[]{:S(2)}) async-start(f32[16,40,128]{2,1,0:T(8,128)} %shard_map.77), calls=%async_computation | async-start | bytes 655360 | tf_op jit(solution)/shard_map/all_to_all | solution.py:705
  10.1 0.0 copy-done
  10.1 0.0 copy-start.4
  10.1 0.1 shard_map.78.refs_2_.refs_3_
  10.2 0.0 copy-done.5
  10.2 1.3 %fusion.3.refs_4_ = f32[10,20,384]{2,1,0:T(8,128)S(1)} fusion(f32[20,10,384]{2,0,1:T(8,128)S(1)} %copy-done.5), kind=kLoop, calls=%fused_computation.5 | loop fusion | flops 537600 | bytes 614400 | tf_op jit(solution)/shard_map/exp | solution.py:43
  11.5 6.1 %all-to-all-done.refs_0_ = f32[16,40,128]{2,1,0:T(8,128)S(1)} async-done(((f32[16,40,128]{2,1,0:T(8,128)}), f32[16,40,128]{2,1,0:T(8,128)S(1)}, u32[]{:S(2)}, u32[]{:S(2)}) %all-to-all-start) | async-done | bytes 327712 | tf_op jit(solution)/shard_map/all_to_all | solution.py:705
  17.7 0.0 copy-done.4
  17.7 0.8 %shard_map.79 = (f32[40,3072]{1,0:T(8,128)S(1)}, f32[144,128]{1,0:T(8,128)S(1)}, f32[96,128]{1,0:T(8,128)S(1)}) custom-call(f32[16,40,128]{2,1,0:T(8,128)S(1)} %all-to-all-done.refs_0_, bf16[416,384]{1,0:T(8,128)(2,1)S(1)} %copy-done.4, f32[40,3072]{1,0:T(8,128)S(1)} %shard_map.78.refs_2_.refs_3_), custom_call_target="tpu_custom_call" | custom-call | bytes 1753088 | tf_op jit(solution)/shard_map/pallas_call | solution.py:362
  18.5 2.6 %collective-permute-start = (f32[96,128]{1,0:T(8,128)S(1)}, f32[96,128]{1,0:T(8,128)S(1)}, u32[]{:S(2)}, u32[]{:S(2)}) collective-permute-start(f32[96,128]{1,0:T(8,128)S(1)} %get-tuple-element.26), channel_id=1, source_target_pairs={{0,4},{4,0},{1,5},{5,1},{2,6},{6,2},{3,7},{7,3},{8,12},{12,8},{9,1... | collective-permute-start | bytes 147464 | tf_op jit(solution)/shard_map/ppermute | solution.py:720
  21.1 0.8 %collective-permute-start.4 = (f32[2,20,384]{2,1,0:T(8,128)S(1)}, f32[2,20,384]{2,1,0:T(8,128)S(1)}, u32[]{:S(2)}, u32[]{:S(2)}) collective-permute-start(f32[2,20,384]{2,1,0:T(8,128)S(1)} %get-tuple-element.38), channel_id=1, source_target_pairs={{1,0},{2,1},{3,2},{4,3},{5,4},{6,5},{7,6},{0,7},{9,8},{10,9},{11,1... | collective-permute-start | bytes 184328 | tf_op jit(solution)/shard_map/ppermute | solution.py:724
  21.9 1.3 %collective-permute-start.3 = (f32[2,20,384]{2,1,0:T(8,128)S(1)}, f32[2,20,384]{2,1,0:T(8,128)S(1)}, u32[]{:S(2)}, u32[]{:S(2)}) collective-permute-start(f32[2,20,384]{2,1,0:T(8,128)S(1)} %get-tuple-element.39), channel_id=1, source_target_pairs={{0,1},{1,2},{2,3},{3,4},{4,5},{5,6},{6,7},{7,0},{8,9},{9,10},{10,1... | collective-permute-start | bytes 184328 | tf_op jit(solution)/shard_map/ppermute | solution.py:723
  23.2 0.1 collective-permute-start.2
  23.3 0.5 collective-permute-start.1
  23.8 1.1 %collective-permute-done.2.refs_6_ = f32[10,2,384]{2,1,0:T(2,128)S(1)} collective-permute-done((f32[10,2,384]{2,1,0:T(2,128)S(1)}, f32[10,2,384]{2,1,0:T(2,128)S(1)}, u32[]{:S(2)}, u32[]{:S(2)}) %collective-permute-start.2) | collective-permute-done | bytes 30752 | tf_op jit(solution)/shard_map/ppermute | solution.py:722
  24.9 1.8 %collective-permute-done.1.refs_5_ = f32[10,2,384]{2,1,0:T(2,128)S(1)} collective-permute-done((f32[10,2,384]{2,1,0:T(2,128)S(1)}, f32[10,2,384]{2,1,0:T(2,128)S(1)}, u32[]{:S(2)}, u32[]{:S(2)}) %collective-permute-start.1) | collective-permute-done | bytes 30752 | tf_op jit(solution)/shard_map/ppermute | solution.py:721
  26.7 0.0 collective-permute-done.refs_2_
  26.7 0.0 collective-permute-done.4.refs_8_
  26.7 2.3 %collective-permute-done.3.refs_7_ = f32[2,20,384]{2,1,0:T(8,128)S(1)} collective-permute-done((f32[2,20,384]{2,1,0:T(8,128)S(1)}, f32[2,20,384]{2,1,0:T(8,128)S(1)}, u32[]{:S(2)}, u32[]{:S(2)}) %collective-permute-start.3) | collective-permute-done | bytes 61472 | tf_op jit(solution)/shard_map/ppermute | solution.py:723
  29.0 1.3 %shard_map.80 = f32[16,80,128]{2,1,0:T(8,128)S(1)} custom-call(f32[40,3072]{1,0:T(8,128)S(1)} %get-tuple-element.22.refs_0_, f32[144,128]{1,0:T(8,128)S(1)} %get-tuple-element.23.refs_1_, f32[96,128]{1,0:T(8,128)S(1)} %collective-permute-done.refs_2_, f32[40,3072]{1,0:T(8,128)S(1)} %shard_map.78.refs_2_.refs_3_, f32[2968,128]{1,0:T(8,128)S(1)} %copy-done, ...), custom_call_target="tpu_custom_call" | custom-call | bytes 3600384 | tf_op jit(solution)/shard_map/pallas_call | solution.py:362
  30.2 0.0 copy-start.1
  30.3 0.0 copy-start.2
  30.3 0.0 copy-start.3
  30.3 14.4 %all_to_all.15.refs_0_ = f32[16,80,128]{2,1,0:T(8,128)S(1)} all-to-all(f32[16,80,128]{2,1,0:T(8,128)S(1)} %shard_map.80), channel_id=1, replica_groups=mesh['gx'=4,'gh'=2,'gl'=4] {'gx','gl'}, dimensions={0} | all-to-all | bytes 1310720 | tf_op jit(solution)/shard_map/all_to_all | solution.py:739
  44.7 0.0 copy-done.1
  44.7 0.0 copy-done.2
  44.7 0.0 copy-done.3
  44.7 2.9 %shard_map.81 = (f32[10,20,384]{2,1,0:T(8,128)S(1)}, f32[10,20,384]{2,1,0:T(8,128)S(1)}, f32[32,1,128]{2,1,0:T(1,128)S(1)}) custom-call(f32[16,80,128]{2,1,0:T(8,128)S(1)} %all_to_all.15.refs_0_, bf16[384,512]{1,0:T(8,128)(2,1)S(1)} %copy-done.3, bf16[384,512]{1,0:T(8,128)(2,1)S(1)} %copy-done.2, f32[10,20,384]{2,1,0:T(8,128)S(1)} %bitcast.17, ...), custom_call_target="tpu_custom_call" | custom-call | bytes 2871296 | tf_op jit(solution)/shard_map/pallas_call | solution.py:362
  47.6 8.8 %all_to_all.16.refs_0_ = f32[32,1,128]{2,1,0:T(1,128)S(1)} all-to-all(f32[32,1,128]{2,1,0:T(1,128)S(1)} %get-tuple-element.33), channel_id=1, replica_groups=mesh['gx'=4,'gh'=2,'gl'=4] {'gx','gh','gl'}, dimensions={0} | all-to-all | bytes 32768 | tf_op jit(solution)/shard_map/all_to_all | solution.py:753
  56.5 1.0 %shard_map.82 = (f32[10,20,384]{2,1,0:T(8,128)}, f32[10,20,384]{2,1,0:T(8,128)}) custom-call(f32[32,1,128]{2,1,0:T(1,128)S(1)} %all_to_all.16.refs_0_, f32[10,20,384]{2,1,0:T(8,128)S(1)} %bitcast.18, f32[10,20,384]{2,1,0:T(8,128)S(1)} %get-tuple-element.34.refs_2_, f32[10,20,384]{2,1,0:T(8,128)S(1)} %get-tuple-element.35.refs_3_), custom_call_target="tpu_custom_call" | custom-call | bytes 1552384 | tf_op jit(solution)/shard_map/pallas_call | solution.py:362
  (2 shorter events, 0.0 us)
Async XLA Ops:
  0.6 9.4 %copy-start = (f32[2968,128]{1,0:T(8,128)S(1)}, f32[2968,128]{1,0:T(8,128)}, u32[]{:S(2)}) copy-start(f32[2968,128]{1,0:T(8,128)} %constant.26.clone.refs_0_.refs_4_) | copy-start | bytes 4558852
  3.6 6.6 %copy-start.5 = (f32[20,10,384]{2,0,1:T(8,128)S(1)}, f32[20,10,384]{2,0,1:T(8,128)}, u32[]{:S(2)}) copy-start(f32[20,10,384]{2,0,1:T(8,128)} %param.6) | copy-start | bytes 921604
  3.6 14.0 %all-to-all-start = ((f32[16,40,128]{2,1,0:T(8,128)}), f32[16,40,128]{2,1,0:T(8,128)S(1)}, u32[]{:S(2)}, u32[]{:S(2)}) async-start(f32[16,40,128]{2,1,0:T(8,128)} %shard_map.77), calls=%async_computation | async-start | bytes 655360 | tf_op jit(solution)/shard_map/all_to_all | solution.py:705
  10.1 7.6 %copy-start.4 = (bf16[416,384]{1,0:T(8,128)(2,1)S(1)}, bf16[416,384]{1,0:T(8,128)(2,1)}, u32[]{:S(2)}) copy-start(bf16[416,384]{1,0:T(8,128)(2,1)} %constant.25.clone.refs_1_.refs_5_) | copy-start | bytes 958468
  18.5 8.2 %collective-permute-start = (f32[96,128]{1,0:T(8,128)S(1)}, f32[96,128]{1,0:T(8,128)S(1)}, u32[]{:S(2)}, u32[]{:S(2)}) collective-permute-start(f32[96,128]{1,0:T(8,128)S(1)} %get-tuple-element.26), channel_id=1, source_target_pairs={{0,4},{4,0},{1,5},{5,1},{2,6},{6,2},{3,7},{7,3},{8,12},{12,8},{9,1... | collective-permute-start | bytes 147464 | tf_op jit(solution)/shard_map/ppermute | solution.py:720
  21.1 5.6 %collective-permute-start.4 = (f32[2,20,384]{2,1,0:T(8,128)S(1)}, f32[2,20,384]{2,1,0:T(8,128)S(1)}, u32[]{:S(2)}, u32[]{:S(2)}) collective-permute-start(f32[2,20,384]{2,1,0:T(8,128)S(1)} %get-tuple-element.38), channel_id=1, source_target_pairs={{1,0},{2,1},{3,2},{4,3},{5,4},{6,5},{7,6},{0,7},{9,8},{10,9},{11,1... | collective-permute-start | bytes 184328 | tf_op jit(solution)/shard_map/ppermute | solution.py:724
  21.9 7.0 %collective-permute-start.3 = (f32[2,20,384]{2,1,0:T(8,128)S(1)}, f32[2,20,384]{2,1,0:T(8,128)S(1)}, u32[]{:S(2)}, u32[]{:S(2)}) collective-permute-start(f32[2,20,384]{2,1,0:T(8,128)S(1)} %get-tuple-element.39), channel_id=1, source_target_pairs={{0,1},{1,2},{2,3},{3,4},{4,5},{5,6},{6,7},{7,0},{8,9},{9,10},{10,1... | collective-permute-start | bytes 184328 | tf_op jit(solution)/shard_map/ppermute | solution.py:723
  23.2 1.6 %collective-permute-start.2 = (f32[10,2,384]{2,1,0:T(2,128)S(1)}, f32[10,2,384]{2,1,0:T(2,128)S(1)}, u32[]{:S(2)}, u32[]{:S(2)}) collective-permute-start(f32[10,2,384]{2,1,0:T(2,128)S(1)} %get-tuple-element.40), channel_id=1, source_target_pairs={{8,0},{16,8},{24,16},{0,24},{9,1},{17,9},{25,17},{1,25},{10,2},{18... | collective-permute-start | bytes 92168 | tf_op jit(solution)/shard_map/ppermute | solution.py:722
  23.3 3.4 %collective-permute-start.1 = (f32[10,2,384]{2,1,0:T(2,128)S(1)}, f32[10,2,384]{2,1,0:T(2,128)S(1)}, u32[]{:S(2)}, u32[]{:S(2)}) collective-permute-start(f32[10,2,384]{2,1,0:T(2,128)S(1)} %get-tuple-element.41), channel_id=1, source_target_pairs={{0,8},{8,16},{16,24},{24,0},{1,9},{9,17},{17,25},{25,1},{2,10},{10... | collective-permute-start | bytes 92168 | tf_op jit(solution)/shard_map/ppermute | solution.py:721
  30.2 14.5 %copy-start.1 = (f32[20,10,384]{2,0,1:T(8,128)S(1)}, f32[20,10,384]{2,0,1:T(8,128)}, u32[]{:S(2)}) copy-start(f32[20,10,384]{2,0,1:T(8,128)} %param.7) | copy-start | bytes 921604
  30.3 14.5 %copy-start.2 = (bf16[384,512]{1,0:T(8,128)(2,1)S(1)}, bf16[384,512]{1,0:T(8,128)(2,1)}, u32[]{:S(2)}) copy-start(bf16[384,512]{1,0:T(8,128)(2,1)} %constant.24.clone.refs_2_) | copy-start | bytes 1179652
  30.3 14.5 %copy-start.3 = (bf16[384,512]{1,0:T(8,128)(2,1)S(1)}, bf16[384,512]{1,0:T(8,128)(2,1)}, u32[]{:S(2)}) copy-start(bf16[384,512]{1,0:T(8,128)(2,1)} %constant.23.clone.refs_1_) | copy-start | bytes 1179652

commit v4 on v3

--- a/solution.py
+++ b/solution.py
@@ -236,6 +236,8 @@
     def fits(self):
         return (
             self.even
+            and self.gx % 2 == 0
+            and self.gl % 2 == 0
             and self.nz % (self.ng * 8) == 0
             and self.nz % LANES == 0
             and self.yq == 2 * HALO - 1
@@ -679,11 +681,13 @@
     def shape(*dims):
         return jax.ShapeDtypeStruct(dims, f32)
 
-    def ring(count):
-        return [(i, (i + 1) % count) for i in range(count)]
-
-    def back(pairs):
-        return [(target, source) for source, target in pairs]
+    def pairs(count, first):
+        low = range(first, count, 2)
+        near = [(i, (i + 1) % count) for i in low]
+        return near + [(target, source) for source, target in near]
+
+    even_x = lax.axis_index("gx") % 2 == 0
+    even_y = lax.axis_index("gl") % 2 == 0
 
     density = density.transpose(1, 0, 2)
     charge = charge.transpose(1, 0, 2)
@@ -707,6 +711,18 @@
         lambda *refs: table_kernel(p, *refs), [shape(p.ny, p.kz * LANES)], [fine]
     )
     eps = permittivity(density)
+    swap_by = lax.ppermute(
+        jnp.where(even_y, eps[:2], eps[p.cy - 2 :]), along_y, pairs(2 * p.gl, 1)
+    )
+    swap_bx = lax.ppermute(
+        jnp.where(even_x, eps[:, :2], eps[:, p.cx - 2 :]), "gx", pairs(p.gx, 1)
+    )
+    swap_ay = lax.ppermute(
+        jnp.where(even_y, eps[p.cy - 2 :], eps[:2]), along_y, pairs(2 * p.gl, 0)
+    )
+    swap_ax = lax.ppermute(
+        jnp.where(even_x, eps[:, p.cx - 2 :], eps[:, :2]), "gx", pairs(p.gx, 0)
+    )
     blocks, eps, table = lax.optimization_barrier(
         (blocks, eps, table)
     )
@@ -718,12 +734,10 @@
     )
     sent, eps = lax.optimization_barrier((sent, eps))
     received = lax.ppermute(sent, "gh", [(0, 1), (1, 0)])
-    ex_low = lax.ppermute(eps[:, p.cx - 2 :], "gx", ring(p.gx))
-    ex_high = lax.ppermute(eps[:, :2], "gx", back(ring(p.gx)))
-    ey_low = lax.ppermute(eps[p.cy - 2 :], along_y, ring(2 * p.gl))
-    ey_high = lax.ppermute(eps[:2], along_y, back(ring(2 * p.gl)))
-    received, ex_low, ex_high, ey_low, ey_high = lax.optimization_barrier(
-        (received, ex_low, ex_high, ey_low, ey_high)
+    ex_low, ex_high = jnp.where(even_x, swap_bx, swap_ax), jnp.where(even_x, swap_ax, swap_bx)
+    ey_low, ey_high = jnp.where(even_y, swap_by, swap_ay), jnp.where(even_y, swap_ay, swap_by)
+    received, eps, ex_low, ex_high, ey_low, ey_high = lax.optimization_barrier(
+        (received, eps, ex_low, ex_high, ey_low, ey_high)
     )
     (blocks,) = call(
         lambda *refs: return_kernel(p, *refs),

time: 57.8 us -> 55 us (0.952)
  waiting for transfers between devices: 11.3 us -> 3.46 us
  starting transfers between devices: 11.7 us -> 15 us
  blocking collectives: 23.3 us -> 24.9 us
    all_to_all x1, waiting for transfers between devices: 6.13 us -> 0.01 us  [local_planes(): blocks = lax.all_to_all(blocks, group, 0, 0)]
    ppermute x4, starting transfers between devices: 2.63 us -> 7.1 us  [the longest x1 3.48 us: local_planes(): lax.ppermute(jnp.where(even_y, eps[:2], eps[p.cy - 2:]), along_y, pairs(2...]
    ppermute x4, waiting for transfers between devices: 5.17 us -> 0.97 us  [the longest x1 0.97 us: local_planes(): lax.ppermute(jnp.where(even_y, eps[:2], eps[p.cy - 2:]), along_y, pairs(2...]
    ppermute x1, waiting for transfers between devices: 0.01 us -> 2.49 us  [local_planes(): received = lax.ppermute(sent, 'gh', [(0, 1), (1, 0)])]
    all_to_all x1, blocking collectives: 8.81 us -> 10.4 us  [local_planes(): sums = lax.all_to_all(sums, ('gx', 'gh', 'gl'), 0, 0)]
    ppermute x1, starting transfers between devices: 2.61 us -> 1.58 us  [local_planes(): received = lax.ppermute(sent, 'gh', [(0, 1), (1, 0)])]
  transfers between devices with their start and end apart: 6 -> 6, of which waited for: 4 -> 2; matrix products, arithmetic and copies ran while one was open for 2% -> 3% of each run, Pallas kernels for 0% -> 2%
where the time goes in v4:
time: 55 us; the launch traced here: 54.7 us
  blocking collectives  24.9 us (45%)
  starting transfers between devices  15 us (27%)
  Pallas kernels  9.13 us (17%)
  waiting for transfers between devices  3.46 us (6%)
  other arithmetic  1.4 us (3%)
  between operations  0.8 us (1%)
    all_to_all x1, blocking collectives, local_planes(): blocks = lax.all_to_all(blocks, group, 0, 0)  14.4 us
    all_to_all x1, blocking collectives, local_planes(): sums = lax.all_to_all(sums, ('gx', 'gh', 'gl'), 0, 0)  10.4 us
    pallas_call x6, Pallas kernels, call(): pl.pallas_call(kernel, out_shape=tuple(outs), in_specs=specs or [VMEM_SPE...  9.13 us
    all_to_all x1, starting transfers between devices, local_planes(): blocks = lax.all_to_all(blocks, group, 0, 0)  6.31 us
    ppermute x1, starting transfers between devices, local_planes(): lax.ppermute(jnp.where(even_y, eps[:2], eps[p.cy - 2:]), along_y, pairs(2...  3.48 us
    ppermute x1, waiting for transfers between devices, local_planes(): received = lax.ppermute(sent, 'gh', [(0, 1), (1, 0)])  2.49 us
    ppermute x1, starting transfers between devices, local_planes(): lax.ppermute(jnp.where(even_x, eps[:, :2], eps[:, p.cx - 2:]), 'gx', pair...  1.63 us
    ppermute x1, starting transfers between devices, local_planes(): received = lax.ppermute(sent, 'gh', [(0, 1), (1, 0)])  1.58 us
  transfers between devices with their start and end apart: 6, of which 2 were waited for; matrix products, arithmetic and copies ran while one was open for 3% of the time, Pallas kernels for 2%

profile of v4, /device:TPU:0, one launch (start us, length us, event | category | flops | bytes accessed | tf_op | source)
XLA Modules:
  0.0 54.7 jit_solution(6876555487682679138)
XLA Ops:
  0.6 0.0 copy-start.5
  0.6 0.0 copy-start
  0.7 3.0 %shard_map.77 = f32[16,40,128]{2,1,0:T(8,128)} custom-call(f32[10,20,384]{2,1,0:T(8,128)} %bitcast.16, bf16[384,512]{1,0:T(8,128)(2,1)} %constant.48.clone.refs_1_, bf16[384,512]{1,0:T(8,128)(2,1)} %constant.49.clone.refs_2_), custom_call_target="tpu_custom_call" | custom-call | bytes 1421312 | tf_op jit(solution)/shard_map/pallas_call | solution.py:364
  3.6 6.3 %all-to-all-start = ((f32[16,40,128]{2,1,0:T(8,128)}), f32[16,40,128]{2,1,0:T(8,128)S(1)}, u32[]{:S(2)}, u32[]{:S(2)}) async-start(f32[16,40,128]{2,1,0:T(8,128)} %shard_map.77), calls=%async_computation | async-start | bytes 655360 | tf_op jit(solution)/shard_map/all_to_all | solution.py:709
  10.0 0.0 copy-done.5
  10.0 0.0 copy-start.4
  10.0 1.3 %fusion.3.refs_4_ = f32[10,20,384]{2,1,0:T(8,128)S(1)} fusion(f32[20,10,384]{2,0,1:T(8,128)S(1)} %copy-done.5), kind=kLoop, calls=%fused_computation.5 | loop fusion | flops 537600 | bytes 614400 | tf_op jit(solution)/shard_map/exp | solution.py:43
  11.4 0.5 collective-permute-start.2
  11.8 1.6 %collective-permute-start.1 = (f32[10,2,384]{2,1,0:T(2,128)S(1)}, f32[10,2,384]{2,1,0:T(2,128)S(1)}, u32[]{:S(2)}, u32[]{:S(2)}) collective-permute-start(f32[10,2,384]{2,1,0:T(2,128)S(1)} %get-tuple-element.43), channel_id=1, source_target_pairs={{8,16},{24,0},{16,8},{0,24},{9,17},{25,1},{17,9},{1,25},{10,18},{2... | collective-permute-start | bytes 92168 | tf_op jit(solution)/shard_map/ppermute | solution.py:717
  13.5 1.5 %collective-permute-start.4 = (f32[2,20,384]{2,1,0:T(8,128)S(1)}, f32[2,20,384]{2,1,0:T(8,128)S(1)}, u32[]{:S(2)}, u32[]{:S(2)}) collective-permute-start(f32[2,20,384]{2,1,0:T(8,128)S(1)} %get-tuple-element.40), channel_id=1, source_target_pairs={{0,1},{2,3},{4,5},{6,7},{1,0},{3,2},{5,4},{7,6},{8,9},{10,11},{12,... | collective-permute-start | bytes 184328 | tf_op jit(solution)/shard_map/ppermute | solution.py:720
  15.0 3.5 %collective-permute-start.3 = (f32[2,20,384]{2,1,0:T(8,128)S(1)}, f32[2,20,384]{2,1,0:T(8,128)S(1)}, u32[]{:S(2)}, u32[]{:S(2)}) collective-permute-start(f32[2,20,384]{2,1,0:T(8,128)S(1)} %get-tuple-element.41), channel_id=1, source_target_pairs={{1,2},{3,4},{5,6},{7,0},{2,1},{4,3},{6,5},{0,7},{9,10},{11,12},{13... | collective-permute-start | bytes 184328 | tf_op jit(solution)/shard_map/ppermute | solution.py:714
  18.5 0.0 copy-done
  18.5 0.1 shard_map.78.refs_2_.refs_3_
  18.6 0.0 collective-permute-done.2
  18.6 0.0 collective-permute-done.1
  18.6 0.0 all-to-all-done.refs_0_
  18.6 0.0 copy-done.4
  18.6 0.8 %shard_map.79 = (f32[40,3072]{1,0:T(8,128)S(1)}, f32[144,128]{1,0:T(8,128)S(1)}, f32[96,128]{1,0:T(8,128)S(1)}) custom-call(f32[16,40,128]{2,1,0:T(8,128)S(1)} %all-to-all-done.refs_0_, bf16[416,384]{1,0:T(8,128)(2,1)S(1)} %copy-done.4, f32[40,3072]{1,0:T(8,128)S(1)} %shard_map.78.refs_2_.refs_3_), custom_call_target="tpu_custom_call" | custom-call | bytes 1753088 | tf_op jit(solution)/shard_map/pallas_call | solution.py:364
  19.5 1.6 %collective-permute-start = (f32[96,128]{1,0:T(8,128)S(1)}, f32[96,128]{1,0:T(8,128)S(1)}, u32[]{:S(2)}, u32[]{:S(2)}) collective-permute-start(f32[96,128]{1,0:T(8,128)S(1)} %get-tuple-element.27), channel_id=1, source_target_pairs={{0,4},{4,0},{1,5},{5,1},{2,6},{6,2},{3,7},{7,3},{8,12},{12,8},{9,1... | collective-permute-start | bytes 147464 | tf_op jit(solution)/shard_map/ppermute | solution.py:736
  21.1 0.0 collective-permute-done.4
  21.1 1.0 %collective-permute-done.3 = f32[2,20,384]{2,1,0:T(8,128)S(1)} collective-permute-done((f32[2,20,384]{2,1,0:T(8,128)S(1)}, f32[2,20,384]{2,1,0:T(8,128)S(1)}, u32[]{:S(2)}, u32[]{:S(2)}) %collective-permute-start.3) | collective-permute-done | bytes 61472 | tf_op jit(solution)/shard_map/ppermute | solution.py:714
  22.1 2.5 %collective-permute-done.refs_2_ = f32[96,128]{1,0:T(8,128)S(1)} collective-permute-done((f32[96,128]{1,0:T(8,128)S(1)}, f32[96,128]{1,0:T(8,128)S(1)}, u32[]{:S(2)}, u32[]{:S(2)}) %collective-permute-start) | collective-permute-done | bytes 49184 | tf_op jit(solution)/shard_map/ppermute | solution.py:736
  24.5 1.3 %shard_map.80 = f32[16,80,128]{2,1,0:T(8,128)S(1)} custom-call(f32[40,3072]{1,0:T(8,128)S(1)} %get-tuple-element.23.refs_0_, f32[144,128]{1,0:T(8,128)S(1)} %get-tuple-element.24.refs_1_, f32[96,128]{1,0:T(8,128)S(1)} %collective-permute-done.refs_2_, f32[40,3072]{1,0:T(8,128)S(1)} %shard_map.78.refs_2_.refs_3_, f32[2968,128]{1,0:T(8,128)S(1)} %copy-done, ...), custom_call_target="tpu_custom_call" | custom-call | bytes 3600384 | tf_op jit(solution)/shard_map/pallas_call | solution.py:364
  25.8 0.0 copy-start.1
  25.8 0.0 copy-start.2
  25.8 0.0 copy-start.3
  25.8 14.4 %all_to_all.15.refs_0_ = f32[16,80,128]{2,1,0:T(8,128)S(1)} all-to-all(f32[16,80,128]{2,1,0:T(8,128)S(1)} %shard_map.80), channel_id=1, replica_groups=mesh['gx'=4,'gh'=2,'gl'=4] {'gx','gl'}, dimensions={0} | all-to-all | bytes 1310720 | tf_op jit(solution)/shard_map/all_to_all | solution.py:753
  40.3 0.0 copy-done.1
  40.3 0.0 copy-done.2
  40.3 0.0 copy-done.3
  40.3 2.9 %shard_map.81 = (f32[10,20,384]{2,1,0:T(8,128)S(1)}, f32[10,20,384]{2,1,0:T(8,128)S(1)}, f32[32,1,128]{2,1,0:T(1,128)S(1)}) custom-call(f32[16,80,128]{2,1,0:T(8,128)S(1)} %all_to_all.15.refs_0_, bf16[384,512]{1,0:T(8,128)(2,1)S(1)} %copy-done.3, bf16[384,512]{1,0:T(8,128)(2,1)S(1)} %copy-done.2, f32[10,20,384]{2,1,0:T(8,128)S(1)} %bitcast.17, ...), custom_call_target="tpu_custom_call" | custom-call | bytes 2871296 | tf_op jit(solution)/shard_map/pallas_call | solution.py:364
  43.2 10.4 %all_to_all.16.refs_0_ = f32[32,1,128]{2,1,0:T(1,128)S(1)} all-to-all(f32[32,1,128]{2,1,0:T(1,128)S(1)} %get-tuple-element.35), channel_id=1, replica_groups=mesh['gx'=4,'gh'=2,'gl'=4] {'gx','gh','gl'}, dimensions={0} | all-to-all | bytes 32768 | tf_op jit(solution)/shard_map/all_to_all | solution.py:767
  53.6 1.0 %shard_map.82 = (f32[10,20,384]{2,1,0:T(8,128)}, f32[10,20,384]{2,1,0:T(8,128)}) custom-call(f32[32,1,128]{2,1,0:T(1,128)S(1)} %all_to_all.16.refs_0_, f32[10,20,384]{2,1,0:T(8,128)S(1)} %bitcast.18, f32[10,20,384]{2,1,0:T(8,128)S(1)} %get-tuple-element.36.refs_2_, f32[10,20,384]{2,1,0:T(8,128)S(1)} %get-tuple-element.37.refs_3_), custom_call_target="tpu_custom_call" | custom-call | bytes 1552384 | tf_op jit(solution)/shard_map/pallas_call | solution.py:364
  (4 shorter events, 0.1 us)
Async XLA Ops:
  0.6 9.3 %copy-start.5 = (f32[20,10,384]{2,0,1:T(8,128)S(1)}, f32[20,10,384]{2,0,1:T(8,128)}, u32[]{:S(2)}) copy-start(f32[20,10,384]{2,0,1:T(8,128)} %param.6) | copy-start | bytes 921604
  0.6 17.8 %copy-start = (f32[2968,128]{1,0:T(8,128)S(1)}, f32[2968,128]{1,0:T(8,128)}, u32[]{:S(2)}) copy-start(f32[2968,128]{1,0:T(8,128)} %constant.51.clone.refs_0_.refs_4_) | copy-start | bytes 4558852
  3.6 15.0 %all-to-all-start = ((f32[16,40,128]{2,1,0:T(8,128)}), f32[16,40,128]{2,1,0:T(8,128)S(1)}, u32[]{:S(2)}, u32[]{:S(2)}) async-start(f32[16,40,128]{2,1,0:T(8,128)} %shard_map.77), calls=%async_computation | async-start | bytes 655360 | tf_op jit(solution)/shard_map/all_to_all | solution.py:709
  10.0 8.7 %copy-start.4 = (bf16[416,384]{1,0:T(8,128)(2,1)S(1)}, bf16[416,384]{1,0:T(8,128)(2,1)}, u32[]{:S(2)}) copy-start(bf16[416,384]{1,0:T(8,128)(2,1)} %constant.50.clone.refs_1_.refs_5_) | copy-start | bytes 958468
  11.4 7.2 %collective-permute-start.2 = (f32[10,2,384]{2,1,0:T(2,128)S(1)}, f32[10,2,384]{2,1,0:T(2,128)S(1)}, u32[]{:S(2)}, u32[]{:S(2)}) collective-permute-start(f32[10,2,384]{2,1,0:T(2,128)S(1)} %get-tuple-element.42), channel_id=1, source_target_pairs={{0,8},{16,24},{8,0},{24,16},{1,9},{17,25},{9,1},{25,17},{2,10},{18... | collective-permute-start | bytes 92168 | tf_op jit(solution)/shard_map/ppermute | solution.py:723
  11.8 6.8 %collective-permute-start.1 = (f32[10,2,384]{2,1,0:T(2,128)S(1)}, f32[10,2,384]{2,1,0:T(2,128)S(1)}, u32[]{:S(2)}, u32[]{:S(2)}) collective-permute-start(f32[10,2,384]{2,1,0:T(2,128)S(1)} %get-tuple-element.43), channel_id=1, source_target_pairs={{8,16},{24,0},{16,8},{0,24},{9,17},{25,1},{17,9},{1,25},{10,18},{2... | collective-permute-start | bytes 92168 | tf_op jit(solution)/shard_map/ppermute | solution.py:717
  13.5 7.6 %collective-permute-start.4 = (f32[2,20,384]{2,1,0:T(8,128)S(1)}, f32[2,20,384]{2,1,0:T(8,128)S(1)}, u32[]{:S(2)}, u32[]{:S(2)}) collective-permute-start(f32[2,20,384]{2,1,0:T(8,128)S(1)} %get-tuple-element.40), channel_id=1, source_target_pairs={{0,1},{2,3},{4,5},{6,7},{1,0},{3,2},{5,4},{7,6},{8,9},{10,11},{12,... | collective-permute-start | bytes 184328 | tf_op jit(solution)/shard_map/ppermute | solution.py:720
  15.0 7.0 %collective-permute-start.3 = (f32[2,20,384]{2,1,0:T(8,128)S(1)}, f32[2,20,384]{2,1,0:T(8,128)S(1)}, u32[]{:S(2)}, u32[]{:S(2)}) collective-permute-start(f32[2,20,384]{2,1,0:T(8,128)S(1)} %get-tuple-element.41), channel_id=1, source_target_pairs={{1,2},{3,4},{5,6},{7,0},{2,1},{4,3},{6,5},{0,7},{9,10},{11,12},{13... | collective-permute-start | bytes 184328 | tf_op jit(solution)/shard_map/ppermute | solution.py:714
  19.5 5.1 %collective-permute-start = (f32[96,128]{1,0:T(8,128)S(1)}, f32[96,128]{1,0:T(8,128)S(1)}, u32[]{:S(2)}, u32[]{:S(2)}) collective-permute-start(f32[96,128]{1,0:T(8,128)S(1)} %get-tuple-element.27), channel_id=1, source_target_pairs={{0,4},{4,0},{1,5},{5,1},{2,6},{6,2},{3,7},{7,3},{8,12},{12,8},{9,1... | collective-permute-start | bytes 147464 | tf_op jit(solution)/shard_map/ppermute | solution.py:736
  25.8 14.5 %copy-start.1 = (f32[20,10,384]{2,0,1:T(8,128)S(1)}, f32[20,10,384]{2,0,1:T(8,128)}, u32[]{:S(2)}) copy-start(f32[20,10,384]{2,0,1:T(8,128)} %param.7) | copy-start | bytes 921604
  25.8 14.5 %copy-start.2 = (bf16[384,512]{1,0:T(8,128)(2,1)S(1)}, bf16[384,512]{1,0:T(8,128)(2,1)}, u32[]{:S(2)}) copy-start(bf16[384,512]{1,0:T(8,128)(2,1)} %constant.49.clone.refs_2_) | copy-start | bytes 1179652
  25.8 14.5 %copy-start.3 = (bf16[384,512]{1,0:T(8,128)(2,1)S(1)}, bf16[384,512]{1,0:T(8,128)(2,1)}, u32[]{:S(2)}) copy-start(bf16[384,512]{1,0:T(8,128)(2,1)} %constant.48.clone.refs_1_) | copy-start | bytes 1179652

commit v5 on v4

--- a/solution.py
+++ b/solution.py
@@ -359,7 +359,7 @@
 ANY_SPEC = pl.BlockSpec(memory_space=pl.ANY)
 
 
-def call(kernel, outs, args, scratch=(), specs=None, limit=VMEM_LIMIT, flops=0):
+def call(kernel, outs, args, scratch=(), specs=None, limit=VMEM_LIMIT):
     nbytes = sum(int(np.prod(a.shape)) * a.dtype.itemsize for a in (*args, *outs))
     return pl.pallas_call(
         kernel,
@@ -368,7 +368,7 @@
         out_specs=tuple([VMEM_SPEC] * len(outs)),
         scratch_shapes=list(scratch),
         compiler_params=pltpu.CompilerParams(vmem_limit_bytes=limit),
-        cost_estimate=pl.CostEstimate(flops=flops, bytes_accessed=nbytes, transcendentals=0),
+        cost_estimate=pl.CostEstimate(flops=0, bytes_accessed=nbytes, transcendentals=0),
     )(*args)
 
 
@@ -559,9 +559,21 @@
                 out[target, at + p.extra :] = jnp.zeros((rest, LANES), jnp.float32)
 
 
+def faces_kernel(p, eps, ex_low, ex_high, ey_low, ey_high, faces_x, faces_y, faces_z, mass):
+    for y in range(p.cy):
+        here = eps[y]
+        line = jnp.concatenate([ex_low[y], here, ex_high[y]], axis=0)
+        faces_x[y, : p.cx + 3] = line[: p.cx + 3] + line[1 : p.cx + 4]
+        faces_z[y] = here + pltpu.roll(here, p.nz - 1, 1)
+        mass[y] = (KAPPA_SCALE / (EPS_SOLVENT - 1.0)) * (here - 1.0)
+    planes = [ey_low[0], ey_low[1], *[eps[y] for y in range(p.cy)], ey_high[0], ey_high[1]]
+    for y in range(p.cy + 3):
+        faces_y[y] = planes[y] + planes[y + 1]
+
+
 def stencil_kernel(
-    p, blocks, high_z, low_z, charge, eps, ex_low, ex_high, ey_low, ey_high,
-    pre, image, sums, lines, field, eps_x, eps_y,
+    p, blocks, high_z, low_z, charge, faces_x, faces_y, faces_z, mass,
+    pre, image, sums, lines, field,
 ):
     lane = lane_index(p.xw)
     windows, at = [], 0
@@ -604,47 +616,35 @@
         field[p.cy + 2 * HALO - 1, HALO + q * p.extra : HALO + (q + 1) * p.extra] = whole[
             at + off : at + off + p.extra
         ]
-    eps_x[:, 0:2, :] = ex_low[...]
-    eps_x[:, 2 : 2 + p.cx, :] = eps[...]
-    eps_x[:, 2 + p.cx : 4 + p.cx, :] = ex_high[...]
-    eps_y[0:2] = ey_low[...]
-    eps_y[2 : 2 + p.cy] = eps[...]
-    eps_y[2 + p.cy : 4 + p.cy] = ey_high[...]
-
     def stretch(flux_at):
         return 27.0 * (flux_at(2) - flux_at(1)) - (flux_at(3) - flux_at(0))
 
     rz = jnp.zeros((p.cx, LANES), jnp.float32)
     dot = jnp.zeros((p.cx, LANES), jnp.float32)
-    faces_y = {}
-
-    def face_y(y):
-        if y not in faces_y:
+    fluxes_y = {}
+
+    def flux_y(y):
+        if y not in fluxes_y:
             val = [field[y + i, HALO : HALO + p.cx, :] for i in range(4)]
-            grad = 27.0 * (val[2] - val[1]) - (val[3] - val[0])
-            faces_y[y] = (eps_y[y] + eps_y[y + 1]) * grad
-        return faces_y[y]
-
+            fluxes_y[y] = faces_y[y] * stretch(lambda i: val[i])
+        return fluxes_y[y]
+
+    n = p.nz
     for y in range(p.cy):
         line = field[HALO + y]
-        val = [line[i : i + p.cx + 3] for i in range(4)]
-        grad = 27.0 * (val[2] - val[1]) - (val[3] - val[0])
-        eps_line = eps_x[y]
-        flux = (eps_line[0 : p.cx + 3] + eps_line[1 : p.cx + 4]) * grad
+        flux = faces_x[y, : p.cx + 3] * stretch(lambda i: line[i : i + p.cx + 3])
         term = stretch(lambda i: flux[i : i + p.cx])
-        term = term + stretch(lambda i: face_y(y + i))
+        term = term + stretch(lambda i: flux_y(y + i))
         here = line[HALO : HALO + p.cx]
-        eps_here = eps[y]
-        n = p.nz
         grad = 27.0 * (pltpu.roll(here, n - 1, 1) - here) - (
             pltpu.roll(here, n - 2, 1) - pltpu.roll(here, 1, 1)
         )
-        flux = (eps_here + pltpu.roll(eps_here, n - 1, 1)) * grad
+        flux = faces_z[y] * grad
         term = term + (
             27.0 * (flux - pltpu.roll(flux, 1, 1))
             - (pltpu.roll(flux, n - 1, 1) - pltpu.roll(flux, 2, 1))
         )
-        result = (KAPPA_SCALE / (EPS_SOLVENT - 1.0)) * (eps_here - 1.0) * here - term * (0.5 / 576.0)
+        result = mass[y] * here - term * (0.5 / 576.0)
         pre[y] = here
         image[y] = result
         one = charge[y] * here
@@ -736,9 +736,15 @@
     received = lax.ppermute(sent, "gh", [(0, 1), (1, 0)])
     ex_low, ex_high = jnp.where(even_x, swap_bx, swap_ax), jnp.where(even_x, swap_ax, swap_bx)
     ey_low, ey_high = jnp.where(even_y, swap_by, swap_ay), jnp.where(even_y, swap_ay, swap_by)
-    received, eps, ex_low, ex_high, ey_low, ey_high = lax.optimization_barrier(
-        (received, eps, ex_low, ex_high, ey_low, ey_high)
-    )
+    brick = (p.cy, p.cx, p.nz)
+    faces = call(
+        lambda *refs: faces_kernel(p, *refs),
+        [
+            shape(p.cy, p.xp, p.nz), shape(p.cy + 3, p.cx, p.nz), shape(*brick), shape(*brick),
+        ],
+        [eps, ex_low, ex_high, ey_low, ey_high],
+    )
+    received, *faces = lax.optimization_barrier((received, *faces))
     (blocks,) = call(
         lambda *refs: return_kernel(p, *refs),
         [shape(p.ng, p.rows, LANES)],
@@ -753,21 +759,17 @@
     blocks = lax.all_to_all(blocks, group, 0, 0)
     pre, image, sums = call(
         lambda *refs: stencil_kernel(p, *refs),
-        [shape(p.cy, p.cx, p.nz), shape(p.cy, p.cx, p.nz), shape(2 * p.ng, 1, LANES)],
-        [
-            blocks, high_z, low_z, charge, eps, ex_low, ex_high, ey_low, ey_high,
-        ],
+        [shape(*brick), shape(*brick), shape(2 * p.ng, 1, LANES)],
+        [blocks, high_z, low_z, charge, *faces],
         [
             pltpu.VMEM((p.lines, p.deep), f32),
             pltpu.VMEM((p.cy + 2 * HALO, p.xw, p.nz), f32),
-            pltpu.VMEM((p.cy, p.cx + 4, p.nz), f32),
-            pltpu.VMEM((p.cy + 4, p.cx, p.nz), f32),
         ],
     )
     sums = lax.all_to_all(sums, ("gx", "gh", "gl"), 0, 0)
     solution_field, residual = call(
         lambda *refs: update_kernel(p, *refs),
-        [shape(p.cy, p.cx, p.nz), shape(p.cy, p.cx, p.nz)],
+        [shape(*brick), shape(*brick)],
         [sums, charge, pre, image],
     )
     return solution_field.transpose(1, 0, 2), residual.transpose(1, 0, 2)

time: 55 us -> 54.8 us (level)
    pallas_call x6 -> x7, Pallas kernels: 9.13 us -> 9.11 us  [call(): pl.pallas_call(kernel, out_shape=tuple(outs), in_specs=specs or [VMEM_SPE...]
where the time goes in v5:
time: 54.8 us; the launch traced here: 54.5 us
  blocking collectives  24.9 us (45%)
  starting transfers between devices  15 us (27%)
  Pallas kernels  9.11 us (17%)
  waiting for transfers between devices  3.27 us (6%)
  other arithmetic  1.4 us (3%)
  between operations  0.8 us (1%)
    all_to_all x1, blocking collectives, local_planes(): blocks = lax.all_to_all(blocks, group, 0, 0)  14.4 us
    all_to_all x1, blocking collectives, local_planes(): sums = lax.all_to_all(sums, ('gx', 'gh', 'gl'), 0, 0)  10.4 us
    pallas_call x7, Pallas kernels, call(): pl.pallas_call(kernel, out_shape=tuple(outs), in_specs=specs or [VMEM_SPE...  9.11 us
    all_to_all x1, starting transfers between devices, local_planes(): blocks = lax.all_to_all(blocks, group, 0, 0)  6.31 us
    ppermute x1, starting transfers between devices, local_planes(): lax.ppermute(jnp.where(even_y, eps[:2], eps[p.cy - 2:]), along_y, pairs(2...  3.48 us
    ppermute x1, waiting for transfers between devices, local_planes(): received = lax.ppermute(sent, 'gh', [(0, 1), (1, 0)])  2.3 us
    ppermute x1, starting transfers between devices, local_planes(): lax.ppermute(jnp.where(even_x, eps[:, :2], eps[:, p.cx - 2:]), 'gx', pair...  1.63 us
    ppermute x1, starting transfers between devices, local_planes(): received = lax.ppermute(sent, 'gh', [(0, 1), (1, 0)])  1.59 us
  transfers between devices with their start and end apart: 6, of which 2 were waited for; matrix products, arithmetic and copies ran while one was open for 3% of the time, Pallas kernels for 2%

profile of v5, /device:TPU:0, one launch (start us, length us, event | category | flops | bytes accessed | tf_op | source)
XLA Modules:
  0.0 54.5 jit_solution(9505967588895501741)
XLA Ops:
  0.6 0.0 copy-start.5
  0.6 0.0 copy-start
  0.7 3.0 %shard_map.77 = f32[16,40,128]{2,1,0:T(8,128)} custom-call(f32[10,20,384]{2,1,0:T(8,128)} %bitcast.16, bf16[384,512]{1,0:T(8,128)(2,1)} %constant.48.clone.refs_1_, bf16[384,512]{1,0:T(8,128)(2,1)} %constant.49.clone.refs_2_), custom_call_target="tpu_custom_call" | custom-call | bytes 1421312 | tf_op jit(solution)/shard_map/pallas_call | solution.py:364
  3.6 6.3 %all-to-all-start = ((f32[16,40,128]{2,1,0:T(8,128)}), f32[16,40,128]{2,1,0:T(8,128)S(1)}, u32[]{:S(2)}, u32[]{:S(2)}) async-start(f32[16,40,128]{2,1,0:T(8,128)} %shard_map.77), calls=%async_computation | async-start | bytes 655360 | tf_op jit(solution)/shard_map/all_to_all | solution.py:709
  10.0 0.0 copy-done.5
  10.0 0.0 copy-start.4
  10.0 1.3 %fusion.3.refs_0_ = f32[10,20,384]{2,1,0:T(8,128)S(1)} fusion(f32[20,10,384]{2,0,1:T(8,128)S(1)} %copy-done.5), kind=kLoop, calls=%fused_computation.5 | loop fusion | flops 537600 | bytes 614400 | tf_op jit(solution)/shard_map/exp | solution.py:43
  11.4 0.5 collective-permute-start.2
  11.8 1.6 %collective-permute-start.1 = (f32[10,2,384]{2,1,0:T(2,128)S(1)}, f32[10,2,384]{2,1,0:T(2,128)S(1)}, u32[]{:S(2)}, u32[]{:S(2)}) collective-permute-start(f32[10,2,384]{2,1,0:T(2,128)S(1)} %get-tuple-element.49), channel_id=1, source_target_pairs={{8,16},{24,0},{16,8},{0,24},{9,17},{25,1},{17,9},{1,25},{10,18},{2... | collective-permute-start | bytes 92168 | tf_op jit(solution)/shard_map/ppermute | solution.py:717
  13.5 1.5 %collective-permute-start.4 = (f32[2,20,384]{2,1,0:T(8,128)S(1)}, f32[2,20,384]{2,1,0:T(8,128)S(1)}, u32[]{:S(2)}, u32[]{:S(2)}) collective-permute-start(f32[2,20,384]{2,1,0:T(8,128)S(1)} %get-tuple-element.46), channel_id=1, source_target_pairs={{0,1},{2,3},{4,5},{6,7},{1,0},{3,2},{5,4},{7,6},{8,9},{10,11},{12,... | collective-permute-start | bytes 184328 | tf_op jit(solution)/shard_map/ppermute | solution.py:720
  15.0 3.5 %collective-permute-start.3 = (f32[2,20,384]{2,1,0:T(8,128)S(1)}, f32[2,20,384]{2,1,0:T(8,128)S(1)}, u32[]{:S(2)}, u32[]{:S(2)}) collective-permute-start(f32[2,20,384]{2,1,0:T(8,128)S(1)} %get-tuple-element.47), channel_id=1, source_target_pairs={{1,2},{3,4},{5,6},{7,0},{2,1},{4,3},{6,5},{0,7},{9,10},{11,12},{13... | collective-permute-start | bytes 184328 | tf_op jit(solution)/shard_map/ppermute | solution.py:714
  18.5 0.0 copy-done
  18.5 0.1 shard_map.78.refs_2_.refs_3_
  18.6 0.0 collective-permute-done.2
  18.6 0.0 collective-permute-done.1
  18.6 0.0 all-to-all-done.refs_0_
  18.6 0.0 copy-done.4
  18.6 0.8 %shard_map.79 = (f32[40,3072]{1,0:T(8,128)S(1)}, f32[144,128]{1,0:T(8,128)S(1)}, f32[96,128]{1,0:T(8,128)S(1)}) custom-call(f32[16,40,128]{2,1,0:T(8,128)S(1)} %all-to-all-done.refs_0_, bf16[416,384]{1,0:T(8,128)(2,1)S(1)} %copy-done.4, f32[40,3072]{1,0:T(8,128)S(1)} %shard_map.78.refs_2_.refs_3_), custom_call_target="tpu_custom_call" | custom-call | bytes 1753088 | tf_op jit(solution)/shard_map/pallas_call | solution.py:364
  19.5 1.6 %collective-permute-start = (f32[96,128]{1,0:T(8,128)S(1)}, f32[96,128]{1,0:T(8,128)S(1)}, u32[]{:S(2)}, u32[]{:S(2)}) collective-permute-start(f32[96,128]{1,0:T(8,128)S(1)} %get-tuple-element.30), channel_id=1, source_target_pairs={{0,4},{4,0},{1,5},{5,1},{2,6},{6,2},{3,7},{7,3},{8,12},{12,8},{9,1... | collective-permute-start | bytes 147464 | tf_op jit(solution)/shard_map/ppermute | solution.py:736
  21.1 0.0 collective-permute-done.4
  21.1 1.0 %collective-permute-done.3 = f32[2,20,384]{2,1,0:T(8,128)S(1)} collective-permute-done((f32[2,20,384]{2,1,0:T(8,128)S(1)}, f32[2,20,384]{2,1,0:T(8,128)S(1)}, u32[]{:S(2)}, u32[]{:S(2)}) %collective-permute-start.3) | collective-permute-done | bytes 61472 | tf_op jit(solution)/shard_map/ppermute | solution.py:714
  22.1 0.2 shard_map.80
  22.2 2.3 %collective-permute-done.refs_2_ = f32[96,128]{1,0:T(8,128)S(1)} collective-permute-done((f32[96,128]{1,0:T(8,128)S(1)}, f32[96,128]{1,0:T(8,128)S(1)}, u32[]{:S(2)}, u32[]{:S(2)}) %collective-permute-start) | collective-permute-done | bytes 49184 | tf_op jit(solution)/shard_map/ppermute | solution.py:736
  24.5 1.3 %shard_map.81 = f32[16,80,128]{2,1,0:T(8,128)S(1)} custom-call(f32[40,3072]{1,0:T(8,128)S(1)} %get-tuple-element.26.refs_0_, f32[144,128]{1,0:T(8,128)S(1)} %get-tuple-element.27.refs_1_, f32[96,128]{1,0:T(8,128)S(1)} %collective-permute-done.refs_2_, f32[40,3072]{1,0:T(8,128)S(1)} %shard_map.78.refs_2_.refs_3_, f32[2968,128]{1,0:T(8,128)S(1)} %copy-done, ...), custom_call_target="tpu_custom_call" | custom-call | bytes 3600384 | tf_op jit(solution)/shard_map/pallas_call | solution.py:364
  25.8 0.0 copy-start.1
  25.8 0.0 copy-start.2
  25.8 0.0 copy-start.3
  25.8 14.4 %all_to_all.15.refs_0_ = f32[16,80,128]{2,1,0:T(8,128)S(1)} all-to-all(f32[16,80,128]{2,1,0:T(8,128)S(1)} %shard_map.81), channel_id=1, replica_groups=mesh['gx'=4,'gh'=2,'gl'=4] {'gx','gl'}, dimensions={0} | all-to-all | bytes 1310720 | tf_op jit(solution)/shard_map/all_to_all | solution.py:759
  40.3 0.0 copy-done.1
  40.3 0.0 copy-done.2
  40.3 0.0 copy-done.3
  40.3 2.7 %shard_map.82 = (f32[10,20,384]{2,1,0:T(8,128)S(1)}, f32[10,20,384]{2,1,0:T(8,128)S(1)}, f32[32,1,128]{2,1,0:T(1,128)S(1)}) custom-call(f32[16,80,128]{2,1,0:T(8,128)S(1)} %all_to_all.15.refs_0_, bf16[384,512]{1,0:T(8,128)(2,1)S(1)} %copy-done.3, bf16[384,512]{1,0:T(8,128)(2,1)S(1)} %copy-done.2, f32[10,20,384]{2,1,0:T(8,128)S(1)} %bitcast.17, ...), custom_call_target="tpu_custom_call" | custom-call | bytes 3762176 | tf_op jit(solution)/shard_map/pallas_call | solution.py:364
  43.0 10.4 %all_to_all.16.refs_0_ = f32[32,1,128]{2,1,0:T(1,128)S(1)} all-to-all(f32[32,1,128]{2,1,0:T(1,128)S(1)} %get-tuple-element.41), channel_id=1, replica_groups=mesh['gx'=4,'gh'=2,'gl'=4] {'gx','gh','gl'}, dimensions={0} | all-to-all | bytes 32768 | tf_op jit(solution)/shard_map/all_to_all | solution.py:769
  53.4 1.1 %shard_map.83 = (f32[10,20,384]{2,1,0:T(8,128)}, f32[10,20,384]{2,1,0:T(8,128)}) custom-call(f32[32,1,128]{2,1,0:T(1,128)S(1)} %all_to_all.16.refs_0_, f32[10,20,384]{2,1,0:T(8,128)S(1)} %bitcast.18, f32[10,20,384]{2,1,0:T(8,128)S(1)} %get-tuple-element.42.refs_2_, f32[10,20,384]{2,1,0:T(8,128)S(1)} %get-tuple-element.43.refs_3_), custom_call_target="tpu_custom_call" | custom-call | bytes 1552384 | tf_op jit(solution)/shard_map/pallas_call | solution.py:364
  (4 shorter events, 0.1 us)
Async XLA Ops:
  0.6 9.3 %copy-start.5 = (f32[20,10,384]{2,0,1:T(8,128)S(1)}, f32[20,10,384]{2,0,1:T(8,128)}, u32[]{:S(2)}) copy-start(f32[20,10,384]{2,0,1:T(8,128)} %param.6) | copy-start | bytes 921604
  0.6 17.8 %copy-start = (f32[2968,128]{1,0:T(8,128)S(1)}, f32[2968,128]{1,0:T(8,128)}, u32[]{:S(2)}) copy-start(f32[2968,128]{1,0:T(8,128)} %constant.51.clone.refs_0_.refs_4_) | copy-start | bytes 4558852
  3.6 15.0 %all-to-all-start = ((f32[16,40,128]{2,1,0:T(8,128)}), f32[16,40,128]{2,1,0:T(8,128)S(1)}, u32[]{:S(2)}, u32[]{:S(2)}) async-start(f32[16,40,128]{2,1,0:T(8,128)} %shard_map.77), calls=%async_computation | async-start | bytes 655360 | tf_op jit(solution)/shard_map/all_to_all | solution.py:709
  10.0 8.7 %copy-start.4 = (bf16[416,384]{1,0:T(8,128)(2,1)S(1)}, bf16[416,384]{1,0:T(8,128)(2,1)}, u32[]{:S(2)}) copy-start(bf16[416,384]{1,0:T(8,128)(2,1)} %constant.50.clone.refs_1_.refs_5_) | copy-start | bytes 958468
  11.4 7.2 %collective-permute-start.2 = (f32[10,2,384]{2,1,0:T(2,128)S(1)}, f32[10,2,384]{2,1,0:T(2,128)S(1)}, u32[]{:S(2)}, u32[]{:S(2)}) collective-permute-start(f32[10,2,384]{2,1,0:T(2,128)S(1)} %get-tuple-element.48), channel_id=1, source_target_pairs={{0,8},{16,24},{8,0},{24,16},{1,9},{17,25},{9,1},{25,17},{2,10},{18... | collective-permute-start | bytes 92168 | tf_op jit(solution)/shard_map/ppermute | solution.py:723
  11.8 6.8 %collective-permute-start.1 = (f32[10,2,384]{2,1,0:T(2,128)S(1)}, f32[10,2,384]{2,1,0:T(2,128)S(1)}, u32[]{:S(2)}, u32[]{:S(2)}) collective-permute-start(f32[10,2,384]{2,1,0:T(2,128)S(1)} %get-tuple-element.49), channel_id=1, source_target_pairs={{8,16},{24,0},{16,8},{0,24},{9,17},{25,1},{17,9},{1,25},{10,18},{2... | collective-permute-start | bytes 92168 | tf_op jit(solution)/shard_map/ppermute | solution.py:717
  13.5 7.6 %collective-permute-start.4 = (f32[2,20,384]{2,1,0:T(8,128)S(1)}, f32[2,20,384]{2,1,0:T(8,128)S(1)}, u32[]{:S(2)}, u32[]{:S(2)}) collective-permute-start(f32[2,20,384]{2,1,0:T(8,128)S(1)} %get-tuple-element.46), channel_id=1, source_target_pairs={{0,1},{2,3},{4,5},{6,7},{1,0},{3,2},{5,4},{7,6},{8,9},{10,11},{12,... | collective-permute-start | bytes 184328 | tf_op jit(solution)/shard_map/ppermute | solution.py:720
  15.0 7.0 %collective-permute-start.3 = (f32[2,20,384]{2,1,0:T(8,128)S(1)}, f32[2,20,384]{2,1,0:T(8,128)S(1)}, u32[]{:S(2)}, u32[]{:S(2)}) collective-permute-start(f32[2,20,384]{2,1,0:T(8,128)S(1)} %get-tuple-element.47), channel_id=1, source_target_pairs={{1,2},{3,4},{5,6},{7,0},{2,1},{4,3},{6,5},{0,7},{9,10},{11,12},{13... | collective-permute-start | bytes 184328 | tf_op jit(solution)/shard_map/ppermute | solution.py:714
  19.5 5.1 %collective-permute-start = (f32[96,128]{1,0:T(8,128)S(1)}, f32[96,128]{1,0:T(8,128)S(1)}, u32[]{:S(2)}, u32[]{:S(2)}) collective-permute-start(f32[96,128]{1,0:T(8,128)S(1)} %get-tuple-element.30), channel_id=1, source_target_pairs={{0,4},{4,0},{1,5},{5,1},{2,6},{6,2},{3,7},{7,3},{8,12},{12,8},{9,1... | collective-permute-start | bytes 147464 | tf_op jit(solution)/shard_map/ppermute | solution.py:736
  25.8 14.5 %copy-start.1 = (f32[20,10,384]{2,0,1:T(8,128)S(1)}, f32[20,10,384]{2,0,1:T(8,128)}, u32[]{:S(2)}) copy-start(f32[20,10,384]{2,0,1:T(8,128)} %param.7) | copy-start | bytes 921604
  25.8 14.5 %copy-start.2 = (bf16[384,512]{1,0:T(8,128)(2,1)S(1)}, bf16[384,512]{1,0:T(8,128)(2,1)}, u32[]{:S(2)}) copy-start(bf16[384,512]{1,0:T(8,128)(2,1)} %constant.49.clone.refs_2_) | copy-start | bytes 1179652
  25.8 14.5 %copy-start.3 = (bf16[384,512]{1,0:T(8,128)(2,1)S(1)}, bf16[384,512]{1,0:T(8,128)(2,1)}, u32[]{:S(2)}) copy-start(bf16[384,512]{1,0:T(8,128)(2,1)} %constant.48.clone.refs_1_) | copy-start | bytes 1179652

commit v6 on v5

--- a/solution.py
+++ b/solution.py
@@ -398,20 +398,23 @@
 def forward_kernel(p, charge_in, high_in, low_in, out, charge, high_z, low_z, sems):
     copies = fetched(((charge_in, charge), (high_in, high_z), (low_in, low_z)), sems)
     copies[0].wait()
-    rows = [padded_rows(charge[y], p.xp) for y in range(p.cy)]
-    high, low = split(jnp.concatenate(rows, axis=0))
-    copies[1].wait()
-    spec = mul(high, high_z[...]) + mul(low, high_z[...])
-    copies[2].wait()
-    spec = spec + mul(high, low_z[...])
     lane = lane_index(p.xp)
-    for target in range(p.ng):
-        chunk, slot = divmod(target, p.group)
-        for part in range(2):
+    ready = False
+    for part in range(2):
+        ys = range(part * p.yq, (part + 1) * p.yq)
+        high, low = split(jnp.concatenate([padded_rows(charge[y], p.xp) for y in ys], axis=0))
+        if not ready:
+            copies[1].wait()
+        spec = mul(high, high_z[...]) + mul(low, high_z[...])
+        if not ready:
+            copies[2].wait()
+            ready = True
+        spec = spec + mul(high, low_z[...])
+        for target in range(p.ng):
+            chunk, slot = divmod(target, p.group)
             block = jnp.zeros((p.xp, LANES), jnp.float32)
             for i in range(p.yq):
-                y = part * p.yq + i
-                piece = spec[y * p.xp : (y + 1) * p.xp, chunk * LANES : (chunk + 1) * LANES]
+                piece = spec[i * p.xp : (i + 1) * p.xp, chunk * LANES : (chunk + 1) * LANES]
                 block = jnp.where(between(lane, i, p.kz), moved(piece, (i - slot) * p.kz), block)
             out[target, part * p.cx : (part + 1) * p.cx] = block[: p.cx]
 
@@ -589,18 +592,29 @@
     for q in range(p.yq):
         windows.append((tail // 8 * 8, 8, q, at))
         at += 8
-    for chunk in range(p.chunks):
-        count = min(p.group, p.ng - chunk * p.group)
-        for first, rows, piece, at in windows:
-            here = lane[:rows]
-            line = jnp.zeros((rows, LANES), jnp.float32)
-            for slot in range(count):
-                part = blocks[chunk * p.group + slot, first : first + rows, :]
-                part = moved(part, (slot - piece) * p.kz)
-                line = jnp.where(between(here, slot, p.kz), part, line)
-            lines[at : at + rows, chunk * LANES : (chunk + 1) * LANES] = line
-    high, low = split(lines[...])
-    whole = mul_t(high, high_z[...]) + mul_t(low, high_z[...]) + mul_t(high, low_z[...])
+    three_z = jnp.concatenate([high_z[...], high_z[...], low_z[...]], axis=1)
+    def assembled(group):
+        parts = []
+        for chunk in range(p.chunks):
+            count = min(p.group, p.ng - chunk * p.group)
+            pieces = []
+            for first, rows, piece, at in group:
+                here = lane[:rows]
+                line = jnp.zeros((rows, LANES), jnp.float32)
+                for slot in range(count):
+                    part = blocks[chunk * p.group + slot, first : first + rows, :]
+                    part = moved(part, (slot - piece) * p.kz)
+                    line = jnp.where(between(here, slot, p.kz), part, line)
+                pieces.append(line)
+            parts.append(jnp.concatenate(pieces, axis=0))
+        return jnp.concatenate(parts, axis=1)
+
+    groups = [windows[p.cy :], windows[: p.yq], windows[p.yq : p.cy]]
+    results = []
+    for group in groups:
+        high, low = split(assembled(group))
+        results.append(mul_t(jnp.concatenate([high, low, high], axis=1), three_z))
+    whole = jnp.concatenate([results[1], results[2], results[0]], axis=0)
     for y in range(p.cy):
         first, rows, piece, at = windows[y]
         off = (y // p.yq) * p.xe - first

time: 54.8 us -> 54.2 us (0.989)
  Pallas kernels: 9.11 us -> 8.56 us
    pallas_call x7, Pallas kernels: 9.11 us -> 8.56 us  [call(): pl.pallas_call(kernel, out_shape=tuple(outs), in_specs=specs or [VMEM_SPE...]
where the time goes in v6:
time: 54.2 us; the launch traced here: 53.9 us
  blocking collectives  24.9 us (46%)
  starting transfers between devices  15 us (28%)
  Pallas kernels  8.56 us (16%)
  waiting for transfers between devices  3.26 us (6%)
  other arithmetic  1.4 us (3%)
  between operations  0.8 us (1%)
    all_to_all x1, blocking collectives, local_planes(): blocks = lax.all_to_all(blocks, group, 0, 0)  14.4 us
    all_to_all x1, blocking collectives, local_planes(): sums = lax.all_to_all(sums, ('gx', 'gh', 'gl'), 0, 0)  10.5 us
    pallas_call x7, Pallas kernels, call(): pl.pallas_call(kernel, out_shape=tuple(outs), in_specs=specs or [VMEM_SPE...  8.56 us
    all_to_all x1, starting transfers between devices, local_planes(): blocks = lax.all_to_all(blocks, group, 0, 0)  6.27 us
    ppermute x1, starting transfers between devices, local_planes(): lax.ppermute(jnp.where(even_y, eps[:2], eps[p.cy - 2:]), along_y, pairs(2...  3.5 us
    ppermute x1, waiting for transfers between devices, local_planes(): received = lax.ppermute(sent, 'gh', [(0, 1), (1, 0)])  2.3 us
    ppermute x1, starting transfers between devices, local_planes(): lax.ppermute(jnp.where(even_x, eps[:, :2], eps[:, p.cx - 2:]), 'gx', pair...  1.63 us
    ppermute x1, starting transfers between devices, local_planes(): received = lax.ppermute(sent, 'gh', [(0, 1), (1, 0)])  1.58 us
  transfers between devices with their start and end apart: 6, of which 2 were waited for; matrix products, arithmetic and copies ran while one was open for 3% of the time, Pallas kernels for 2%

profile of v6, /device:TPU:0, one launch (start us, length us, event | category | flops | bytes accessed | tf_op | source)
XLA Modules:
  0.0 53.9 jit_solution(4707090752667994499)
XLA Ops:
  0.6 0.0 copy-start.5
  0.6 0.0 copy-start
  0.7 2.9 %shard_map.77 = f32[16,40,128]{2,1,0:T(8,128)} custom-call(f32[10,20,384]{2,1,0:T(8,128)} %bitcast.16, bf16[384,512]{1,0:T(8,128)(2,1)} %constant.48.clone.refs_1_, bf16[384,512]{1,0:T(8,128)(2,1)} %constant.49.clone.refs_2_), custom_call_target="tpu_custom_call" | custom-call | bytes 1421312 | tf_op jit(solution)/shard_map/pallas_call | solution.py:364
  3.5 6.3 %all-to-all-start = ((f32[16,40,128]{2,1,0:T(8,128)}), f32[16,40,128]{2,1,0:T(8,128)S(1)}, u32[]{:S(2)}, u32[]{:S(2)}) async-start(f32[16,40,128]{2,1,0:T(8,128)} %shard_map.77), calls=%async_computation | async-start | bytes 655360 | tf_op jit(solution)/shard_map/all_to_all | solution.py:723
  9.8 0.0 copy-done.5
  9.8 0.0 copy-start.4
  9.9 1.3 %fusion.3.refs_0_ = f32[10,20,384]{2,1,0:T(8,128)S(1)} fusion(f32[20,10,384]{2,0,1:T(8,128)S(1)} %copy-done.5), kind=kLoop, calls=%fused_computation.5 | loop fusion | flops 537600 | bytes 614400 | tf_op jit(solution)/shard_map/exp | solution.py:43
  11.2 0.5 collective-permute-start.2
  11.7 1.6 %collective-permute-start.1 = (f32[10,2,384]{2,1,0:T(2,128)S(1)}, f32[10,2,384]{2,1,0:T(2,128)S(1)}, u32[]{:S(2)}, u32[]{:S(2)}) collective-permute-start(f32[10,2,384]{2,1,0:T(2,128)S(1)} %get-tuple-element.49), channel_id=1, source_target_pairs={{8,16},{24,0},{16,8},{0,24},{9,17},{25,1},{17,9},{1,25},{10,18},{2... | collective-permute-start | bytes 92168 | tf_op jit(solution)/shard_map/ppermute | solution.py:731
  13.3 1.5 %collective-permute-start.4 = (f32[2,20,384]{2,1,0:T(8,128)S(1)}, f32[2,20,384]{2,1,0:T(8,128)S(1)}, u32[]{:S(2)}, u32[]{:S(2)}) collective-permute-start(f32[2,20,384]{2,1,0:T(8,128)S(1)} %get-tuple-element.46), channel_id=1, source_target_pairs={{0,1},{2,3},{4,5},{6,7},{1,0},{3,2},{5,4},{7,6},{8,9},{10,11},{12,... | collective-permute-start | bytes 184328 | tf_op jit(solution)/shard_map/ppermute | solution.py:734
  14.9 3.5 %collective-permute-start.3 = (f32[2,20,384]{2,1,0:T(8,128)S(1)}, f32[2,20,384]{2,1,0:T(8,128)S(1)}, u32[]{:S(2)}, u32[]{:S(2)}) collective-permute-start(f32[2,20,384]{2,1,0:T(8,128)S(1)} %get-tuple-element.47), channel_id=1, source_target_pairs={{1,2},{3,4},{5,6},{7,0},{2,1},{4,3},{6,5},{0,7},{9,10},{11,12},{13... | collective-permute-start | bytes 184328 | tf_op jit(solution)/shard_map/ppermute | solution.py:728
  18.4 0.0 copy-done
  18.4 0.1 shard_map.78.refs_2_.refs_3_
  18.5 0.0 collective-permute-done.2
  18.5 0.0 collective-permute-done.1
  18.5 0.0 all-to-all-done.refs_0_
  18.5 0.0 copy-done.4
  18.5 0.8 %shard_map.79 = (f32[40,3072]{1,0:T(8,128)S(1)}, f32[144,128]{1,0:T(8,128)S(1)}, f32[96,128]{1,0:T(8,128)S(1)}) custom-call(f32[16,40,128]{2,1,0:T(8,128)S(1)} %all-to-all-done.refs_0_, bf16[416,384]{1,0:T(8,128)(2,1)S(1)} %copy-done.4, f32[40,3072]{1,0:T(8,128)S(1)} %shard_map.78.refs_2_.refs_3_), custom_call_target="tpu_custom_call" | custom-call | bytes 1753088 | tf_op jit(solution)/shard_map/pallas_call | solution.py:364
  19.4 1.6 %collective-permute-start = (f32[96,128]{1,0:T(8,128)S(1)}, f32[96,128]{1,0:T(8,128)S(1)}, u32[]{:S(2)}, u32[]{:S(2)}) collective-permute-start(f32[96,128]{1,0:T(8,128)S(1)} %get-tuple-element.30), channel_id=1, source_target_pairs={{0,4},{4,0},{1,5},{5,1},{2,6},{6,2},{3,7},{7,3},{8,12},{12,8},{9,1... | collective-permute-start | bytes 147464 | tf_op jit(solution)/shard_map/ppermute | solution.py:750
  21.0 0.0 collective-permute-done.4
  21.0 0.9 %collective-permute-done.3 = f32[2,20,384]{2,1,0:T(8,128)S(1)} collective-permute-done((f32[2,20,384]{2,1,0:T(8,128)S(1)}, f32[2,20,384]{2,1,0:T(8,128)S(1)}, u32[]{:S(2)}, u32[]{:S(2)}) %collective-permute-start.3) | collective-permute-done | bytes 61472 | tf_op jit(solution)/shard_map/ppermute | solution.py:728
  21.9 0.2 shard_map.80
  22.1 2.3 %collective-permute-done.refs_2_ = f32[96,128]{1,0:T(8,128)S(1)} collective-permute-done((f32[96,128]{1,0:T(8,128)S(1)}, f32[96,128]{1,0:T(8,128)S(1)}, u32[]{:S(2)}, u32[]{:S(2)}) %collective-permute-start) | collective-permute-done | bytes 49184 | tf_op jit(solution)/shard_map/ppermute | solution.py:750
  24.4 1.2 %shard_map.81 = f32[16,80,128]{2,1,0:T(8,128)S(1)} custom-call(f32[40,3072]{1,0:T(8,128)S(1)} %get-tuple-element.26.refs_0_, f32[144,128]{1,0:T(8,128)S(1)} %get-tuple-element.27.refs_1_, f32[96,128]{1,0:T(8,128)S(1)} %collective-permute-done.refs_2_, f32[40,3072]{1,0:T(8,128)S(1)} %shard_map.78.refs_2_.refs_3_, f32[2968,128]{1,0:T(8,128)S(1)} %copy-done, ...), custom_call_target="tpu_custom_call" | custom-call | bytes 3600384 | tf_op jit(solution)/shard_map/pallas_call | solution.py:364
  25.7 0.0 copy-start.1
  25.7 0.0 copy-start.2
  25.7 0.0 copy-start.3
  25.7 14.4 %all_to_all.15.refs_0_ = f32[16,80,128]{2,1,0:T(8,128)S(1)} all-to-all(f32[16,80,128]{2,1,0:T(8,128)S(1)} %shard_map.81), channel_id=1, replica_groups=mesh['gx'=4,'gh'=2,'gl'=4] {'gx','gl'}, dimensions={0} | all-to-all | bytes 1310720 | tf_op jit(solution)/shard_map/all_to_all | solution.py:773
  40.1 0.0 copy-done.1
  40.1 0.0 copy-done.2
  40.1 0.0 copy-done.3
  40.2 2.2 %shard_map.82 = (f32[10,20,384]{2,1,0:T(8,128)S(1)}, f32[10,20,384]{2,1,0:T(8,128)S(1)}, f32[32,1,128]{2,1,0:T(1,128)S(1)}) custom-call(f32[16,80,128]{2,1,0:T(8,128)S(1)} %all_to_all.15.refs_0_, bf16[384,512]{1,0:T(8,128)(2,1)S(1)} %copy-done.3, bf16[384,512]{1,0:T(8,128)(2,1)S(1)} %copy-done.2, f32[10,20,384]{2,1,0:T(8,128)S(1)} %bitcast.17, ...), custom_call_target="tpu_custom_call" | custom-call | bytes 3762176 | tf_op jit(solution)/shard_map/pallas_call | solution.py:364
  42.4 10.5 %all_to_all.16.refs_0_ = f32[32,1,128]{2,1,0:T(1,128)S(1)} all-to-all(f32[32,1,128]{2,1,0:T(1,128)S(1)} %get-tuple-element.41), channel_id=1, replica_groups=mesh['gx'=4,'gh'=2,'gl'=4] {'gx','gh','gl'}, dimensions={0} | all-to-all | bytes 32768 | tf_op jit(solution)/shard_map/all_to_all | solution.py:783
  52.9 1.1 %shard_map.83 = (f32[10,20,384]{2,1,0:T(8,128)}, f32[10,20,384]{2,1,0:T(8,128)}) custom-call(f32[32,1,128]{2,1,0:T(1,128)S(1)} %all_to_all.16.refs_0_, f32[10,20,384]{2,1,0:T(8,128)S(1)} %bitcast.18, f32[10,20,384]{2,1,0:T(8,128)S(1)} %get-tuple-element.42.refs_2_, f32[10,20,384]{2,1,0:T(8,128)S(1)} %get-tuple-element.43.refs_3_), custom_call_target="tpu_custom_call" | custom-call | bytes 1552384 | tf_op jit(solution)/shard_map/pallas_call | solution.py:364
  (4 shorter events, 0.1 us)
Async XLA Ops:
  0.6 9.2 %copy-start.5 = (f32[20,10,384]{2,0,1:T(8,128)S(1)}, f32[20,10,384]{2,0,1:T(8,128)}, u32[]{:S(2)}) copy-start(f32[20,10,384]{2,0,1:T(8,128)} %param.6) | copy-start | bytes 921604
  0.6 17.7 %copy-start = (f32[2968,128]{1,0:T(8,128)S(1)}, f32[2968,128]{1,0:T(8,128)}, u32[]{:S(2)}) copy-start(f32[2968,128]{1,0:T(8,128)} %constant.51.clone.refs_0_.refs_4_) | copy-start | bytes 4558852
  3.5 15.0 %all-to-all-start = ((f32[16,40,128]{2,1,0:T(8,128)}), f32[16,40,128]{2,1,0:T(8,128)S(1)}, u32[]{:S(2)}, u32[]{:S(2)}) async-start(f32[16,40,128]{2,1,0:T(8,128)} %shard_map.77), calls=%async_computation | async-start | bytes 655360 | tf_op jit(solution)/shard_map/all_to_all | solution.py:723
  9.8 8.7 %copy-start.4 = (bf16[416,384]{1,0:T(8,128)(2,1)S(1)}, bf16[416,384]{1,0:T(8,128)(2,1)}, u32[]{:S(2)}) copy-start(bf16[416,384]{1,0:T(8,128)(2,1)} %constant.50.clone.refs_1_.refs_5_) | copy-start | bytes 958468
  11.2 7.2 %collective-permute-start.2 = (f32[10,2,384]{2,1,0:T(2,128)S(1)}, f32[10,2,384]{2,1,0:T(2,128)S(1)}, u32[]{:S(2)}, u32[]{:S(2)}) collective-permute-start(f32[10,2,384]{2,1,0:T(2,128)S(1)} %get-tuple-element.48), channel_id=1, source_target_pairs={{0,8},{16,24},{8,0},{24,16},{1,9},{17,25},{9,1},{25,17},{2,10},{18... | collective-permute-start | bytes 92168 | tf_op jit(solution)/shard_map/ppermute | solution.py:737
  11.7 6.8 %collective-permute-start.1 = (f32[10,2,384]{2,1,0:T(2,128)S(1)}, f32[10,2,384]{2,1,0:T(2,128)S(1)}, u32[]{:S(2)}, u32[]{:S(2)}) collective-permute-start(f32[10,2,384]{2,1,0:T(2,128)S(1)} %get-tuple-element.49), channel_id=1, source_target_pairs={{8,16},{24,0},{16,8},{0,24},{9,17},{25,1},{17,9},{1,25},{10,18},{2... | collective-permute-start | bytes 92168 | tf_op jit(solution)/shard_map/ppermute | solution.py:731
  13.3 7.6 %collective-permute-start.4 = (f32[2,20,384]{2,1,0:T(8,128)S(1)}, f32[2,20,384]{2,1,0:T(8,128)S(1)}, u32[]{:S(2)}, u32[]{:S(2)}) collective-permute-start(f32[2,20,384]{2,1,0:T(8,128)S(1)} %get-tuple-element.46), channel_id=1, source_target_pairs={{0,1},{2,3},{4,5},{6,7},{1,0},{3,2},{5,4},{7,6},{8,9},{10,11},{12,... | collective-permute-start | bytes 184328 | tf_op jit(solution)/shard_map/ppermute | solution.py:734
  14.9 7.0 %collective-permute-start.3 = (f32[2,20,384]{2,1,0:T(8,128)S(1)}, f32[2,20,384]{2,1,0:T(8,128)S(1)}, u32[]{:S(2)}, u32[]{:S(2)}) collective-permute-start(f32[2,20,384]{2,1,0:T(8,128)S(1)} %get-tuple-element.47), channel_id=1, source_target_pairs={{1,2},{3,4},{5,6},{7,0},{2,1},{4,3},{6,5},{0,7},{9,10},{11,12},{13... | collective-permute-start | bytes 184328 | tf_op jit(solution)/shard_map/ppermute | solution.py:728
  19.4 5.0 %collective-permute-start = (f32[96,128]{1,0:T(8,128)S(1)}, f32[96,128]{1,0:T(8,128)S(1)}, u32[]{:S(2)}, u32[]{:S(2)}) collective-permute-start(f32[96,128]{1,0:T(8,128)S(1)} %get-tuple-element.30), channel_id=1, source_target_pairs={{0,4},{4,0},{1,5},{5,1},{2,6},{6,2},{3,7},{7,3},{8,12},{12,8},{9,1... | collective-permute-start | bytes 147464 | tf_op jit(solution)/shard_map/ppermute | solution.py:750
  25.7 14.5 %copy-start.1 = (f32[20,10,384]{2,0,1:T(8,128)S(1)}, f32[20,10,384]{2,0,1:T(8,128)}, u32[]{:S(2)}) copy-start(f32[20,10,384]{2,0,1:T(8,128)} %param.7) | copy-start | bytes 921604
  25.7 14.5 %copy-start.2 = (bf16[384,512]{1,0:T(8,128)(2,1)S(1)}, bf16[384,512]{1,0:T(8,128)(2,1)}, u32[]{:S(2)}) copy-start(bf16[384,512]{1,0:T(8,128)(2,1)} %constant.49.clone.refs_2_) | copy-start | bytes 1179652
  25.7 14.5 %copy-start.3 = (bf16[384,512]{1,0:T(8,128)(2,1)S(1)}, bf16[384,512]{1,0:T(8,128)(2,1)}, u32[]{:S(2)}) copy-start(bf16[384,512]{1,0:T(8,128)(2,1)} %constant.48.clone.refs_1_) | copy-start | bytes 1179652

commit v7 on v6

--- a/solution.py
+++ b/solution.py
@@ -228,10 +228,9 @@
         self.group = LANES // max(self.kz, 1)
         self.chunks = -(-self.ng // self.group)
         self.deep = self.chunks * LANES
-        self.extra = self.cx // self.yq if self.yq else 0
-        self.rows = up(2 * self.xe + self.cx + self.extra, 8)
+        self.third = self.kz // HALO
+        self.rows = up(2 * self.xe + self.cx, 8)
         self.mirror = self.nx // 2 + 1
-        self.lines = self.cy * self.xw + (2 * HALO - 1) * self.xp + self.yq * 8
 
     def fits(self):
         return (
@@ -241,7 +240,8 @@
             and self.nz % (self.ng * 8) == 0
             and self.nz % LANES == 0
             and self.yq == 2 * HALO - 1
-            and self.cx == 4 * self.yq
+            and self.kz % (8 * HALO) == 0
+            and self.step + self.third <= LANES
             and self.step <= LANES
             and self.step % 8 == 0
             and self.nx <= LANES
@@ -381,8 +381,12 @@
     return values if shift == 0 else pltpu.roll(values, shift, 1)
 
 
+def within(lane, first, count):
+    return (lane >= first) & (lane < first + count)
+
+
 def between(lane, slot, width):
-    return (lane >= slot * width) & (lane < (slot + 1) * width)
+    return within(lane, slot * width, width)
 
 
 def fetched(pairs, sems):
@@ -522,27 +526,19 @@
     cut = p.gx * p.xw
     wide_rows = x_bwd[:cut, :]
     own_rows = x_bwd[cut:, :]
-    gap = jnp.zeros((LANES - p.step, LANES), jnp.float32)
-    slots = lane_index(p.extra)
-    rest = p.rows - 2 * p.xe - p.cx - p.extra
+    rest = p.rows - 2 * p.xe - p.cx
+
+    def filled(pieces, part):
+        first = base + (gl + 1) * 2 * p.step + p.edge - p.kz + part * p.third
+        pieces = [planes[pl.ds(at, count), :] for at, count in (*pieces, (first, p.third))]
+        return padded_rows(jnp.concatenate(pieces, axis=0), LANES)
+
     for gl in range(p.gl):
         start = base + gl * 2 * p.step
         end = start + 2 * p.step
-        last = planes[pl.ds(end + p.edge - p.kz, p.kz), :]
-        both = jnp.concatenate(
-            [planes[pl.ds(start, LANES), :], planes[pl.ds(start + p.step, LANES), :]], axis=0
-        )
-        wide = mul_t(wide_rows, stacked(both, 1))
-        sides = jnp.concatenate(
-            [
-                planes[pl.ds(start - p.edge, p.edge), :],
-                planes[pl.ds(end, p.edge - p.kz), :],
-                gap,
-                *[last] * p.yq,
-                gap,
-            ],
-            axis=0,
-        )
+        both = [filled([(start + i * p.step, p.step)], i) for i in range(2)]
+        wide = mul_t(wide_rows, stacked(jnp.concatenate(both, axis=0), 1))
+        sides = filled([(start - p.edge, p.edge), (end, p.edge - p.kz)], 2)
         side = mul_t(own_rows, stacked(sides, 1))
         for gx in range(p.gx):
             target = gx * p.gl + gl
@@ -551,15 +547,9 @@
                     gx * p.xw : gx * p.xw + p.xe, half * LANES : (half + 1) * LANES
                 ]
             at, line = 2 * p.xe, gx * p.xp
-            out[target, at : at + p.cx] = side[line : line + p.cx, :LANES]
-            at += p.cx
-            extra = jnp.zeros((p.extra, LANES), jnp.float32)
-            for q in range(p.yq):
-                value = side[line + q * p.extra : line + (q + 1) * p.extra, LANES:]
-                extra = jnp.where(between(slots, q, p.kz), value, extra)
-            out[target, at : at + p.extra] = extra
+            out[target, at : at + p.cx] = side[line : line + p.cx]
             if rest:
-                out[target, at + p.extra :] = jnp.zeros((rest, LANES), jnp.float32)
+                out[target, at + p.cx :] = jnp.zeros((rest, LANES), jnp.float32)
 
 
 def faces_kernel(p, eps, ex_low, ex_high, ey_low, ey_high, faces_x, faces_y, faces_z, mass):
@@ -576,37 +566,41 @@
 
 def stencil_kernel(
     p, blocks, high_z, low_z, charge, faces_x, faces_y, faces_z, mass,
-    pre, image, sums, lines, field,
+    pre, image, sums, field,
 ):
     lane = lane_index(p.xw)
-    windows, at = [], 0
-    for y in range(p.cy):
-        half = y // p.yq
-        windows.append((half * p.xe // 8 * 8, p.xw, y % p.yq, at))
-        at += p.xw
     side = 2 * p.xe
-    for h in range(2 * HALO - 1):
-        windows.append((side // 8 * 8, p.xp, h, at))
-        at += p.xp
-    tail = side + p.cx
-    for q in range(p.yq):
-        windows.append((tail // 8 * 8, 8, q, at))
-        at += 8
+
+    def line_of(chunk, first, rows, source_lane, skip, count):
+        here = lane[:rows]
+        line = jnp.zeros((rows, LANES), jnp.float32)
+        for slot in range(min(p.group, p.ng - chunk * p.group)):
+            part = blocks[chunk * p.group + slot, first : first + rows, :]
+            at = slot * p.kz + skip
+            line = jnp.where(within(here, at, count), moved(part, at - source_lane), line)
+        return line
+
+    def plain(first, rows, piece):
+        return rows, lambda chunk: line_of(chunk, first, rows, piece * p.kz, 0, p.kz)
+
+    def last_layer(chunk):
+        total = 0.0
+        for part, row in enumerate((HALO, p.xe + HALO, side)):
+            first = max(0, row - HALO) // 8 * 8 if part < 2 else row // 8 * 8
+            rows = p.xw if part < 2 else p.xp
+            line = line_of(chunk, first, rows, p.step, part * p.third, p.third)
+            total = total + line[row - first : row - first + p.cx]
+        return padded_rows(total, p.xp)
+
+    windows = [plain(y // p.yq * p.xe // 8 * 8, p.xw, y % p.yq) for y in range(p.cy)]
+    windows += [plain(side // 8 * 8, p.xp, h) for h in range(2 * HALO - 1)]
+    windows.append((p.xp, last_layer))
     three_z = jnp.concatenate([high_z[...], high_z[...], low_z[...]], axis=1)
+
     def assembled(group):
         parts = []
         for chunk in range(p.chunks):
-            count = min(p.group, p.ng - chunk * p.group)
-            pieces = []
-            for first, rows, piece, at in group:
-                here = lane[:rows]
-                line = jnp.zeros((rows, LANES), jnp.float32)
-                for slot in range(count):
-                    part = blocks[chunk * p.group + slot, first : first + rows, :]
-                    part = moved(part, (slot - piece) * p.kz)
-                    line = jnp.where(between(here, slot, p.kz), part, line)
-                pieces.append(line)
-            parts.append(jnp.concatenate(pieces, axis=0))
+            parts.append(jnp.concatenate([make(chunk) for rows, make in group], axis=0))
         return jnp.concatenate(parts, axis=1)
 
     groups = [windows[p.cy :], windows[: p.yq], windows[p.yq : p.cy]]
@@ -615,21 +609,15 @@
         high, low = split(assembled(group))
         results.append(mul_t(jnp.concatenate([high, low, high], axis=1), three_z))
     whole = jnp.concatenate([results[1], results[2], results[0]], axis=0)
+    starts = np.cumsum([0] + [rows for rows, make in windows])
     for y in range(p.cy):
-        first, rows, piece, at = windows[y]
-        off = (y // p.yq) * p.xe - first
-        field[HALO + y, : p.xe] = whole[at + off : at + off + p.xe]
-    for h in range(2 * HALO - 1):
-        first, rows, piece, at = windows[p.cy + h]
-        off = side - first
+        at = int(starts[y]) + y // p.yq * p.xe % 8
+        field[HALO + y, : p.xe] = whole[at : at + p.xe]
+    for h in range(2 * HALO):
+        at = int(starts[p.cy + h]) + (side % 8 if h < 2 * HALO - 1 else 0)
         y = h if h < HALO else h + p.cy
-        field[y, HALO : HALO + p.cx] = whole[at + off : at + off + p.cx]
-    for q in range(p.yq):
-        first, rows, piece, at = windows[p.cy + 2 * HALO - 1 + q]
-        off = tail - first
-        field[p.cy + 2 * HALO - 1, HALO + q * p.extra : HALO + (q + 1) * p.extra] = whole[
-            at + off : at + off + p.extra
-        ]
+        field[y, HALO : HALO + p.cx] = whole[at : at + p.cx]
+
     def stretch(flux_at):
         return 27.0 * (flux_at(2) - flux_at(1)) - (flux_at(3) - flux_at(0))
 
@@ -776,7 +764,6 @@
         [shape(*brick), shape(*brick), shape(2 * p.ng, 1, LANES)],
         [blocks, high_z, low_z, charge, *faces],
         [
-            pltpu.VMEM((p.lines, p.deep), f32),
             pltpu.VMEM((p.cy + 2 * HALO, p.xw, p.nz), f32),
         ],
     )

time: 54.2 us -> 53.3 us (0.983)
  blocking collectives: 24.9 us -> 24.1 us
    all_to_all x1, blocking collectives: 14.4 us -> 13.7 us  [local_planes(): blocks = lax.all_to_all(blocks, group, 0, 0)]
where the time goes in v7:
time: 53.3 us; the launch traced here: 53 us
  blocking collectives  24.1 us (45%)
  starting transfers between devices  15 us (28%)
  Pallas kernels  8.55 us (16%)
  waiting for transfers between devices  3.26 us (6%)
  other arithmetic  1.4 us (3%)
  between operations  0.78 us (1%)
    all_to_all x1, blocking collectives, local_planes(): blocks = lax.all_to_all(blocks, group, 0, 0)  13.7 us
    all_to_all x1, blocking collectives, local_planes(): sums = lax.all_to_all(sums, ('gx', 'gh', 'gl'), 0, 0)  10.3 us
    pallas_call x7, Pallas kernels, call(): pl.pallas_call(kernel, out_shape=tuple(outs), in_specs=specs or [VMEM_SPE...  8.55 us
    all_to_all x1, starting transfers between devices, local_planes(): blocks = lax.all_to_all(blocks, group, 0, 0)  6.27 us
    ppermute x1, starting transfers between devices, local_planes(): lax.ppermute(jnp.where(even_y, eps[:2], eps[p.cy - 2:]), along_y, pairs(2...  3.5 us
    ppermute x1, waiting for transfers between devices, local_planes(): received = lax.ppermute(sent, 'gh', [(0, 1), (1, 0)])  2.3 us
    ppermute x1, starting transfers between devices, local_planes(): lax.ppermute(jnp.where(even_x, eps[:, :2], eps[:, p.cx - 2:]), 'gx', pair...  1.63 us
    ppermute x1, starting transfers between devices, local_planes(): received = lax.ppermute(sent, 'gh', [(0, 1), (1, 0)])  1.58 us
  transfers between devices with their start and end apart: 6, of which 2 were waited for; matrix products, arithmetic and copies ran while one was open for 3% of the time, Pallas kernels for 2%

profile of v7, /device:TPU:0, one launch (start us, length us, event | category | flops | bytes accessed | tf_op | source)
XLA Modules:
  0.0 53.0 jit_solution(12193731994864832817)
XLA Ops:
  0.6 0.0 copy-start.5
  0.6 0.0 copy-start
  0.7 2.9 %shard_map.77 = f32[16,40,128]{2,1,0:T(8,128)} custom-call(f32[10,20,384]{2,1,0:T(8,128)} %bitcast.16, bf16[384,512]{1,0:T(8,128)(2,1)} %constant.48.clone.refs_1_, bf16[384,512]{1,0:T(8,128)(2,1)} %constant.49.clone.refs_2_), custom_call_target="tpu_custom_call" | custom-call | bytes 1421312 | tf_op jit(solution)/shard_map/pallas_call | solution.py:364
  3.5 6.3 %all-to-all-start = ((f32[16,40,128]{2,1,0:T(8,128)}), f32[16,40,128]{2,1,0:T(8,128)S(1)}, u32[]{:S(2)}, u32[]{:S(2)}) async-start(f32[16,40,128]{2,1,0:T(8,128)} %shard_map.77), calls=%async_computation | async-start | bytes 655360 | tf_op jit(solution)/shard_map/all_to_all | solution.py:711
  9.8 0.0 copy-done.5
  9.8 0.0 copy-start.4
  9.9 1.3 %fusion.3.refs_0_ = f32[10,20,384]{2,1,0:T(8,128)S(1)} fusion(f32[20,10,384]{2,0,1:T(8,128)S(1)} %copy-done.5), kind=kLoop, calls=%fused_computation.5 | loop fusion | flops 537600 | bytes 614400 | tf_op jit(solution)/shard_map/exp | solution.py:43
  11.2 0.5 collective-permute-start.2
  11.7 1.6 %collective-permute-start.1 = (f32[10,2,384]{2,1,0:T(2,128)S(1)}, f32[10,2,384]{2,1,0:T(2,128)S(1)}, u32[]{:S(2)}, u32[]{:S(2)}) collective-permute-start(f32[10,2,384]{2,1,0:T(2,128)S(1)} %get-tuple-element.49), channel_id=1, source_target_pairs={{8,16},{24,0},{16,8},{0,24},{9,17},{25,1},{17,9},{1,25},{10,18},{2... | collective-permute-start | bytes 92168 | tf_op jit(solution)/shard_map/ppermute | solution.py:719
  13.3 1.5 %collective-permute-start.4 = (f32[2,20,384]{2,1,0:T(8,128)S(1)}, f32[2,20,384]{2,1,0:T(8,128)S(1)}, u32[]{:S(2)}, u32[]{:S(2)}) collective-permute-start(f32[2,20,384]{2,1,0:T(8,128)S(1)} %get-tuple-element.46), channel_id=1, source_target_pairs={{0,1},{2,3},{4,5},{6,7},{1,0},{3,2},{5,4},{7,6},{8,9},{10,11},{12,... | collective-permute-start | bytes 184328 | tf_op jit(solution)/shard_map/ppermute | solution.py:722
  14.9 3.5 %collective-permute-start.3 = (f32[2,20,384]{2,1,0:T(8,128)S(1)}, f32[2,20,384]{2,1,0:T(8,128)S(1)}, u32[]{:S(2)}, u32[]{:S(2)}) collective-permute-start(f32[2,20,384]{2,1,0:T(8,128)S(1)} %get-tuple-element.47), channel_id=1, source_target_pairs={{1,2},{3,4},{5,6},{7,0},{2,1},{4,3},{6,5},{0,7},{9,10},{11,12},{13... | collective-permute-start | bytes 184328 | tf_op jit(solution)/shard_map/ppermute | solution.py:716
  18.4 0.0 copy-done
  18.4 0.1 shard_map.78.refs_2_.refs_3_
  18.5 0.0 collective-permute-done.2
  18.5 0.0 collective-permute-done.1
  18.5 0.0 all-to-all-done.refs_0_
  18.5 0.0 copy-done.4
  18.5 0.8 %shard_map.79 = (f32[40,3072]{1,0:T(8,128)S(1)}, f32[144,128]{1,0:T(8,128)S(1)}, f32[96,128]{1,0:T(8,128)S(1)}) custom-call(f32[16,40,128]{2,1,0:T(8,128)S(1)} %all-to-all-done.refs_0_, bf16[416,384]{1,0:T(8,128)(2,1)S(1)} %copy-done.4, f32[40,3072]{1,0:T(8,128)S(1)} %shard_map.78.refs_2_.refs_3_), custom_call_target="tpu_custom_call" | custom-call | bytes 1753088 | tf_op jit(solution)/shard_map/pallas_call | solution.py:364
  19.4 1.6 %collective-permute-start = (f32[96,128]{1,0:T(8,128)S(1)}, f32[96,128]{1,0:T(8,128)S(1)}, u32[]{:S(2)}, u32[]{:S(2)}) collective-permute-start(f32[96,128]{1,0:T(8,128)S(1)} %get-tuple-element.30), channel_id=1, source_target_pairs={{0,4},{4,0},{1,5},{5,1},{2,6},{6,2},{3,7},{7,3},{8,12},{12,8},{9,1... | collective-permute-start | bytes 147464 | tf_op jit(solution)/shard_map/ppermute | solution.py:738
  21.0 0.0 collective-permute-done.4
  21.0 0.9 %collective-permute-done.3 = f32[2,20,384]{2,1,0:T(8,128)S(1)} collective-permute-done((f32[2,20,384]{2,1,0:T(8,128)S(1)}, f32[2,20,384]{2,1,0:T(8,128)S(1)}, u32[]{:S(2)}, u32[]{:S(2)}) %collective-permute-start.3) | collective-permute-done | bytes 61472 | tf_op jit(solution)/shard_map/ppermute | solution.py:716
  21.9 0.2 shard_map.80
  22.1 2.3 %collective-permute-done.refs_2_ = f32[96,128]{1,0:T(8,128)S(1)} collective-permute-done((f32[96,128]{1,0:T(8,128)S(1)}, f32[96,128]{1,0:T(8,128)S(1)}, u32[]{:S(2)}, u32[]{:S(2)}) %collective-permute-start) | collective-permute-done | bytes 49184 | tf_op jit(solution)/shard_map/ppermute | solution.py:738
  24.4 0.0 copy-start.1
  24.4 0.0 copy-start.2
  24.4 0.0 copy-start.3
  24.4 1.2 %shard_map.81 = f32[16,72,128]{2,1,0:T(8,128)S(1)} custom-call(f32[40,3072]{1,0:T(8,128)S(1)} %get-tuple-element.26.refs_0_, f32[144,128]{1,0:T(8,128)S(1)} %get-tuple-element.27.refs_1_, f32[96,128]{1,0:T(8,128)S(1)} %collective-permute-done.refs_2_, f32[40,3072]{1,0:T(8,128)S(1)} %shard_map.78.refs_2_.refs_3_, f32[2968,128]{1,0:T(8,128)S(1)} %copy-done, ...), custom_call_target="tpu_custom_call" | custom-call | bytes 3534848 | tf_op jit(solution)/shard_map/pallas_call | solution.py:364
  25.6 13.7 %all_to_all.15.refs_0_ = f32[16,72,128]{2,1,0:T(8,128)S(1)} all-to-all(f32[16,72,128]{2,1,0:T(8,128)S(1)} %shard_map.81), channel_id=1, replica_groups=mesh['gx'=4,'gh'=2,'gl'=4] {'gx','gl'}, dimensions={0} | all-to-all | bytes 1179648 | tf_op jit(solution)/shard_map/all_to_all | solution.py:761
  39.3 0.0 copy-done.1
  39.3 0.0 copy-done.2
  39.3 0.0 copy-done.3
  39.3 2.3 %shard_map.82 = (f32[10,20,384]{2,1,0:T(8,128)S(1)}, f32[10,20,384]{2,1,0:T(8,128)S(1)}, f32[32,1,128]{2,1,0:T(1,128)S(1)}) custom-call(f32[16,72,128]{2,1,0:T(8,128)S(1)} %all_to_all.15.refs_0_, bf16[384,512]{1,0:T(8,128)(2,1)S(1)} %copy-done.3, bf16[384,512]{1,0:T(8,128)(2,1)S(1)} %copy-done.2, f32[10,20,384]{2,1,0:T(8,128)S(1)} %bitcast.17, ...), custom_call_target="tpu_custom_call" | custom-call | bytes 3696640 | tf_op jit(solution)/shard_map/pallas_call | solution.py:364
  41.7 10.3 %all_to_all.16.refs_0_ = f32[32,1,128]{2,1,0:T(1,128)S(1)} all-to-all(f32[32,1,128]{2,1,0:T(1,128)S(1)} %get-tuple-element.41), channel_id=1, replica_groups=mesh['gx'=4,'gh'=2,'gl'=4] {'gx','gh','gl'}, dimensions={0} | all-to-all | bytes 32768 | tf_op jit(solution)/shard_map/all_to_all | solution.py:770
  52.0 1.0 %shard_map.83 = (f32[10,20,384]{2,1,0:T(8,128)}, f32[10,20,384]{2,1,0:T(8,128)}) custom-call(f32[32,1,128]{2,1,0:T(1,128)S(1)} %all_to_all.16.refs_0_, f32[10,20,384]{2,1,0:T(8,128)S(1)} %bitcast.18, f32[10,20,384]{2,1,0:T(8,128)S(1)} %get-tuple-element.42.refs_2_, f32[10,20,384]{2,1,0:T(8,128)S(1)} %get-tuple-element.43.refs_3_), custom_call_target="tpu_custom_call" | custom-call | bytes 1552384 | tf_op jit(solution)/shard_map/pallas_call | solution.py:364
  (4 shorter events, 0.1 us)
Async XLA Ops:
  0.6 9.2 %copy-start.5 = (f32[20,10,384]{2,0,1:T(8,128)S(1)}, f32[20,10,384]{2,0,1:T(8,128)}, u32[]{:S(2)}) copy-start(f32[20,10,384]{2,0,1:T(8,128)} %param.6) | copy-start | bytes 921604
  0.6 17.7 %copy-start = (f32[2968,128]{1,0:T(8,128)S(1)}, f32[2968,128]{1,0:T(8,128)}, u32[]{:S(2)}) copy-start(f32[2968,128]{1,0:T(8,128)} %constant.51.clone.refs_0_.refs_4_) | copy-start | bytes 4558852
  3.5 15.0 %all-to-all-start = ((f32[16,40,128]{2,1,0:T(8,128)}), f32[16,40,128]{2,1,0:T(8,128)S(1)}, u32[]{:S(2)}, u32[]{:S(2)}) async-start(f32[16,40,128]{2,1,0:T(8,128)} %shard_map.77), calls=%async_computation | async-start | bytes 655360 | tf_op jit(solution)/shard_map/all_to_all | solution.py:711
  9.8 8.7 %copy-start.4 = (bf16[416,384]{1,0:T(8,128)(2,1)S(1)}, bf16[416,384]{1,0:T(8,128)(2,1)}, u32[]{:S(2)}) copy-start(bf16[416,384]{1,0:T(8,128)(2,1)} %constant.50.clone.refs_1_.refs_5_) | copy-start | bytes 958468
  11.2 7.2 %collective-permute-start.2 = (f32[10,2,384]{2,1,0:T(2,128)S(1)}, f32[10,2,384]{2,1,0:T(2,128)S(1)}, u32[]{:S(2)}, u32[]{:S(2)}) collective-permute-start(f32[10,2,384]{2,1,0:T(2,128)S(1)} %get-tuple-element.48), channel_id=1, source_target_pairs={{0,8},{16,24},{8,0},{24,16},{1,9},{17,25},{9,1},{25,17},{2,10},{18... | collective-permute-start | bytes 92168 | tf_op jit(solution)/shard_map/ppermute | solution.py:725
  11.7 6.8 %collective-permute-start.1 = (f32[10,2,384]{2,1,0:T(2,128)S(1)}, f32[10,2,384]{2,1,0:T(2,128)S(1)}, u32[]{:S(2)}, u32[]{:S(2)}) collective-permute-start(f32[10,2,384]{2,1,0:T(2,128)S(1)} %get-tuple-element.49), channel_id=1, source_target_pairs={{8,16},{24,0},{16,8},{0,24},{9,17},{25,1},{17,9},{1,25},{10,18},{2... | collective-permute-start | bytes 92168 | tf_op jit(solution)/shard_map/ppermute | solution.py:719
  13.3 7.6 %collective-permute-start.4 = (f32[2,20,384]{2,1,0:T(8,128)S(1)}, f32[2,20,384]{2,1,0:T(8,128)S(1)}, u32[]{:S(2)}, u32[]{:S(2)}) collective-permute-start(f32[2,20,384]{2,1,0:T(8,128)S(1)} %get-tuple-element.46), channel_id=1, source_target_pairs={{0,1},{2,3},{4,5},{6,7},{1,0},{3,2},{5,4},{7,6},{8,9},{10,11},{12,... | collective-permute-start | bytes 184328 | tf_op jit(solution)/shard_map/ppermute | solution.py:722
  14.9 7.0 %collective-permute-start.3 = (f32[2,20,384]{2,1,0:T(8,128)S(1)}, f32[2,20,384]{2,1,0:T(8,128)S(1)}, u32[]{:S(2)}, u32[]{:S(2)}) collective-permute-start(f32[2,20,384]{2,1,0:T(8,128)S(1)} %get-tuple-element.47), channel_id=1, source_target_pairs={{1,2},{3,4},{5,6},{7,0},{2,1},{4,3},{6,5},{0,7},{9,10},{11,12},{13... | collective-permute-start | bytes 184328 | tf_op jit(solution)/shard_map/ppermute | solution.py:716
  19.4 5.0 %collective-permute-start = (f32[96,128]{1,0:T(8,128)S(1)}, f32[96,128]{1,0:T(8,128)S(1)}, u32[]{:S(2)}, u32[]{:S(2)}) collective-permute-start(f32[96,128]{1,0:T(8,128)S(1)} %get-tuple-element.30), channel_id=1, source_target_pairs={{0,4},{4,0},{1,5},{5,1},{2,6},{6,2},{3,7},{7,3},{8,12},{12,8},{9,1... | collective-permute-start | bytes 147464 | tf_op jit(solution)/shard_map/ppermute | solution.py:738
  24.4 14.9 %copy-start.1 = (f32[20,10,384]{2,0,1:T(8,128)S(1)}, f32[20,10,384]{2,0,1:T(8,128)}, u32[]{:S(2)}) copy-start(f32[20,10,384]{2,0,1:T(8,128)} %param.7) | copy-start | bytes 921604
  24.4 14.9 %copy-start.2 = (bf16[384,512]{1,0:T(8,128)(2,1)S(1)}, bf16[384,512]{1,0:T(8,128)(2,1)}, u32[]{:S(2)}) copy-start(bf16[384,512]{1,0:T(8,128)(2,1)} %constant.49.clone.refs_2_) | copy-start | bytes 1179652
  24.4 14.9 %copy-start.3 = (bf16[384,512]{1,0:T(8,128)(2,1)S(1)}, bf16[384,512]{1,0:T(8,128)(2,1)}, u32[]{:S(2)}) copy-start(bf16[384,512]{1,0:T(8,128)(2,1)} %constant.48.clone.refs_1_) | copy-start | bytes 1179652

commit v8 on v7

--- a/solution.py
+++ b/solution.py
@@ -174,6 +174,28 @@
     return np.concatenate([high, low, high], axis=1)
 
 
+def three(table):
+    parts, rest = [], np.asarray(table, np.float64)
+    for _ in range(3):
+        parts.append(rest.astype(ml_dtypes.bfloat16))
+        rest = rest - parts[-1].astype(np.float64)
+    return parts
+
+
+def sixths(table):
+    one, two, last = three(table)
+    return np.concatenate([one, one, one, two, two, last], axis=1)
+
+
+def spread(values, axis):
+    parts, rest = [], values
+    for _ in range(3):
+        parts.append(rest.astype(jnp.bfloat16))
+        rest = rest - parts[-1].astype(jnp.float32)
+    one, two, last = parts
+    return jnp.concatenate([one, two, last, one, two, one], axis=axis)
+
+
 def split(values):
     high = values.astype(jnp.bfloat16)
     low = (values - high.astype(jnp.float32)).astype(jnp.bfloat16)
@@ -259,7 +281,7 @@
         place = owner // self.group * LANES + owner % self.group * self.kz + wave % self.kz
         table = np.zeros((self.nz, self.deep))
         table[:, place] = cas_table(wave, wave, self.nz)
-        return halves(table)
+        return three(table)
 
     def x_waves(self):
         return np.concatenate([np.arange(self.mirror), np.arange(self.nx - 1, self.mirror - 1, -1)])
@@ -272,7 +294,7 @@
     def y_both(self):
         table = np.zeros((self.ny, self.yp))
         table[:, : self.ny] = cas_table(np.arange(self.ny), np.arange(self.ny), self.ny)
-        return thirds(table)
+        return table
 
     def ends(self):
         low = np.arange(HALO)
@@ -281,12 +303,12 @@
     def y_ends(self):
         table = np.zeros((8, self.yp))
         table[: 2 * HALO, : self.ny] = cas_table(self.ends(), np.arange(self.ny), self.ny)
-        return thirds(table)
+        return sixths(table)
 
     def y_sources(self):
-        columns = cas_table(np.arange(self.ny), self.ends(), self.ny).T
-        wide = np.broadcast_to(columns[:, :, None], (2 * HALO, self.ny, LANES))
-        return np.ascontiguousarray(wide).astype(np.float32)
+        table = np.zeros((self.ny, LANES), np.float32)
+        table[:, : 2 * HALO] = cas_table(np.arange(self.ny), self.ends(), self.ny)
+        return table
 
     def x_backward(self):
         wide = np.zeros((self.gx * self.xw, LANES))
@@ -298,7 +320,7 @@
             x = g * self.cx + np.arange(self.cx)
             own[g * self.xp : g * self.xp + self.cx, : self.nx] = cas_table(x, waves, self.nx)
         scale = 4.0 * np.pi / (self.nx * self.nz)
-        return thirds(np.concatenate([wide, own], axis=0) * scale)
+        return np.concatenate(three(np.concatenate([wide, own], axis=0) * scale), axis=1)
 
     def plane(self):
         plane = np.full((self.ny, LANES), 1e30)
@@ -307,7 +329,8 @@
         return plane.astype(np.float32)
 
     def coarse_pack(self):
-        parts = [self.x_forward(), self.y_both(), self.y_ends(), self.x_backward()]
+        parts = [self.x_forward(), thirds(self.y_both()), sixths(self.y_both())]
+        parts += [self.y_ends(), self.x_backward()]
         width = max(part.shape[1] for part in parts)
         self.places, rows = [], 0
         for part in parts:
@@ -329,7 +352,7 @@
     def join_rows(self, ref, row):
         me = lax.axis_index("gx") * self.gl + lax.axis_index("gl")
         size = (2 * HALO + 1) * self.kz
-        start = (2 * HALO + 1) * self.ny + me * size + row * self.kz
+        start = 2 * self.ny + me * size + row * self.kz
         return ref[pl.ds(pl.multiple_of(start, 8), self.kz), :]
 
     def joins(self):
@@ -436,7 +459,7 @@
 
 
 def solve_kernel(p, blocks, coarse, table, spectrum_out, own, sent, turned, ends):
-    x_fwd, y_both, y_ends = (p.coarse(coarse, i) for i in range(3))
+    x_fwd, y_both, y_ends = (p.coarse(coarse, i) for i in (0, 1, 3))
     columns = []
     for gl in range(p.gl):
         for part in range(2):
@@ -453,7 +476,7 @@
     along_y = mul(y_both, stacked(padded_rows(field, p.yp), 0))
     solved = along_y * table[...]
     spectrum_out[...] = solved
-    at_ends = mul(y_ends, stacked(padded_rows(solved, p.yp), 0))
+    at_ends = mul(y_ends, spread(padded_rows(solved, p.yp), 0))
     for k in range(p.kz):
         ends[pl.ds(k, 8, stride=p.kz), :] = lanes_of(at_ends, k)
     own[...] = ends[pl.ds(0, 2 * HALO * p.kz), :]
@@ -469,8 +492,11 @@
     p, spectrum_in, own, received, table, fine, coarse,
     out, sources, planes,
 ):
-    y_both, x_bwd = p.coarse(coarse, 1), p.coarse(coarse, 3)
-    y_sources = [fine[(j + 1) * p.ny : (j + 2) * p.ny, :] for j in range(2 * HALO)]
+    y_back, x_bwd = p.coarse(coarse, 2), p.coarse(coarse, 4)
+    one, two, last = (x_bwd[:, i * LANES : (i + 1) * LANES] for i in range(3))
+    x_bwd = jnp.concatenate([one, one, one, two, two, last], axis=1)
+    columns = fine[p.ny : 2 * p.ny, :]
+    y_sources = [jnp.broadcast_to(columns[:, j : j + 1], columns.shape) for j in range(2 * HALO)]
     lane = lane_index(p.kz)
     free = LANES - p.nx
     part = [received[pl.ds(i * p.kz, p.kz), :] for i in range(4)]
@@ -515,7 +541,7 @@
             spectrum_in[:, k * LANES : (k + 1) * LANES]
             + added * table[:, k * LANES : (k + 1) * LANES]
         )
-    back_y = mul(y_both, stacked(padded_rows(jnp.concatenate(whole, axis=1), p.yp), 0))
+    back_y = mul(y_back, spread(padded_rows(jnp.concatenate(whole, axis=1), p.yp), 0))
     base = p.edge
     for k in range(p.kz):
         planes[pl.ds(base + k, p.ny, stride=p.kz), :] = lanes_of(back_y, k)
@@ -537,9 +563,9 @@
         start = base + gl * 2 * p.step
         end = start + 2 * p.step
         both = [filled([(start + i * p.step, p.step)], i) for i in range(2)]
-        wide = mul_t(wide_rows, stacked(jnp.concatenate(both, axis=0), 1))
+        wide = mul_t(wide_rows, spread(jnp.concatenate(both, axis=0), 1))
         sides = filled([(start - p.edge, p.edge), (end, p.edge - p.kz)], 2)
-        side = mul_t(own_rows, stacked(sides, 1))
+        side = mul_t(own_rows, spread(sides, 1))
         for gx in range(p.gx):
             target = gx * p.gl + gl
             for half in range(2):
@@ -565,7 +591,7 @@
 
 
 def stencil_kernel(
-    p, blocks, high_z, low_z, charge, faces_x, faces_y, faces_z, mass,
+    p, blocks, high_z, low_z, last_z, charge, faces_x, faces_y, faces_z, mass,
     pre, image, sums, field,
 ):
     lane = lane_index(p.xw)
@@ -595,7 +621,8 @@
     windows = [plain(y // p.yq * p.xe // 8 * 8, p.xw, y % p.yq) for y in range(p.cy)]
     windows += [plain(side // 8 * 8, p.xp, h) for h in range(2 * HALO - 1)]
     windows.append((p.xp, last_layer))
-    three_z = jnp.concatenate([high_z[...], high_z[...], low_z[...]], axis=1)
+    one, two, last = high_z[...], low_z[...], last_z[...]
+    six_z = jnp.concatenate([one, one, one, two, two, last], axis=1)
 
     def assembled(group):
         parts = []
@@ -603,12 +630,20 @@
             parts.append(jnp.concatenate([make(chunk) for rows, make in group], axis=0))
         return jnp.concatenate(parts, axis=1)
 
-    groups = [windows[p.cy :], windows[: p.yq], windows[p.yq : p.cy]]
+    groups = [windows[: p.yq + 1], windows[p.yq + 1 :]]
     results = []
     for group in groups:
-        high, low = split(assembled(group))
-        results.append(mul_t(jnp.concatenate([high, low, high], axis=1), three_z))
-    whole = jnp.concatenate([results[1], results[2], results[0]], axis=0)
+        value = assembled(group)
+        rows = value.shape[0]
+        parts, rest = [], value
+        for _ in range(3):
+            parts.append(rest.astype(jnp.bfloat16))
+            rest = rest - parts[-1].astype(jnp.float32)
+        tall = mul_t(jnp.concatenate(parts, axis=0), one)
+        second = mul_t(jnp.concatenate(parts[:2], axis=0), two)
+        small = tall[2 * rows :] + second[rows:] + mul_t(parts[0], last)
+        results.append(tall[:rows] + ((tall[rows : 2 * rows] + second[:rows]) + small))
+    whole = jnp.concatenate(results, axis=0)
     starts = np.cumsum([0] + [rows for rows, make in windows])
     for y in range(p.cy):
         at = int(starts[y]) + y // p.yq * p.xe % 8
@@ -693,7 +728,7 @@
 
     density = density.transpose(1, 0, 2)
     charge = charge.transpose(1, 0, 2)
-    high_z, low_z = (jnp.asarray(part) for part in p.z_forward())
+    high_z, low_z, last_z = (jnp.asarray(part) for part in p.z_forward())
     coarse, fine = jnp.asarray(p.coarse_pack()), jnp.asarray(p.fine_pack())
     (blocks,) = call(
         lambda *refs: forward_kernel(p, *refs),
@@ -762,7 +797,7 @@
     pre, image, sums = call(
         lambda *refs: stencil_kernel(p, *refs),
         [shape(*brick), shape(*brick), shape(2 * p.ng, 1, LANES)],
-        [blocks, high_z, low_z, charge, *faces],
+        [blocks, high_z, low_z, last_z, charge, *faces],
         [
             pltpu.VMEM((p.cy + 2 * HALO, p.xw, p.nz), f32),
         ],

time: 53.3 us -> 54.3 us (1.019)
  Pallas kernels: 8.55 us -> 9.35 us
    pallas_call x7, Pallas kernels: 8.55 us -> 9.35 us  [call(): pl.pallas_call(kernel, out_shape=tuple(outs), in_specs=specs or [VMEM_SPE...]
where the time goes in v8:
time: 54.3 us; the launch traced here: 54 us
  blocking collectives  24.2 us (45%)
  starting transfers between devices  15 us (28%)
  Pallas kernels  9.35 us (17%)
  waiting for transfers between devices  3.26 us (6%)
  other arithmetic  1.4 us (3%)
  between operations  0.81 us (1%)
    all_to_all x1, blocking collectives, local_planes(): blocks = lax.all_to_all(blocks, group, 0, 0)  13.9 us
    all_to_all x1, blocking collectives, local_planes(): sums = lax.all_to_all(sums, ('gx', 'gh', 'gl'), 0, 0)  10.3 us
    pallas_call x7, Pallas kernels, call(): pl.pallas_call(kernel, out_shape=tuple(outs), in_specs=specs or [VMEM_SPE...  9.35 us
    all_to_all x1, starting transfers between devices, local_planes(): blocks = lax.all_to_all(blocks, group, 0, 0)  6.3 us
    ppermute x1, starting transfers between devices, local_planes(): lax.ppermute(jnp.where(even_y, eps[:2], eps[p.cy - 2:]), along_y, pairs(2...  3.49 us
    ppermute x1, waiting for transfers between devices, local_planes(): received = lax.ppermute(sent, 'gh', [(0, 1), (1, 0)])  2.46 us
    ppermute x1, starting transfers between devices, local_planes(): lax.ppermute(jnp.where(even_x, eps[:, :2], eps[:, p.cx - 2:]), 'gx', pair...  1.63 us
    ppermute x1, starting transfers between devices, local_planes(): received = lax.ppermute(sent, 'gh', [(0, 1), (1, 0)])  1.57 us
  transfers between devices with their start and end apart: 6, of which 2 were waited for; matrix products, arithmetic and copies ran while one was open for 3% of the time, Pallas kernels for 2%

profile of v8, /device:TPU:0, one launch (start us, length us, event | category | flops | bytes accessed | tf_op | source)
XLA Modules:
  0.0 54.0 jit_solution(4052234308926396995)
XLA Ops:
  0.6 0.0 copy-start.6
  0.6 0.0 copy-start
  0.7 2.8 %shard_map.86 = f32[16,40,128]{2,1,0:T(8,128)} custom-call(f32[10,20,384]{2,1,0:T(8,128)} %bitcast.16, bf16[384,512]{1,0:T(8,128)(2,1)} %constant.50.clone.refs_1_, bf16[384,512]{1,0:T(8,128)(2,1)} %constant.51.clone.refs_2_), custom_call_target="tpu_custom_call" | custom-call | bytes 1421312 | tf_op jit(solution)/shard_map/pallas_call | solution.py:387
  3.5 6.3 %all-to-all-start = ((f32[16,40,128]{2,1,0:T(8,128)}), f32[16,40,128]{2,1,0:T(8,128)S(1)}, u32[]{:S(2)}, u32[]{:S(2)}) async-start(f32[16,40,128]{2,1,0:T(8,128)} %shard_map.86), calls=%async_computation | async-start | bytes 655360 | tf_op jit(solution)/shard_map/all_to_all | solution.py:746
  9.8 0.0 copy-done.6
  9.8 1.3 %fusion.3.refs_0_ = f32[10,20,384]{2,1,0:T(8,128)S(1)} fusion(f32[20,10,384]{2,0,1:T(8,128)S(1)} %copy-done.6), kind=kLoop, calls=%fused_computation.5 | loop fusion | flops 537600 | bytes 614400 | tf_op jit(solution)/shard_map/exp | solution.py:43
  11.2 0.0 copy-start.4
  11.2 0.5 collective-permute-start.2
  11.7 1.6 %collective-permute-start.1 = (f32[10,2,384]{2,1,0:T(2,128)S(1)}, f32[10,2,384]{2,1,0:T(2,128)S(1)}, u32[]{:S(2)}, u32[]{:S(2)}) collective-permute-start(f32[10,2,384]{2,1,0:T(2,128)S(1)} %get-tuple-element.49), channel_id=1, source_target_pairs={{8,16},{24,0},{16,8},{0,24},{9,17},{25,1},{17,9},{1,25},{10,18},{2... | collective-permute-start | bytes 92168 | tf_op jit(solution)/shard_map/ppermute | solution.py:754
  13.3 1.5 %collective-permute-start.4 = (f32[2,20,384]{2,1,0:T(8,128)S(1)}, f32[2,20,384]{2,1,0:T(8,128)S(1)}, u32[]{:S(2)}, u32[]{:S(2)}) collective-permute-start(f32[2,20,384]{2,1,0:T(8,128)S(1)} %get-tuple-element.46), channel_id=1, source_target_pairs={{0,1},{2,3},{4,5},{6,7},{1,0},{3,2},{5,4},{7,6},{8,9},{10,11},{12,... | collective-permute-start | bytes 184328 | tf_op jit(solution)/shard_map/ppermute | solution.py:757
  14.8 3.5 %collective-permute-start.3 = (f32[2,20,384]{2,1,0:T(8,128)S(1)}, f32[2,20,384]{2,1,0:T(8,128)S(1)}, u32[]{:S(2)}, u32[]{:S(2)}) collective-permute-start(f32[2,20,384]{2,1,0:T(8,128)S(1)} %get-tuple-element.47), channel_id=1, source_target_pairs={{1,2},{3,4},{5,6},{7,0},{2,1},{4,3},{6,5},{0,7},{9,10},{11,12},{13... | collective-permute-start | bytes 184328 | tf_op jit(solution)/shard_map/ppermute | solution.py:751
  18.3 0.0 copy-done
  18.3 0.1 shard_map.87.refs_2_.refs_3_
  18.4 0.0 collective-permute-done.2
  18.4 0.0 collective-permute-done.1
  18.5 0.0 all-to-all-done.refs_0_
  18.5 0.0 copy-done.4
  18.5 1.0 %shard_map.88 = (f32[40,3072]{1,0:T(8,128)S(1)}, f32[144,128]{1,0:T(8,128)S(1)}, f32[96,128]{1,0:T(8,128)S(1)}) custom-call(f32[16,40,128]{2,1,0:T(8,128)S(1)} %all-to-all-done.refs_0_, bf16[464,384]{1,0:T(8,128)(2,1)S(1)} %copy-done.4, f32[40,3072]{1,0:T(8,128)S(1)} %shard_map.87.refs_2_.refs_3_), custom_call_target="tpu_custom_call" | custom-call | bytes 1789952 | tf_op jit(solution)/shard_map/pallas_call | solution.py:387
  19.5 1.6 %collective-permute-start = (f32[96,128]{1,0:T(8,128)S(1)}, f32[96,128]{1,0:T(8,128)S(1)}, u32[]{:S(2)}, u32[]{:S(2)}) collective-permute-start(f32[96,128]{1,0:T(8,128)S(1)} %get-tuple-element.30), channel_id=1, source_target_pairs={{0,4},{4,0},{1,5},{5,1},{2,6},{6,2},{3,7},{7,3},{8,12},{12,8},{9,1... | collective-permute-start | bytes 147464 | tf_op jit(solution)/shard_map/ppermute | solution.py:773
  21.1 0.0 collective-permute-done.4
  21.1 0.8 %collective-permute-done.3 = f32[2,20,384]{2,1,0:T(8,128)S(1)} collective-permute-done((f32[2,20,384]{2,1,0:T(8,128)S(1)}, f32[2,20,384]{2,1,0:T(8,128)S(1)}, u32[]{:S(2)}, u32[]{:S(2)}) %collective-permute-start.3) | collective-permute-done | bytes 61472 | tf_op jit(solution)/shard_map/ppermute | solution.py:751
  21.9 0.2 shard_map.89
  22.1 2.5 %collective-permute-done.refs_2_ = f32[96,128]{1,0:T(8,128)S(1)} collective-permute-done((f32[96,128]{1,0:T(8,128)S(1)}, f32[96,128]{1,0:T(8,128)S(1)}, u32[]{:S(2)}, u32[]{:S(2)}) %collective-permute-start) | collective-permute-done | bytes 49184 | tf_op jit(solution)/shard_map/ppermute | solution.py:773
  24.6 0.0 copy-start.5
  24.6 1.6 %shard_map.90 = f32[16,72,128]{2,1,0:T(8,128)S(1)} custom-call(f32[40,3072]{1,0:T(8,128)S(1)} %get-tuple-element.26.refs_0_, f32[144,128]{1,0:T(8,128)S(1)} %get-tuple-element.27.refs_1_, f32[96,128]{1,0:T(8,128)S(1)} %collective-permute-done.refs_2_, f32[40,3072]{1,0:T(8,128)S(1)} %shard_map.87.refs_2_.refs_3_, f32[2768,128]{1,0:T(8,128)S(1)} %copy-done, ...), custom_call_target="tpu_custom_call" | custom-call | bytes 3469312 | tf_op jit(solution)/shard_map/pallas_call | solution.py:387
  26.1 0.0 copy-start.1
  26.1 0.0 copy-start.2
  26.2 0.0 copy-start.3
  26.2 13.9 %all_to_all.15.refs_0_ = f32[16,72,128]{2,1,0:T(8,128)S(1)} all-to-all(f32[16,72,128]{2,1,0:T(8,128)S(1)} %shard_map.90), channel_id=1, replica_groups=mesh['gx'=4,'gh'=2,'gl'=4] {'gx','gl'}, dimensions={0} | all-to-all | bytes 1179648 | tf_op jit(solution)/shard_map/all_to_all | solution.py:796
  40.0 0.0 copy-done.5
  40.0 0.0 copy-done.1
  40.0 0.0 copy-done.2
  40.0 0.0 copy-done.3
  40.1 2.6 %shard_map.91 = (f32[10,20,384]{2,1,0:T(8,128)S(1)}, f32[10,20,384]{2,1,0:T(8,128)S(1)}, f32[32,1,128]{2,1,0:T(1,128)S(1)}) custom-call(f32[16,72,128]{2,1,0:T(8,128)S(1)} %all_to_all.15.refs_0_, bf16[384,512]{1,0:T(8,128)(2,1)S(1)} %copy-done.3, bf16[384,512]{1,0:T(8,128)(2,1)S(1)} %copy-done.2, bf16[384,512]{1,0:T(8,128)(2,1)S(1)} %copy-done.5, ...), custom_call_target="tpu_custom_call" | custom-call | bytes 4089856 | tf_op jit(solution)/shard_map/pallas_call | solution.py:387
  42.7 10.3 %all_to_all.16.refs_0_ = f32[32,1,128]{2,1,0:T(1,128)S(1)} all-to-all(f32[32,1,128]{2,1,0:T(1,128)S(1)} %get-tuple-element.41), channel_id=1, replica_groups=mesh['gx'=4,'gh'=2,'gl'=4] {'gx','gh','gl'}, dimensions={0} | all-to-all | bytes 32768 | tf_op jit(solution)/shard_map/all_to_all | solution.py:805
  53.0 1.1 %shard_map.92 = (f32[10,20,384]{2,1,0:T(8,128)}, f32[10,20,384]{2,1,0:T(8,128)}) custom-call(f32[32,1,128]{2,1,0:T(1,128)S(1)} %all_to_all.16.refs_0_, f32[10,20,384]{2,1,0:T(8,128)S(1)} %bitcast.18, f32[10,20,384]{2,1,0:T(8,128)S(1)} %get-tuple-element.42.refs_2_, f32[10,20,384]{2,1,0:T(8,128)S(1)} %get-tuple-element.43.refs_3_), custom_call_target="tpu_custom_call" | custom-call | bytes 1552384 | tf_op jit(solution)/shard_map/pallas_call | solution.py:387
  (4 shorter events, 0.1 us)
Async XLA Ops:
  0.6 9.2 %copy-start.6 = (f32[20,10,384]{2,0,1:T(8,128)S(1)}, f32[20,10,384]{2,0,1:T(8,128)}, u32[]{:S(2)}) copy-start(f32[20,10,384]{2,0,1:T(8,128)} %param.7) | copy-start | bytes 921604
  0.6 17.7 %copy-start = (f32[2768,128]{1,0:T(8,128)S(1)}, f32[2768,128]{1,0:T(8,128)}, u32[]{:S(2)}) copy-start(f32[2768,128]{1,0:T(8,128)} %constant.54.clone.refs_0_.refs_4_) | copy-start | bytes 4251652
  3.5 15.0 %all-to-all-start = ((f32[16,40,128]{2,1,0:T(8,128)}), f32[16,40,128]{2,1,0:T(8,128)S(1)}, u32[]{:S(2)}, u32[]{:S(2)}) async-start(f32[16,40,128]{2,1,0:T(8,128)} %shard_map.86), calls=%async_computation | async-start | bytes 655360 | tf_op jit(solution)/shard_map/all_to_all | solution.py:746
  11.2 7.3 %copy-start.4 = (bf16[464,384]{1,0:T(8,128)(2,1)S(1)}, bf16[464,384]{1,0:T(8,128)(2,1)}, u32[]{:S(2)}) copy-start(bf16[464,384]{1,0:T(8,128)(2,1)} %constant.53.clone.refs_1_.refs_5_) | copy-start | bytes 1069060
  11.2 7.2 %collective-permute-start.2 = (f32[10,2,384]{2,1,0:T(2,128)S(1)}, f32[10,2,384]{2,1,0:T(2,128)S(1)}, u32[]{:S(2)}, u32[]{:S(2)}) collective-permute-start(f32[10,2,384]{2,1,0:T(2,128)S(1)} %get-tuple-element.48), channel_id=1, source_target_pairs={{0,8},{16,24},{8,0},{24,16},{1,9},{17,25},{9,1},{25,17},{2,10},{18... | collective-permute-start | bytes 92168 | tf_op jit(solution)/shard_map/ppermute | solution.py:760
  11.7 6.8 %collective-permute-start.1 = (f32[10,2,384]{2,1,0:T(2,128)S(1)}, f32[10,2,384]{2,1,0:T(2,128)S(1)}, u32[]{:S(2)}, u32[]{:S(2)}) collective-permute-start(f32[10,2,384]{2,1,0:T(2,128)S(1)} %get-tuple-element.49), channel_id=1, source_target_pairs={{8,16},{24,0},{16,8},{0,24},{9,17},{25,1},{17,9},{1,25},{10,18},{2... | collective-permute-start | bytes 92168 | tf_op jit(solution)/shard_map/ppermute | solution.py:754
  13.3 7.8 %collective-permute-start.4 = (f32[2,20,384]{2,1,0:T(8,128)S(1)}, f32[2,20,384]{2,1,0:T(8,128)S(1)}, u32[]{:S(2)}, u32[]{:S(2)}) collective-permute-start(f32[2,20,384]{2,1,0:T(8,128)S(1)} %get-tuple-element.46), channel_id=1, source_target_pairs={{0,1},{2,3},{4,5},{6,7},{1,0},{3,2},{5,4},{7,6},{8,9},{10,11},{12,... | collective-permute-start | bytes 184328 | tf_op jit(solution)/shard_map/ppermute | solution.py:757
  14.8 7.0 %collective-permute-start.3 = (f32[2,20,384]{2,1,0:T(8,128)S(1)}, f32[2,20,384]{2,1,0:T(8,128)S(1)}, u32[]{:S(2)}, u32[]{:S(2)}) collective-permute-start(f32[2,20,384]{2,1,0:T(8,128)S(1)} %get-tuple-element.47), channel_id=1, source_target_pairs={{1,2},{3,4},{5,6},{7,0},{2,1},{4,3},{6,5},{0,7},{9,10},{11,12},{13... | collective-permute-start | bytes 184328 | tf_op jit(solution)/shard_map/ppermute | solution.py:751
  19.5 5.0 %collective-permute-start = (f32[96,128]{1,0:T(8,128)S(1)}, f32[96,128]{1,0:T(8,128)S(1)}, u32[]{:S(2)}, u32[]{:S(2)}) collective-permute-start(f32[96,128]{1,0:T(8,128)S(1)} %get-tuple-element.30), channel_id=1, source_target_pairs={{0,4},{4,0},{1,5},{5,1},{2,6},{6,2},{3,7},{7,3},{8,12},{12,8},{9,1... | collective-permute-start | bytes 147464 | tf_op jit(solution)/shard_map/ppermute | solution.py:773
  24.6 15.5 %copy-start.5 = (bf16[384,512]{1,0:T(8,128)(2,1)S(1)}, bf16[384,512]{1,0:T(8,128)(2,1)}, u32[]{:S(2)}) copy-start(bf16[384,512]{1,0:T(8,128)(2,1)} %constant.52.clone.refs_3_) | copy-start | bytes 1179652
  26.1 13.9 %copy-start.1 = (f32[20,10,384]{2,0,1:T(8,128)S(1)}, f32[20,10,384]{2,0,1:T(8,128)}, u32[]{:S(2)}) copy-start(f32[20,10,384]{2,0,1:T(8,128)} %param.8) | copy-start | bytes 921604
  26.1 13.9 %copy-start.2 = (bf16[384,512]{1,0:T(8,128)(2,1)S(1)}, bf16[384,512]{1,0:T(8,128)(2,1)}, u32[]{:S(2)}) copy-start(bf16[384,512]{1,0:T(8,128)(2,1)} %constant.51.clone.refs_2_) | copy-start | bytes 1179652
  26.2 13.9 %copy-start.3 = (bf16[384,512]{1,0:T(8,128)(2,1)S(1)}, bf16[384,512]{1,0:T(8,128)(2,1)}, u32[]{:S(2)}) copy-start(bf16[384,512]{1,0:T(8,128)(2,1)} %constant.50.clone.refs_1_) | copy-start | bytes 1179652

commit v9 on v8

--- a/solution.py
+++ b/solution.py
@@ -630,7 +630,7 @@
             parts.append(jnp.concatenate([make(chunk) for rows, make in group], axis=0))
         return jnp.concatenate(parts, axis=1)
 
-    groups = [windows[: p.yq + 1], windows[p.yq + 1 :]]
+    groups = [windows[: p.yq + 3], windows[p.yq + 3 :]]
     results = []
     for group in groups:
         value = assembled(group)
@@ -769,7 +769,6 @@
         [blocks, coarse, table],
         [pltpu.VMEM((p.ny * p.kz + LANES, LANES), f32), pltpu.VMEM((8 * p.kz, LANES), f32)],
     )
-    sent, eps = lax.optimization_barrier((sent, eps))
     received = lax.ppermute(sent, "gh", [(0, 1), (1, 0)])
     ex_low, ex_high = jnp.where(even_x, swap_bx, swap_ax), jnp.where(even_x, swap_ax, swap_bx)
     ey_low, ey_high = jnp.where(even_y, swap_by, swap_ay), jnp.where(even_y, swap_ay, swap_by)

time: 54.3 us -> 54.2 us (level)
  no operation moved by 1% of the time
where the time goes in v9:
time: 54.2 us; the launch traced here: 53.9 us
  blocking collectives  24.2 us (45%)
  starting transfers between devices  15 us (28%)
  Pallas kernels  9.26 us (17%)
  waiting for transfers between devices  3.26 us (6%)
  other arithmetic  1.4 us (3%)
  between operations  0.81 us (1%)
    all_to_all x1, blocking collectives, local_planes(): blocks = lax.all_to_all(blocks, group, 0, 0)  13.9 us
    all_to_all x1, blocking collectives, local_planes(): sums = lax.all_to_all(sums, ('gx', 'gh', 'gl'), 0, 0)  10.3 us
    pallas_call x7, Pallas kernels, call(): pl.pallas_call(kernel, out_shape=tuple(outs), in_specs=specs or [VMEM_SPE...  9.26 us
    all_to_all x1, starting transfers between devices, local_planes(): blocks = lax.all_to_all(blocks, group, 0, 0)  6.3 us
    ppermute x1, starting transfers between devices, local_planes(): lax.ppermute(jnp.where(even_y, eps[:2], eps[p.cy - 2:]), along_y, pairs(2...  3.49 us
    ppermute x1, waiting for transfers between devices, local_planes(): received = lax.ppermute(sent, 'gh', [(0, 1), (1, 0)])  2.46 us
    ppermute x1, starting transfers between devices, local_planes(): lax.ppermute(jnp.where(even_x, eps[:, :2], eps[:, p.cx - 2:]), 'gx', pair...  1.63 us
    ppermute x1, starting transfers between devices, local_planes(): received = lax.ppermute(sent, 'gh', [(0, 1), (1, 0)])  1.57 us
  transfers between devices with their start and end apart: 6, of which 2 were waited for; matrix products, arithmetic and copies ran while one was open for 3% of the time, Pallas kernels for 2%

profile of v9, /device:TPU:0, one launch (start us, length us, event | category | flops | bytes accessed | tf_op | source)
XLA Modules:
  0.0 53.9 jit_solution(18111464123057268682)
XLA Ops:
  0.6 0.0 copy-start.6
  0.6 0.0 copy-start
  0.7 2.8 %shard_map.86 = f32[16,40,128]{2,1,0:T(8,128)} custom-call(f32[10,20,384]{2,1,0:T(8,128)} %bitcast.16, bf16[384,512]{1,0:T(8,128)(2,1)} %constant.50.clone.refs_1_, bf16[384,512]{1,0:T(8,128)(2,1)} %constant.51.clone.refs_2_), custom_call_target="tpu_custom_call" | custom-call | bytes 1421312 | tf_op jit(solution)/shard_map/pallas_call | solution.py:387
  3.5 6.3 %all-to-all-start = ((f32[16,40,128]{2,1,0:T(8,128)}), f32[16,40,128]{2,1,0:T(8,128)S(1)}, u32[]{:S(2)}, u32[]{:S(2)}) async-start(f32[16,40,128]{2,1,0:T(8,128)} %shard_map.86), calls=%async_computation | async-start | bytes 655360 | tf_op jit(solution)/shard_map/all_to_all | solution.py:746
  9.8 0.0 copy-done.6
  9.8 1.3 %fusion.3.refs_0_ = f32[10,20,384]{2,1,0:T(8,128)S(1)} fusion(f32[20,10,384]{2,0,1:T(8,128)S(1)} %copy-done.6), kind=kLoop, calls=%fused_computation.5 | loop fusion | flops 537600 | bytes 614400 | tf_op jit(solution)/shard_map/exp | solution.py:43
  11.2 0.0 copy-start.4
  11.2 0.5 collective-permute-start.2
  11.7 1.6 %collective-permute-start.1 = (f32[10,2,384]{2,1,0:T(2,128)S(1)}, f32[10,2,384]{2,1,0:T(2,128)S(1)}, u32[]{:S(2)}, u32[]{:S(2)}) collective-permute-start(f32[10,2,384]{2,1,0:T(2,128)S(1)} %get-tuple-element.45), channel_id=1, source_target_pairs={{8,16},{24,0},{16,8},{0,24},{9,17},{25,1},{17,9},{1,25},{10,18},{2... | collective-permute-start | bytes 92168 | tf_op jit(solution)/shard_map/ppermute | solution.py:754
  13.3 1.5 %collective-permute-start.4 = (f32[2,20,384]{2,1,0:T(8,128)S(1)}, f32[2,20,384]{2,1,0:T(8,128)S(1)}, u32[]{:S(2)}, u32[]{:S(2)}) collective-permute-start(f32[2,20,384]{2,1,0:T(8,128)S(1)} %get-tuple-element.42), channel_id=1, source_target_pairs={{0,1},{2,3},{4,5},{6,7},{1,0},{3,2},{5,4},{7,6},{8,9},{10,11},{12,... | collective-permute-start | bytes 184328 | tf_op jit(solution)/shard_map/ppermute | solution.py:757
  14.8 3.5 %collective-permute-start.3 = (f32[2,20,384]{2,1,0:T(8,128)S(1)}, f32[2,20,384]{2,1,0:T(8,128)S(1)}, u32[]{:S(2)}, u32[]{:S(2)}) collective-permute-start(f32[2,20,384]{2,1,0:T(8,128)S(1)} %get-tuple-element.43), channel_id=1, source_target_pairs={{1,2},{3,4},{5,6},{7,0},{2,1},{4,3},{6,5},{0,7},{9,10},{11,12},{13... | collective-permute-start | bytes 184328 | tf_op jit(solution)/shard_map/ppermute | solution.py:751
  18.3 0.0 copy-done
  18.3 0.1 shard_map.87.refs_2_.refs_3_
  18.4 0.0 collective-permute-done.2
  18.4 0.0 collective-permute-done.1
  18.5 0.0 all-to-all-done.refs_0_
  18.5 0.0 copy-done.4
  18.5 1.0 %shard_map.88 = (f32[40,3072]{1,0:T(8,128)S(1)}, f32[144,128]{1,0:T(8,128)S(1)}, f32[96,128]{1,0:T(8,128)S(1)}) custom-call(f32[16,40,128]{2,1,0:T(8,128)S(1)} %all-to-all-done.refs_0_, bf16[464,384]{1,0:T(8,128)(2,1)S(1)} %copy-done.4, f32[40,3072]{1,0:T(8,128)S(1)} %shard_map.87.refs_2_.refs_3_), custom_call_target="tpu_custom_call" | custom-call | bytes 1789952 | tf_op jit(solution)/shard_map/pallas_call | solution.py:387
  19.5 1.6 %collective-permute-start = (f32[96,128]{1,0:T(8,128)S(1)}, f32[96,128]{1,0:T(8,128)S(1)}, u32[]{:S(2)}, u32[]{:S(2)}) collective-permute-start(f32[96,128]{1,0:T(8,128)S(1)} %get-tuple-element.26), channel_id=1, source_target_pairs={{0,4},{4,0},{1,5},{5,1},{2,6},{6,2},{3,7},{7,3},{8,12},{12,8},{9,1... | collective-permute-start | bytes 147464 | tf_op jit(solution)/shard_map/ppermute | solution.py:772
  21.1 0.0 collective-permute-done.4
  21.1 0.8 %collective-permute-done.3 = f32[2,20,384]{2,1,0:T(8,128)S(1)} collective-permute-done((f32[2,20,384]{2,1,0:T(8,128)S(1)}, f32[2,20,384]{2,1,0:T(8,128)S(1)}, u32[]{:S(2)}, u32[]{:S(2)}) %collective-permute-start.3) | collective-permute-done | bytes 61472 | tf_op jit(solution)/shard_map/ppermute | solution.py:751
  21.9 0.2 shard_map.89
  22.1 2.5 %collective-permute-done.refs_2_ = f32[96,128]{1,0:T(8,128)S(1)} collective-permute-done((f32[96,128]{1,0:T(8,128)S(1)}, f32[96,128]{1,0:T(8,128)S(1)}, u32[]{:S(2)}, u32[]{:S(2)}) %collective-permute-start) | collective-permute-done | bytes 49184 | tf_op jit(solution)/shard_map/ppermute | solution.py:772
  24.6 0.0 copy-start.5
  24.6 1.6 %shard_map.90 = f32[16,72,128]{2,1,0:T(8,128)S(1)} custom-call(f32[40,3072]{1,0:T(8,128)S(1)} %get-tuple-element.24.refs_0_, f32[144,128]{1,0:T(8,128)S(1)} %get-tuple-element.25.refs_1_, f32[96,128]{1,0:T(8,128)S(1)} %collective-permute-done.refs_2_, f32[40,3072]{1,0:T(8,128)S(1)} %shard_map.87.refs_2_.refs_3_, f32[2768,128]{1,0:T(8,128)S(1)} %copy-done, ...), custom_call_target="tpu_custom_call" | custom-call | bytes 3469312 | tf_op jit(solution)/shard_map/pallas_call | solution.py:387
  26.1 0.0 copy-start.1
  26.1 0.0 copy-start.2
  26.2 0.0 copy-start.3
  26.2 13.9 %all_to_all.15.refs_0_ = f32[16,72,128]{2,1,0:T(8,128)S(1)} all-to-all(f32[16,72,128]{2,1,0:T(8,128)S(1)} %shard_map.90), channel_id=1, replica_groups=mesh['gx'=4,'gh'=2,'gl'=4] {'gx','gl'}, dimensions={0} | all-to-all | bytes 1179648 | tf_op jit(solution)/shard_map/all_to_all | solution.py:795
  40.0 0.0 copy-done.5
  40.0 0.0 copy-done.1
  40.0 0.0 copy-done.2
  40.0 0.0 copy-done.3
  40.1 2.5 %shard_map.91 = (f32[10,20,384]{2,1,0:T(8,128)S(1)}, f32[10,20,384]{2,1,0:T(8,128)S(1)}, f32[32,1,128]{2,1,0:T(1,128)S(1)}) custom-call(f32[16,72,128]{2,1,0:T(8,128)S(1)} %all_to_all.15.refs_0_, bf16[384,512]{1,0:T(8,128)(2,1)S(1)} %copy-done.3, bf16[384,512]{1,0:T(8,128)(2,1)S(1)} %copy-done.2, bf16[384,512]{1,0:T(8,128)(2,1)S(1)} %copy-done.5, ...), custom_call_target="tpu_custom_call" | custom-call | bytes 4089856 | tf_op jit(solution)/shard_map/pallas_call | solution.py:387
  42.6 10.3 %all_to_all.16.refs_0_ = f32[32,1,128]{2,1,0:T(1,128)S(1)} all-to-all(f32[32,1,128]{2,1,0:T(1,128)S(1)} %get-tuple-element.37), channel_id=1, replica_groups=mesh['gx'=4,'gh'=2,'gl'=4] {'gx','gh','gl'}, dimensions={0} | all-to-all | bytes 32768 | tf_op jit(solution)/shard_map/all_to_all | solution.py:804
  52.9 1.1 %shard_map.92 = (f32[10,20,384]{2,1,0:T(8,128)}, f32[10,20,384]{2,1,0:T(8,128)}) custom-call(f32[32,1,128]{2,1,0:T(1,128)S(1)} %all_to_all.16.refs_0_, f32[10,20,384]{2,1,0:T(8,128)S(1)} %bitcast.18, f32[10,20,384]{2,1,0:T(8,128)S(1)} %get-tuple-element.38.refs_2_, f32[10,20,384]{2,1,0:T(8,128)S(1)} %get-tuple-element.39.refs_3_), custom_call_target="tpu_custom_call" | custom-call | bytes 1552384 | tf_op jit(solution)/shard_map/pallas_call | solution.py:387
  (4 shorter events, 0.1 us)
Async XLA Ops:
  0.6 9.2 %copy-start.6 = (f32[20,10,384]{2,0,1:T(8,128)S(1)}, f32[20,10,384]{2,0,1:T(8,128)}, u32[]{:S(2)}) copy-start(f32[20,10,384]{2,0,1:T(8,128)} %param.7) | copy-start | bytes 921604
  0.6 17.7 %copy-start = (f32[2768,128]{1,0:T(8,128)S(1)}, f32[2768,128]{1,0:T(8,128)}, u32[]{:S(2)}) copy-start(f32[2768,128]{1,0:T(8,128)} %constant.54.clone.refs_0_.refs_4_) | copy-start | bytes 4251652
  3.5 15.0 %all-to-all-start = ((f32[16,40,128]{2,1,0:T(8,128)}), f32[16,40,128]{2,1,0:T(8,128)S(1)}, u32[]{:S(2)}, u32[]{:S(2)}) async-start(f32[16,40,128]{2,1,0:T(8,128)} %shard_map.86), calls=%async_computation | async-start | bytes 655360 | tf_op jit(solution)/shard_map/all_to_all | solution.py:746
  11.2 7.3 %copy-start.4 = (bf16[464,384]{1,0:T(8,128)(2,1)S(1)}, bf16[464,384]{1,0:T(8,128)(2,1)}, u32[]{:S(2)}) copy-start(bf16[464,384]{1,0:T(8,128)(2,1)} %constant.53.clone.refs_1_.refs_5_) | copy-start | bytes 1069060
  11.2 7.2 %collective-permute-start.2 = (f32[10,2,384]{2,1,0:T(2,128)S(1)}, f32[10,2,384]{2,1,0:T(2,128)S(1)}, u32[]{:S(2)}, u32[]{:S(2)}) collective-permute-start(f32[10,2,384]{2,1,0:T(2,128)S(1)} %get-tuple-element.44), channel_id=1, source_target_pairs={{0,8},{16,24},{8,0},{24,16},{1,9},{17,25},{9,1},{25,17},{2,10},{18... | collective-permute-start | bytes 92168 | tf_op jit(solution)/shard_map/ppermute | solution.py:760
  11.7 6.8 %collective-permute-start.1 = (f32[10,2,384]{2,1,0:T(2,128)S(1)}, f32[10,2,384]{2,1,0:T(2,128)S(1)}, u32[]{:S(2)}, u32[]{:S(2)}) collective-permute-start(f32[10,2,384]{2,1,0:T(2,128)S(1)} %get-tuple-element.45), channel_id=1, source_target_pairs={{8,16},{24,0},{16,8},{0,24},{9,17},{25,1},{17,9},{1,25},{10,18},{2... | collective-permute-start | bytes 92168 | tf_op jit(solution)/shard_map/ppermute | solution.py:754
  13.3 7.8 %collective-permute-start.4 = (f32[2,20,384]{2,1,0:T(8,128)S(1)}, f32[2,20,384]{2,1,0:T(8,128)S(1)}, u32[]{:S(2)}, u32[]{:S(2)}) collective-permute-start(f32[2,20,384]{2,1,0:T(8,128)S(1)} %get-tuple-element.42), channel_id=1, source_target_pairs={{0,1},{2,3},{4,5},{6,7},{1,0},{3,2},{5,4},{7,6},{8,9},{10,11},{12,... | collective-permute-start | bytes 184328 | tf_op jit(solution)/shard_map/ppermute | solution.py:757
  14.8 7.0 %collective-permute-start.3 = (f32[2,20,384]{2,1,0:T(8,128)S(1)}, f32[2,20,384]{2,1,0:T(8,128)S(1)}, u32[]{:S(2)}, u32[]{:S(2)}) collective-permute-start(f32[2,20,384]{2,1,0:T(8,128)S(1)} %get-tuple-element.43), channel_id=1, source_target_pairs={{1,2},{3,4},{5,6},{7,0},{2,1},{4,3},{6,5},{0,7},{9,10},{11,12},{13... | collective-permute-start | bytes 184328 | tf_op jit(solution)/shard_map/ppermute | solution.py:751
  19.5 5.0 %collective-permute-start = (f32[96,128]{1,0:T(8,128)S(1)}, f32[96,128]{1,0:T(8,128)S(1)}, u32[]{:S(2)}, u32[]{:S(2)}) collective-permute-start(f32[96,128]{1,0:T(8,128)S(1)} %get-tuple-element.26), channel_id=1, source_target_pairs={{0,4},{4,0},{1,5},{5,1},{2,6},{6,2},{3,7},{7,3},{8,12},{12,8},{9,1... | collective-permute-start | bytes 147464 | tf_op jit(solution)/shard_map/ppermute | solution.py:772
  24.6 15.5 %copy-start.5 = (bf16[384,512]{1,0:T(8,128)(2,1)S(1)}, bf16[384,512]{1,0:T(8,128)(2,1)}, u32[]{:S(2)}) copy-start(bf16[384,512]{1,0:T(8,128)(2,1)} %constant.52.clone.refs_3_) | copy-start | bytes 1179652
  26.1 13.9 %copy-start.1 = (f32[20,10,384]{2,0,1:T(8,128)S(1)}, f32[20,10,384]{2,0,1:T(8,128)}, u32[]{:S(2)}) copy-start(f32[20,10,384]{2,0,1:T(8,128)} %param.8) | copy-start | bytes 921604
  26.1 13.9 %copy-start.2 = (bf16[384,512]{1,0:T(8,128)(2,1)S(1)}, bf16[384,512]{1,0:T(8,128)(2,1)}, u32[]{:S(2)}) copy-start(bf16[384,512]{1,0:T(8,128)(2,1)} %constant.51.clone.refs_2_) | copy-start | bytes 1179652
  26.2 13.9 %copy-start.3 = (bf16[384,512]{1,0:T(8,128)(2,1)S(1)}, bf16[384,512]{1,0:T(8,128)(2,1)}, u32[]{:S(2)}) copy-start(bf16[384,512]{1,0:T(8,128)(2,1)} %constant.50.clone.refs_1_) | copy-start | bytes 1179652

commit v10 on v9

--- a/solution.py
+++ b/solution.py
@@ -182,9 +182,11 @@
     return parts
 
 
-def sixths(table):
-    one, two, last = three(table)
-    return np.concatenate([one, one, one, two, two, last], axis=1)
+def tower(parts, lib):
+    one, two, last = parts
+    none = lib.zeros_like(one)
+    rows = [(one, one, one), (two, two, none), (last, none, none)]
+    return lib.concatenate([lib.concatenate(row, axis=1) for row in rows], axis=0)
 
 
 def spread(values, axis):
@@ -192,8 +194,12 @@
     for _ in range(3):
         parts.append(rest.astype(jnp.bfloat16))
         rest = rest - parts[-1].astype(jnp.float32)
-    one, two, last = parts
-    return jnp.concatenate([one, two, last, one, two, one], axis=axis)
+    return jnp.concatenate(parts, axis=axis)
+
+
+def summed(tall):
+    rows = tall.shape[0] // 3
+    return tall[:rows] + (tall[rows : 2 * rows] + tall[2 * rows :])
 
 
 def split(values):
@@ -303,7 +309,7 @@
     def y_ends(self):
         table = np.zeros((8, self.yp))
         table[: 2 * HALO, : self.ny] = cas_table(self.ends(), np.arange(self.ny), self.ny)
-        return sixths(table)
+        return tower(three(table), np)
 
     def y_sources(self):
         table = np.zeros((self.ny, LANES), np.float32)
@@ -329,7 +335,7 @@
         return plane.astype(np.float32)
 
     def coarse_pack(self):
-        parts = [self.x_forward(), thirds(self.y_both()), sixths(self.y_both())]
+        parts = [self.x_forward(), thirds(self.y_both()), tower(three(self.y_both()), np)]
         parts += [self.y_ends(), self.x_backward()]
         width = max(part.shape[1] for part in parts)
         self.places, rows = [], 0
@@ -476,7 +482,7 @@
     along_y = mul(y_both, stacked(padded_rows(field, p.yp), 0))
     solved = along_y * table[...]
     spectrum_out[...] = solved
-    at_ends = mul(y_ends, spread(padded_rows(solved, p.yp), 0))
+    at_ends = summed(mul(y_ends, spread(padded_rows(solved, p.yp), 0)))
     for k in range(p.kz):
         ends[pl.ds(k, 8, stride=p.kz), :] = lanes_of(at_ends, k)
     own[...] = ends[pl.ds(0, 2 * HALO * p.kz), :]
@@ -494,7 +500,6 @@
 ):
     y_back, x_bwd = p.coarse(coarse, 2), p.coarse(coarse, 4)
     one, two, last = (x_bwd[:, i * LANES : (i + 1) * LANES] for i in range(3))
-    x_bwd = jnp.concatenate([one, one, one, two, two, last], axis=1)
     columns = fine[p.ny : 2 * p.ny, :]
     y_sources = [jnp.broadcast_to(columns[:, j : j + 1], columns.shape) for j in range(2 * HALO)]
     lane = lane_index(p.kz)
@@ -541,7 +546,7 @@
             spectrum_in[:, k * LANES : (k + 1) * LANES]
             + added * table[:, k * LANES : (k + 1) * LANES]
         )
-    back_y = mul(y_back, spread(padded_rows(jnp.concatenate(whole, axis=1), p.yp), 0))
+    back_y = summed(mul(y_back, spread(padded_rows(jnp.concatenate(whole, axis=1), p.yp), 0)))
     base = p.edge
     for k in range(p.kz):
         planes[pl.ds(base + k, p.ny, stride=p.kz), :] = lanes_of(back_y, k)
@@ -550,8 +555,8 @@
         planes[pl.ds(base - (i + 1) * p.kz, p.kz), :] = far_high[i]
         planes[pl.ds(after + i * p.kz, p.kz), :] = far_low[i]
     cut = p.gx * p.xw
-    wide_rows = x_bwd[:cut, :]
-    own_rows = x_bwd[cut:, :]
+    wide_rows = tower([part[:cut] for part in (one, two, last)], jnp)
+    own_rows = tower([part[cut:] for part in (one, two, last)], jnp)
     rest = p.rows - 2 * p.xe - p.cx
 
     def filled(pieces, part):
@@ -563,9 +568,9 @@
         start = base + gl * 2 * p.step
         end = start + 2 * p.step
         both = [filled([(start + i * p.step, p.step)], i) for i in range(2)]
-        wide = mul_t(wide_rows, spread(jnp.concatenate(both, axis=0), 1))
+        wide = summed(mul_t(wide_rows, spread(jnp.concatenate(both, axis=0), 1)))
         sides = filled([(start - p.edge, p.edge), (end, p.edge - p.kz)], 2)
-        side = mul_t(own_rows, spread(sides, 1))
+        side = summed(mul_t(own_rows, spread(sides, 1)))
         for gx in range(p.gx):
             target = gx * p.gl + gl
             for half in range(2):

time: 54.2 us -> 54.1 us (level)
  no operation moved by 1% of the time
where the time goes in v10:
time: 54.1 us; the launch traced here: 53.8 us
  blocking collectives  24.2 us (45%)
  starting transfers between devices  15 us (28%)
  Pallas kernels  9.13 us (17%)
  waiting for transfers between devices  3.27 us (6%)
  other arithmetic  1.4 us (3%)
  between operations  0.81 us (1%)
    all_to_all x1, blocking collectives, local_planes(): blocks = lax.all_to_all(blocks, group, 0, 0)  13.9 us
    all_to_all x1, blocking collectives, local_planes(): sums = lax.all_to_all(sums, ('gx', 'gh', 'gl'), 0, 0)  10.3 us
    pallas_call x7, Pallas kernels, call(): pl.pallas_call(kernel, out_shape=tuple(outs), in_specs=specs or [VMEM_SPE...  9.13 us
    all_to_all x1, starting transfers between devices, local_planes(): blocks = lax.all_to_all(blocks, group, 0, 0)  6.3 us
    ppermute x1, starting transfers between devices, local_planes(): lax.ppermute(jnp.where(even_y, eps[:2], eps[p.cy - 2:]), along_y, pairs(2...  3.49 us
    ppermute x1, waiting for transfers between devices, local_planes(): received = lax.ppermute(sent, 'gh', [(0, 1), (1, 0)])  2.32 us
    ppermute x1, starting transfers between devices, local_planes(): lax.ppermute(jnp.where(even_x, eps[:, :2], eps[:, p.cx - 2:]), 'gx', pair...  1.63 us
    ppermute x1, starting transfers between devices, local_planes(): received = lax.ppermute(sent, 'gh', [(0, 1), (1, 0)])  1.58 us
  transfers between devices with their start and end apart: 6, of which 2 were waited for; matrix products, arithmetic and copies ran while one was open for 3% of the time, Pallas kernels for 2%

profile of v10, /device:TPU:0, one launch (start us, length us, event | category | flops | bytes accessed | tf_op | source)
XLA Modules:
  0.0 53.8 jit_solution(15490024875759777715)
XLA Ops:
  0.6 0.0 copy-start.6
  0.6 0.0 copy-start
  0.7 2.8 %shard_map.86 = f32[16,40,128]{2,1,0:T(8,128)} custom-call(f32[10,20,384]{2,1,0:T(8,128)} %bitcast.16, bf16[384,512]{1,0:T(8,128)(2,1)} %constant.50.clone.refs_1_, bf16[384,512]{1,0:T(8,128)(2,1)} %constant.51.clone.refs_2_), custom_call_target="tpu_custom_call" | custom-call | bytes 1421312 | tf_op jit(solution)/shard_map/pallas_call | solution.py:393
  3.5 6.3 %all-to-all-start = ((f32[16,40,128]{2,1,0:T(8,128)}), f32[16,40,128]{2,1,0:T(8,128)S(1)}, u32[]{:S(2)}, u32[]{:S(2)}) async-start(f32[16,40,128]{2,1,0:T(8,128)} %shard_map.86), calls=%async_computation | async-start | bytes 655360 | tf_op jit(solution)/shard_map/all_to_all | solution.py:751
  9.8 0.0 copy-done.6
  9.8 1.3 %fusion.3.refs_0_ = f32[10,20,384]{2,1,0:T(8,128)S(1)} fusion(f32[20,10,384]{2,0,1:T(8,128)S(1)} %copy-done.6), kind=kLoop, calls=%fused_computation.5 | loop fusion | flops 537600 | bytes 614400 | tf_op jit(solution)/shard_map/exp | solution.py:43
  11.2 0.0 copy-start.2
  11.2 0.5 collective-permute-start.2
  11.7 1.6 %collective-permute-start.1 = (f32[10,2,384]{2,1,0:T(2,128)S(1)}, f32[10,2,384]{2,1,0:T(2,128)S(1)}, u32[]{:S(2)}, u32[]{:S(2)}) collective-permute-start(f32[10,2,384]{2,1,0:T(2,128)S(1)} %get-tuple-element.45), channel_id=1, source_target_pairs={{8,16},{24,0},{16,8},{0,24},{9,17},{25,1},{17,9},{1,25},{10,18},{2... | collective-permute-start | bytes 92168 | tf_op jit(solution)/shard_map/ppermute | solution.py:759
  13.3 1.5 %collective-permute-start.4 = (f32[2,20,384]{2,1,0:T(8,128)S(1)}, f32[2,20,384]{2,1,0:T(8,128)S(1)}, u32[]{:S(2)}, u32[]{:S(2)}) collective-permute-start(f32[2,20,384]{2,1,0:T(8,128)S(1)} %get-tuple-element.42), channel_id=1, source_target_pairs={{0,1},{2,3},{4,5},{6,7},{1,0},{3,2},{5,4},{7,6},{8,9},{10,11},{12,... | collective-permute-start | bytes 184328 | tf_op jit(solution)/shard_map/ppermute | solution.py:762
  14.8 3.5 %collective-permute-start.3 = (f32[2,20,384]{2,1,0:T(8,128)S(1)}, f32[2,20,384]{2,1,0:T(8,128)S(1)}, u32[]{:S(2)}, u32[]{:S(2)}) collective-permute-start(f32[2,20,384]{2,1,0:T(8,128)S(1)} %get-tuple-element.43), channel_id=1, source_target_pairs={{1,2},{3,4},{5,6},{7,0},{2,1},{4,3},{6,5},{0,7},{9,10},{11,12},{13... | collective-permute-start | bytes 184328 | tf_op jit(solution)/shard_map/ppermute | solution.py:756
  18.3 0.0 copy-done
  18.3 0.1 shard_map.87.refs_2_.refs_3_
  18.4 0.0 collective-permute-done.2
  18.4 0.0 collective-permute-done.1
  18.5 0.0 all-to-all-done.refs_0_
  18.5 0.0 copy-done.2
  18.5 0.9 %shard_map.88 = (f32[40,3072]{1,0:T(8,128)S(1)}, f32[144,128]{1,0:T(8,128)S(1)}, f32[96,128]{1,0:T(8,128)S(1)}) custom-call(f32[16,40,128]{2,1,0:T(8,128)S(1)} %all-to-all-done.refs_0_, bf16[560,384]{1,0:T(8,128)(2,1)S(1)} %copy-done.2, f32[40,3072]{1,0:T(8,128)S(1)} %shard_map.87.refs_2_.refs_3_), custom_call_target="tpu_custom_call" | custom-call | bytes 1863680 | tf_op jit(solution)/shard_map/pallas_call | solution.py:393
  19.4 1.6 %collective-permute-start = (f32[96,128]{1,0:T(8,128)S(1)}, f32[96,128]{1,0:T(8,128)S(1)}, u32[]{:S(2)}, u32[]{:S(2)}) collective-permute-start(f32[96,128]{1,0:T(8,128)S(1)} %get-tuple-element.26), channel_id=1, source_target_pairs={{0,4},{4,0},{1,5},{5,1},{2,6},{6,2},{3,7},{7,3},{8,12},{12,8},{9,1... | collective-permute-start | bytes 147464 | tf_op jit(solution)/shard_map/ppermute | solution.py:777
  21.0 0.0 collective-permute-done.4
  21.0 0.9 %collective-permute-done.3 = f32[2,20,384]{2,1,0:T(8,128)S(1)} collective-permute-done((f32[2,20,384]{2,1,0:T(8,128)S(1)}, f32[2,20,384]{2,1,0:T(8,128)S(1)}, u32[]{:S(2)}, u32[]{:S(2)}) %collective-permute-start.3) | collective-permute-done | bytes 61472 | tf_op jit(solution)/shard_map/ppermute | solution.py:756
  21.9 0.2 shard_map.89
  22.1 2.3 %collective-permute-done.refs_2_ = f32[96,128]{1,0:T(8,128)S(1)} collective-permute-done((f32[96,128]{1,0:T(8,128)S(1)}, f32[96,128]{1,0:T(8,128)S(1)}, u32[]{:S(2)}, u32[]{:S(2)}) %collective-permute-start) | collective-permute-done | bytes 49184 | tf_op jit(solution)/shard_map/ppermute | solution.py:777
  24.4 0.0 copy-start.5
  24.4 1.6 %shard_map.90 = f32[16,72,128]{2,1,0:T(8,128)S(1)} custom-call(f32[40,3072]{1,0:T(8,128)S(1)} %get-tuple-element.24.refs_0_, f32[144,128]{1,0:T(8,128)S(1)} %get-tuple-element.25.refs_1_, f32[96,128]{1,0:T(8,128)S(1)} %collective-permute-done.refs_2_, f32[40,3072]{1,0:T(8,128)S(1)} %shard_map.87.refs_2_.refs_3_, f32[2768,128]{1,0:T(8,128)S(1)} %copy-done, ...), custom_call_target="tpu_custom_call" | custom-call | bytes 3543040 | tf_op jit(solution)/shard_map/pallas_call | solution.py:393
  26.0 0.0 copy-start.1
  26.0 0.0 copy-start.3
  26.0 0.0 copy-start.4
  26.1 13.9 %all_to_all.15.refs_0_ = f32[16,72,128]{2,1,0:T(8,128)S(1)} all-to-all(f32[16,72,128]{2,1,0:T(8,128)S(1)} %shard_map.90), channel_id=1, replica_groups=mesh['gx'=4,'gh'=2,'gl'=4] {'gx','gl'}, dimensions={0} | all-to-all | bytes 1179648 | tf_op jit(solution)/shard_map/all_to_all | solution.py:800
  39.9 0.0 copy-done.5
  39.9 0.0 copy-done.1
  39.9 0.0 copy-done.3
  39.9 0.0 copy-done.4
  39.9 2.5 %shard_map.91 = (f32[10,20,384]{2,1,0:T(8,128)S(1)}, f32[10,20,384]{2,1,0:T(8,128)S(1)}, f32[32,1,128]{2,1,0:T(1,128)S(1)}) custom-call(f32[16,72,128]{2,1,0:T(8,128)S(1)} %all_to_all.15.refs_0_, bf16[384,512]{1,0:T(8,128)(2,1)S(1)} %copy-done.4, bf16[384,512]{1,0:T(8,128)(2,1)S(1)} %copy-done.3, bf16[384,512]{1,0:T(8,128)(2,1)S(1)} %copy-done.5, ...), custom_call_target="tpu_custom_call" | custom-call | bytes 4089856 | tf_op jit(solution)/shard_map/pallas_call | solution.py:393
  42.5 10.3 %all_to_all.16.refs_0_ = f32[32,1,128]{2,1,0:T(1,128)S(1)} all-to-all(f32[32,1,128]{2,1,0:T(1,128)S(1)} %get-tuple-element.37), channel_id=1, replica_groups=mesh['gx'=4,'gh'=2,'gl'=4] {'gx','gh','gl'}, dimensions={0} | all-to-all | bytes 32768 | tf_op jit(solution)/shard_map/all_to_all | solution.py:809
  52.8 1.0 %shard_map.92 = (f32[10,20,384]{2,1,0:T(8,128)}, f32[10,20,384]{2,1,0:T(8,128)}) custom-call(f32[32,1,128]{2,1,0:T(1,128)S(1)} %all_to_all.16.refs_0_, f32[10,20,384]{2,1,0:T(8,128)S(1)} %bitcast.18, f32[10,20,384]{2,1,0:T(8,128)S(1)} %get-tuple-element.38.refs_2_, f32[10,20,384]{2,1,0:T(8,128)S(1)} %get-tuple-element.39.refs_3_), custom_call_target="tpu_custom_call" | custom-call | bytes 1552384 | tf_op jit(solution)/shard_map/pallas_call | solution.py:393
  (4 shorter events, 0.1 us)
Async XLA Ops:
  0.6 9.2 %copy-start.6 = (f32[20,10,384]{2,0,1:T(8,128)S(1)}, f32[20,10,384]{2,0,1:T(8,128)}, u32[]{:S(2)}) copy-start(f32[20,10,384]{2,0,1:T(8,128)} %param.7) | copy-start | bytes 921604
  0.6 17.7 %copy-start = (f32[2768,128]{1,0:T(8,128)S(1)}, f32[2768,128]{1,0:T(8,128)}, u32[]{:S(2)}) copy-start(f32[2768,128]{1,0:T(8,128)} %constant.54.clone.refs_0_.refs_4_) | copy-start | bytes 4251652
  3.5 15.0 %all-to-all-start = ((f32[16,40,128]{2,1,0:T(8,128)}), f32[16,40,128]{2,1,0:T(8,128)S(1)}, u32[]{:S(2)}, u32[]{:S(2)}) async-start(f32[16,40,128]{2,1,0:T(8,128)} %shard_map.86), calls=%async_computation | async-start | bytes 655360 | tf_op jit(solution)/shard_map/all_to_all | solution.py:751
  11.2 7.3 %copy-start.2 = (bf16[560,384]{1,0:T(8,128)(2,1)S(1)}, bf16[560,384]{1,0:T(8,128)(2,1)}, u32[]{:S(2)}) copy-start(bf16[560,384]{1,0:T(8,128)(2,1)} %constant.53.clone.refs_1_.refs_5_) | copy-start | bytes 1290244
  11.2 7.2 %collective-permute-start.2 = (f32[10,2,384]{2,1,0:T(2,128)S(1)}, f32[10,2,384]{2,1,0:T(2,128)S(1)}, u32[]{:S(2)}, u32[]{:S(2)}) collective-permute-start(f32[10,2,384]{2,1,0:T(2,128)S(1)} %get-tuple-element.44), channel_id=1, source_target_pairs={{0,8},{16,24},{8,0},{24,16},{1,9},{17,25},{9,1},{25,17},{2,10},{18... | collective-permute-start | bytes 92168 | tf_op jit(solution)/shard_map/ppermute | solution.py:765
  11.7 6.8 %collective-permute-start.1 = (f32[10,2,384]{2,1,0:T(2,128)S(1)}, f32[10,2,384]{2,1,0:T(2,128)S(1)}, u32[]{:S(2)}, u32[]{:S(2)}) collective-permute-start(f32[10,2,384]{2,1,0:T(2,128)S(1)} %get-tuple-element.45), channel_id=1, source_target_pairs={{8,16},{24,0},{16,8},{0,24},{9,17},{25,1},{17,9},{1,25},{10,18},{2... | collective-permute-start | bytes 92168 | tf_op jit(solution)/shard_map/ppermute | solution.py:759
  13.3 7.6 %collective-permute-start.4 = (f32[2,20,384]{2,1,0:T(8,128)S(1)}, f32[2,20,384]{2,1,0:T(8,128)S(1)}, u32[]{:S(2)}, u32[]{:S(2)}) collective-permute-start(f32[2,20,384]{2,1,0:T(8,128)S(1)} %get-tuple-element.42), channel_id=1, source_target_pairs={{0,1},{2,3},{4,5},{6,7},{1,0},{3,2},{5,4},{7,6},{8,9},{10,11},{12,... | collective-permute-start | bytes 184328 | tf_op jit(solution)/shard_map/ppermute | solution.py:762
  14.8 7.0 %collective-permute-start.3 = (f32[2,20,384]{2,1,0:T(8,128)S(1)}, f32[2,20,384]{2,1,0:T(8,128)S(1)}, u32[]{:S(2)}, u32[]{:S(2)}) collective-permute-start(f32[2,20,384]{2,1,0:T(8,128)S(1)} %get-tuple-element.43), channel_id=1, source_target_pairs={{1,2},{3,4},{5,6},{7,0},{2,1},{4,3},{6,5},{0,7},{9,10},{11,12},{13... | collective-permute-start | bytes 184328 | tf_op jit(solution)/shard_map/ppermute | solution.py:756
  19.4 5.0 %collective-permute-start = (f32[96,128]{1,0:T(8,128)S(1)}, f32[96,128]{1,0:T(8,128)S(1)}, u32[]{:S(2)}, u32[]{:S(2)}) collective-permute-start(f32[96,128]{1,0:T(8,128)S(1)} %get-tuple-element.26), channel_id=1, source_target_pairs={{0,4},{4,0},{1,5},{5,1},{2,6},{6,2},{3,7},{7,3},{8,12},{12,8},{9,1... | collective-permute-start | bytes 147464 | tf_op jit(solution)/shard_map/ppermute | solution.py:777
  24.4 15.5 %copy-start.5 = (bf16[384,512]{1,0:T(8,128)(2,1)S(1)}, bf16[384,512]{1,0:T(8,128)(2,1)}, u32[]{:S(2)}) copy-start(bf16[384,512]{1,0:T(8,128)(2,1)} %constant.52.clone.refs_3_) | copy-start | bytes 1179652
  26.0 13.9 %copy-start.1 = (f32[20,10,384]{2,0,1:T(8,128)S(1)}, f32[20,10,384]{2,0,1:T(8,128)}, u32[]{:S(2)}) copy-start(f32[20,10,384]{2,0,1:T(8,128)} %param.8) | copy-start | bytes 921604
  26.0 13.9 %copy-start.3 = (bf16[384,512]{1,0:T(8,128)(2,1)S(1)}, bf16[384,512]{1,0:T(8,128)(2,1)}, u32[]{:S(2)}) copy-start(bf16[384,512]{1,0:T(8,128)(2,1)} %constant.51.clone.refs_2_) | copy-start | bytes 1179652
  26.0 13.9 %copy-start.4 = (bf16[384,512]{1,0:T(8,128)(2,1)S(1)}, bf16[384,512]{1,0:T(8,128)(2,1)}, u32[]{:S(2)}) copy-start(bf16[384,512]{1,0:T(8,128)(2,1)} %constant.50.clone.refs_1_) | copy-start | bytes 1179652
